TPU v7x, 32 devices: a whole 2x2x4 slice. The times are simulated.
32 devices in a mesh: weights: 4 (over y, x), context: 2 (over core), tensor: 4 (over z).
Axes of the slice: x: 2, y: 2, z: 4, core: 2. Of those that a mesh axis runs over, the one named last changes fastest.
Arguments:
- layer_in: bfloat16 [4, 1024, 2048], P('weights', 'context'), may hold values from -6 to 6
- norm_gains: bfloat16 [2048, 2], P(('weights', 'context')), may hold values from 0.5 to 1.5
- qkv_weight: bfloat16 [2048, 3, 2048], P(('weights', 'context'), None, 'tensor'), may hold values from -0.125 to 0.125
- qk_gains: bfloat16 [128, 2, 16], P(('weights', 'context'), None, 'tensor'), may hold values from 0.5 to 1.5
- out_weight: bfloat16 [2048, 2048], P(('weights', 'context'), 'tensor'), may hold values from -0.5 to 0.5
- router: bfloat16 [2048, 16], P(('weights', 'context')), may hold values from -0.0625 to 0.0625
- expert_in: bfloat16 [16, 2, 2048, 1024], P(('weights', 'context'), None, None, 'tensor'), may hold values from -0.125 to 0.125
- expert_out: bfloat16 [16, 1024, 2048], P(('weights', 'context'), 'tensor'), may hold values from -1.75 to 1.75
- grad_out: bfloat16 [4, 1024, 2048], P('weights', 'context'), may hold values from -6 to 6
- segments: int32 [4, 1024], P('weights'), may hold values from 0 to 15, never falling along the last dimension, each value on 1 to 512 neighbouring positions
- routes: int32 [4, 1024, 8], P('weights', 'context'), may hold values from 0 to 15, all different within a row
- route_order: int32 [4, 2, 4096], P('weights', 'context'), may hold values from 0 to 4095, each once within a row
Outputs:
- layer_out: bfloat16 [4, 1024, 2048], P('weights', 'context')
- grad_in: float32 [4, 1024, 2048], P('weights', 'context')
- grad_norm_gains: float32 [2048, 2], P(('weights', 'context', 'tensor'))
- grad_qkv: float32 [2048, 3, 2048], P(('weights', 'context'), None, 'tensor')
- grad_qk_gains: float32 [128, 2, 16], P(('weights', 'context'), None, 'tensor')
- grad_out_weight: float32 [2048, 2048], P(('weights', 'context'), 'tensor')
- grad_router: float32 [2048, 16], P(('weights', 'context'), 'tensor')
- grad_expert_in: float32 [16, 2, 2048, 1024], P(('weights', 'context'), None, None, 'tensor')
- grad_expert_out: float32 [16, 1024, 2048], P(('weights', 'context'), 'tensor')
Inputs may be any that keep to these rules, and one draw needn't show every extreme that they name: `segments`: segment numbers never fall along a sequence; each segment covers 1 to 512 tokens, and one covers exactly 512. The 8 routes of a token name different experts; every expert is named by some token. `route_order`: within each device block the 4096 values, over pairs in token-major order, are each of 0 to 4095 once.
All inputs are finite; a program needn't handle non-finite values.
Results may differ from a plain program's by a relative error of at most 0.015.
Values may be sent and summed in bfloat16 or wider, within the bound.
A program may use at most 384 MiB of HBM per device.

v0:
```python
import math

import jax
import jax.numpy as jnp
from jax import lax
from jax.sharding import PartitionSpec as P

epsilon = 1e-05
rotary_base = 10000.0


def passed_along(value, axis, steps):
    count = lax.axis_size(axis)
    leading, last = (max(0, -steps), min(count, count - steps))
    return lax.ppermute(value, axis, [(source, source + steps) for source in range(leading, last)])


def rotate_half(values_in):
    middle = values_in.shape[-1] // 2
    return jnp.concatenate([-values_in[..., middle:], values_in[..., :middle]], axis=-1)


def rotate_back(grads_in):
    middle = grads_in.shape[-1] // 2
    return jnp.concatenate([grads_in[..., middle:], -grads_in[..., :middle]], axis=-1)


def rotary_tables(positions, head_size):
    frequency = rotary_base ** (-(2.0 * jnp.arange(head_size // 2, dtype=jnp.float32)) / head_size)
    angle_table = positions.astype(jnp.float32)[:, None] * frequency[None, :]
    angle_table = jnp.concatenate([angle_table, angle_table], axis=1)
    return (jnp.cos(angle_table), jnp.sin(angle_table))


def place_pairs(pair_expert, rank, expert_total, capacity):
    pair_count = pair_expert.shape[0]
    by_rank = (
        jnp.zeros((pair_count,), jnp.int32).at[rank].set(jnp.arange(pair_count, dtype=jnp.int32))
    )
    sorted_expert = pair_expert[by_rank]
    onehot = (sorted_expert[:, None] == jnp.arange(expert_total, dtype=jnp.int32)[None, :]).astype(
        jnp.int32
    )
    running = jnp.cumsum(onehot, axis=0)
    sorted_slot = jnp.sum(running * onehot, axis=1) - 1
    slot_index = jnp.zeros((pair_count,), jnp.int32).at[by_rank].set(sorted_slot)
    kept_pair = slot_index < capacity
    dest_row = jnp.where(kept_pair, pair_expert * capacity + slot_index, expert_total * capacity)
    slot_pair = (
        jnp.full((expert_total * capacity + 1,), pair_count, jnp.int32)
        .at[dest_row]
        .set(jnp.arange(pair_count, dtype=jnp.int32))[:-1]
    )
    return (kept_pair, dest_row, slot_pair)


def row_sums(partial_rows):
    return lax.psum(partial_rows, "tensor")


def tensor_sum(partial_rows):
    return lax.psum(partial_rows, "tensor")


def to_owners(slot_rows):
    return lax.all_to_all(
        slot_rows, ("weights", "context"), split_axis=0, concat_axis=0, tiled=True
    )


def expert_front(slot_inputs, expert_in):
    both_pre = jnp.einsum(
        "sncd,ngdf->sncgf", slot_inputs, expert_in, preferred_element_type=jnp.float32
    )
    return (both_pre[..., 0, :], both_pre[..., 1, :])


def per_device(
    layer_in,
    norm_gains,
    qkv_weight,
    qk_gains,
    out_weight,
    router,
    expert_in,
    expert_out,
    grad_out,
    segments,
    routes,
    route_order,
):
    group_count = lax.axis_size(("weights", "context"))
    tensor_count = lax.axis_size("tensor")
    context_rank = lax.axis_index("context")
    tensor_rank = lax.axis_index("tensor")
    seq_count, half_len, model_width = layer_in.shape
    token_count = seq_count * half_len
    top_count = routes.shape[2]
    qkv_full, out_full, qk_gain_full, gain_full, router_full = (
        lax.all_gather(qkv_weight, ("weights", "context"), axis=0, tiled=True),
        lax.all_gather(out_weight, ("weights", "context"), axis=0, tiled=True),
        lax.all_gather(qk_gains, ("weights", "context"), axis=0, tiled=True),
        lax.all_gather(norm_gains, ("weights", "context"), axis=0, tiled=True),
        lax.all_gather(router, ("weights", "context"), axis=0, tiled=True),
    )
    head_size = qk_gain_full.shape[0]
    local_heads = qk_gain_full.shape[2]
    expert_total = router_full.shape[1]
    gain_attn = gain_full[:, 0].astype(jnp.float32)
    gain_ffn = gain_full[:, 1].astype(jnp.float32)
    query_gain = qk_gain_full[:, 0, :].astype(jnp.float32).T.reshape(-1)
    key_gain = qk_gain_full[:, 1, :].astype(jnp.float32).T.reshape(-1)
    inv_root = 1.0 / math.sqrt(head_size)
    residual = layer_in.reshape(token_count, model_width).astype(jnp.float32)
    scale_one = lax.rsqrt(jnp.mean(residual * residual, axis=1, keepdims=True) + epsilon)
    unit_one = residual * scale_one
    normed_one = (unit_one * gain_attn).astype(jnp.bfloat16)
    projected = jnp.einsum("td,dgf->tgf", normed_one, qkv_full, preferred_element_type=jnp.float32)
    query_raw = projected[:, 0]
    key_raw = projected[:, 1]
    value_raw = projected[:, 2]
    square_sums = row_sums(
        jnp.stack(
            [jnp.sum(query_raw * query_raw, axis=1), jnp.sum(key_raw * key_raw, axis=1)], axis=1
        )
    )
    query_scale = lax.rsqrt(square_sums[:, 0:1] / model_width + epsilon)
    key_scale = lax.rsqrt(square_sums[:, 1:2] / model_width + epsilon)
    heads_shape = (seq_count, half_len, local_heads, head_size)
    query_hat = (query_raw * query_scale * query_gain).reshape(heads_shape)
    key_hat = (key_raw * key_scale * key_gain).reshape(heads_shape)
    query_pos = context_rank * half_len + jnp.arange(half_len, dtype=jnp.int32)
    cosine_table, sine_table = rotary_tables(query_pos, head_size)
    cosine_table = cosine_table[None, :, None, :]
    sine_table = sine_table[None, :, None, :]
    query_rot = (query_hat * cosine_table + rotate_half(query_hat) * sine_table).astype(
        jnp.bfloat16
    )
    key_rot = (key_hat * cosine_table + rotate_half(key_hat) * sine_table).astype(jnp.bfloat16)
    value_low = value_raw.astype(jnp.bfloat16).reshape(heads_shape)
    key_prev, value_prev = passed_along((key_rot, value_low), "context", 1)
    all_keys = jnp.concatenate([key_prev, key_rot], axis=1)
    all_values = jnp.concatenate([value_prev, value_low], axis=1)
    key_pos = jnp.concatenate([query_pos - half_len, query_pos])
    seg_query = lax.dynamic_slice_in_dim(segments, context_rank * half_len, half_len, 1)
    seg_prev = lax.dynamic_slice_in_dim(
        segments, jnp.maximum(context_rank - 1, 0) * half_len, half_len, 1
    )
    seg_keys = jnp.concatenate([seg_prev, seg_query], axis=1)
    causal = (key_pos[None, :] >= 0) & (key_pos[None, :] <= query_pos[:, None])
    allowed = causal[None] & (seg_query[:, :, None] == seg_keys[:, None, :])

    def score_block(queries, key_rows):
        raw_scores = (
            jnp.einsum("sqhd,skhd->shqk", queries, key_rows, preferred_element_type=jnp.float32)
            * inv_root
        )
        return jnp.where(allowed[:, None], raw_scores, -1e30)

    scores = score_block(query_rot, all_keys)
    row_max = jnp.max(scores, axis=-1, keepdims=True)
    exponent = jnp.exp(scores - row_max)
    row_total = jnp.sum(exponent, axis=-1, keepdims=True)
    log_total = row_max + jnp.log(row_total)
    attn_probs = (exponent / row_total).astype(jnp.bfloat16)
    attended = jnp.einsum(
        "shqk,skhd->sqhd", attn_probs, all_values, preferred_element_type=jnp.float32
    )
    attended_low = attended.reshape(token_count, -1).astype(jnp.bfloat16)
    attn_partial = jnp.einsum(
        "tf,df->td", attended_low, out_full, preferred_element_type=jnp.float32
    )
    hidden = residual + tensor_sum(attn_partial)
    scale_two = lax.rsqrt(jnp.mean(hidden * hidden, axis=1, keepdims=True) + epsilon)
    unit_two = hidden * scale_two
    normed_two = (unit_two * gain_ffn).astype(jnp.bfloat16)
    logits = jnp.dot(normed_two, router_full, preferred_element_type=jnp.float32)
    router_probs = jax.nn.softmax(logits, axis=1)
    capacity = token_count * top_count * 9 // (8 * expert_total)
    local_experts = expert_in.shape[0]
    pair_count = token_count * top_count
    token_routes = routes.reshape(token_count, top_count)
    kept_pair, dest_row, slot_pair = place_pairs(
        token_routes.reshape(pair_count), route_order.reshape(pair_count), expert_total, capacity
    )
    zero_row = jnp.zeros((1, model_width), jnp.bfloat16)
    zero_wide = jnp.zeros((1, model_width), jnp.float32)
    slot_shape = (group_count, local_experts, capacity, model_width)
    dispatch_rows = jnp.concatenate([normed_two, zero_row], axis=0)[slot_pair // top_count].reshape(
        slot_shape
    )
    received = lax.all_to_all(
        dispatch_rows, ("weights", "context"), split_axis=0, concat_axis=0, tiled=True
    )
    gate_pre, up_pre = expert_front(received, expert_in)
    sigmoid_gate = jax.nn.sigmoid(gate_pre)
    silu_gate = gate_pre * sigmoid_gate
    activated = (silu_gate * up_pre).astype(jnp.bfloat16)
    expert_partial = jnp.einsum(
        "sncf,nfd->sncd", activated, expert_out, preferred_element_type=jnp.float32
    )
    kept_float = kept_pair.reshape(token_count, top_count).astype(jnp.float32)
    gate_weight = jnp.take_along_axis(router_probs, token_routes, axis=1) * kept_float
    upstream = grad_out.reshape(token_count, model_width).astype(jnp.float32)
    returned = to_owners(expert_partial).reshape(expert_total * capacity, model_width)
    picked = jnp.concatenate([returned, zero_wide], axis=0)[dest_row].reshape(
        token_count, top_count, model_width
    )
    moe_partial = jnp.sum(gate_weight[:, :, None] * picked, axis=1)
    dot_partial = jnp.sum(upstream[:, None, :] * picked, axis=2)
    moe_total, dot_total = lax.psum((moe_partial, dot_partial), "tensor")
    layer_out = (hidden + moe_total).astype(jnp.bfloat16).reshape(layer_in.shape)
    d_gate = dot_total * kept_float
    route_hot = (
        token_routes[:, :, None] == jnp.arange(expert_total, dtype=jnp.int32)[None, None, :]
    ).astype(jnp.float32)
    d_probs = jnp.sum(d_gate[:, :, None] * route_hot, axis=1)
    d_logits = (
        router_probs * (d_probs - jnp.sum(router_probs * d_probs, axis=1, keepdims=True))
    ).astype(jnp.bfloat16)
    d_pair = (
        (gate_weight[:, :, None] * upstream[:, None, :])
        .astype(jnp.bfloat16)
        .reshape(pair_count, model_width)
    )
    d_slots = jnp.concatenate([d_pair, zero_row], axis=0)[slot_pair].reshape(slot_shape)
    d_received = lax.all_to_all(
        d_slots, ("weights", "context"), split_axis=0, concat_axis=0, tiled=True
    )
    d_activated = jnp.einsum(
        "sncd,nfd->sncf", d_received, expert_out, preferred_element_type=jnp.float32
    )
    grad_expert_out = jnp.einsum(
        "sncf,sncd->nfd", activated, d_received, preferred_element_type=jnp.float32
    )
    d_gate_pre = d_activated * up_pre * sigmoid_gate * (1.0 + gate_pre * (1.0 - sigmoid_gate))
    d_up_pre = d_activated * silu_gate
    d_both = jnp.stack([d_gate_pre, d_up_pre], axis=3).astype(jnp.bfloat16)
    d_inputs = jnp.einsum("sncgf,ngdf->sncd", d_both, expert_in, preferred_element_type=jnp.float32)
    grad_expert_in = jnp.einsum(
        "sncd,sncgf->ngdf", received, d_both, preferred_element_type=jnp.float32
    )
    d_returned = to_owners(d_inputs).reshape(expert_total * capacity, model_width)
    d_normed_part = jnp.sum(
        jnp.concatenate([d_returned, zero_wide], axis=0)[dest_row].reshape(
            token_count, top_count, model_width
        ),
        axis=1,
    )
    d_normed_two = tensor_sum(d_normed_part) + jnp.dot(
        d_logits, router_full.T, preferred_element_type=jnp.float32
    )
    d_router = jnp.dot(normed_two.T, d_logits, preferred_element_type=jnp.float32)
    d_gain_ffn = jnp.sum(d_normed_two * unit_two, axis=0)
    scaled_ffn = gain_ffn * d_normed_two
    d_hidden = upstream + scale_two * (
        scaled_ffn - unit_two * jnp.mean(scaled_ffn * unit_two, axis=1, keepdims=True)
    )
    d_hidden_low = d_hidden.astype(jnp.bfloat16)
    d_out_weight = jnp.einsum(
        "td,tf->df", d_hidden_low, attended_low, preferred_element_type=jnp.float32
    )
    d_attended = (
        jnp.dot(d_hidden_low, out_full, preferred_element_type=jnp.float32)
        .astype(jnp.bfloat16)
        .reshape(heads_shape)
    )
    probs_again = jnp.exp(score_block(query_rot, all_keys) - log_total)
    probs_again_low = probs_again.astype(jnp.bfloat16)
    d_probs_att = jnp.einsum(
        "sqhd,skhd->shqk", d_attended, all_values, preferred_element_type=jnp.float32
    )
    d_values_all = jnp.einsum(
        "shqk,sqhd->skhd", probs_again_low, d_attended, preferred_element_type=jnp.float32
    )
    row_dot = jnp.sum(probs_again * d_probs_att, axis=-1, keepdims=True)
    d_scores = (probs_again * (d_probs_att - row_dot)).astype(jnp.bfloat16)
    d_query_rot = (
        jnp.einsum("shqk,skhd->sqhd", d_scores, all_keys, preferred_element_type=jnp.float32)
        * inv_root
    )
    d_keys_all = (
        jnp.einsum("shqk,sqhd->skhd", d_scores, query_rot, preferred_element_type=jnp.float32)
        * inv_root
    )
    back_key, back_value = (
        passed_along(d_keys_all[:, :half_len].astype(jnp.bfloat16), "context", -1).astype(
            jnp.float32
        ),
        passed_along(d_values_all[:, :half_len].astype(jnp.bfloat16), "context", -1).astype(
            jnp.float32
        ),
    )
    d_key_rot = d_keys_all[:, half_len:] + back_key
    d_value = (d_values_all[:, half_len:] + back_value).reshape(token_count, -1)
    d_query_hat = (d_query_rot * cosine_table + rotate_back(d_query_rot * sine_table)).reshape(
        token_count, -1
    )
    d_key_hat = (d_key_rot * cosine_table + rotate_back(d_key_rot * sine_table)).reshape(
        token_count, -1
    )
    centre = row_sums(
        jnp.stack(
            [
                jnp.sum(query_gain * d_query_hat * query_raw, axis=1),
                jnp.sum(key_gain * d_key_hat * key_raw, axis=1),
            ],
            axis=1,
        )
    )
    d_query_raw = (
        query_scale * query_gain * d_query_hat
        - query_raw * (query_scale**3 / model_width) * centre[:, 0:1]
    )
    d_key_raw = (
        key_scale * key_gain * d_key_hat - key_raw * (key_scale**3 / model_width) * centre[:, 1:2]
    )
    d_query_gain = (
        jnp.sum(d_query_hat * query_raw * query_scale, axis=0).reshape(local_heads, head_size).T
    )
    d_key_gain = jnp.sum(d_key_hat * key_raw * key_scale, axis=0).reshape(local_heads, head_size).T
    d_qk_gains = jnp.stack([d_query_gain, d_key_gain], axis=1)
    d_projected = jnp.stack([d_query_raw, d_key_raw, d_value], axis=1).astype(jnp.bfloat16)
    d_normed_one = tensor_sum(
        jnp.einsum("tgf,dgf->td", d_projected, qkv_full, preferred_element_type=jnp.float32)
    )
    d_qkv = jnp.einsum("td,tgf->dgf", normed_one, d_projected, preferred_element_type=jnp.float32)
    d_gain_attn = jnp.sum(d_normed_one * unit_one, axis=0)
    scaled_attn = gain_attn * d_normed_one
    grad_in = d_hidden + scale_one * (
        scaled_attn - unit_one * jnp.mean(scaled_attn * unit_one, axis=1, keepdims=True)
    )
    d_norm_gains = jnp.stack([d_gain_attn, d_gain_ffn], axis=1)
    grad_qkv, grad_out_weight, grad_qk_gains, gain_rows, router_rows = (
        lax.psum_scatter(d_qkv, ("weights", "context"), scatter_dimension=0, tiled=True),
        lax.psum_scatter(d_out_weight, ("weights", "context"), scatter_dimension=0, tiled=True),
        lax.psum_scatter(d_qk_gains, ("weights", "context"), scatter_dimension=0, tiled=True),
        lax.psum_scatter(d_norm_gains, ("weights", "context"), scatter_dimension=0, tiled=True),
        lax.psum_scatter(d_router, ("weights", "context"), scatter_dimension=0, tiled=True),
    )
    gain_share = gain_rows.shape[0] // tensor_count
    grad_norm_gains = lax.dynamic_slice_in_dim(gain_rows, tensor_rank * gain_share, gain_share, 0)
    router_share = expert_total // tensor_count
    grad_router = lax.dynamic_slice_in_dim(router_rows, tensor_rank * router_share, router_share, 1)
    return (
        layer_out,
        grad_in.reshape(layer_in.shape),
        grad_norm_gains,
        grad_qkv,
        grad_qk_gains,
        grad_out_weight,
        grad_router,
        grad_expert_in,
        grad_expert_out,
    )


def solution(mesh):
    placed = (
        P("weights", "context", None),
        P(("weights", "context"), None),
        P(("weights", "context"), None, "tensor"),
        P(("weights", "context"), None, "tensor"),
        P(("weights", "context"), "tensor"),
        P(("weights", "context"), None),
        P(("weights", "context"), None, None, "tensor"),
        P(("weights", "context"), "tensor", None),
        P("weights", "context", None),
        P("weights", None),
        P("weights", "context", None),
        P("weights", "context", None),
    )
    return jax.shard_map(
        per_device,
        mesh=mesh,
        in_specs=placed,
        out_specs=(
            P("weights", "context", None),
            P("weights", "context", None),
            P(("weights", "context", "tensor"), None),
            P(("weights", "context"), None, "tensor"),
            P(("weights", "context"), None, "tensor"),
            P(("weights", "context"), "tensor"),
            P(("weights", "context"), "tensor"),
            P(("weights", "context"), None, None, "tensor"),
            P(("weights", "context"), "tensor", None),
        ),
        check_vma=False,
    )
```

profile of v0, /device:TPU:0, one launch (start us, length us, event | category | flops | bytes accessed | tf_op | source)
XLA Modules:
  0.0 2391.7 jit_solution(14579723764830482774)
XLA Ops:
  37.8 22.4 all-gather.3.cloned.1.call-done
  106.4 15.5 scatter_custom_fusion
  122.0 23.0 gather_fusion
  150.7 15.5 scatter_custom_fusion.1
  175.7 81.8 %all-reduce.9.cloned.1.call-done = f32[512,2048]{1,0:T(8,128)} async-done(((f32[512,2048]{1,0:T(8,128)}), f32[512,2048]{1,0:T(8,128)}) %all-reduce.9.cloned.1.call-update) | async-done | bytes 4194320 | tf_op jit(solution)/shard_map/psum | solution.py:62
  264.2 33.0 %gather_fusion.5 = f32[4096]{0:T(1024)S(1)} fusion(f32[512,16]{0,1:T(8,128)S(1)} %fusion.91, s32[4096]{0:T(1024)S(1)} %reshape.887), kind=kCustom, calls=%fused_computation.5 | custom fusion | bytes 65536 | tf_op jit(solution)/shard_map/jit(take_along_axis)/gather | solution.py:203
  298.0 15.5 scatter_custom_fusion.2
  316.7 36.9 %gather_fusion.1 = bf16[4608,2048]{1,0:T(8,128)(2,1)} fusion(bf16[513,2048]{1,0:T(8,128)(2,1)} %concatenate.76, s32[5120]{0:T(1024)S(1)} %pad_clamp_fusion.1), kind=kCustom, calls=%fused_computation.1 | custom fusion | bytes 37767168 | tf_op jit(solution)/shard_map/gather | solution.py:189
  372.8 43.0 %gather_fusion.3 = bf16[4608,2048]{1,0:T(8,128)(2,1)} fusion(bf16[4097,2048]{1,0:T(8,128)(2,1)} %concatenate.78, s32[5120]{0:T(1024)S(1)} %pad_clamp_fusion), kind=kCustom, calls=%fused_computation.3 | custom fusion | bytes 37767168 | tf_op jit(solution)/shard_map/gather | solution.py:226
  415.9 150.2 %all-to-all-done = bf16[8,2,288,2048]{3,2,1,0:T(8,128)(2,1)} async-done(((bf16[8,2,288,2048]{3,2,1,0:T(8,128)(2,1)}), bf16[8,2,288,2048]{3,2,1,0:T(8,128)(2,1)}, u32[]{:S(2)}, u32[]{:S(2)}) %all-to-all-start) | async-done | bytes 18874400 | tf_op jit(solution)/shard_map/all_to_all | solution.py:192
  572.2 17.3 fusion.43
  589.4 189.2 %all-to-all-done.2 = bf16[8,2,288,2048]{3,2,1,0:T(8,128)(2,1)} async-done(((bf16[8,2,288,2048]{3,2,1,0:T(8,128)(2,1)}), bf16[8,2,288,2048]{3,2,1,0:T(8,128)(2,1)}, u32[]{:S(2)}, u32[]{:S(2)}) %all-to-all-start.2) | async-done | bytes 18874400 | tf_op jit(solution)/shard_map/all_to_all | solution.py:227
  778.6 14.5 fusion.52
  793.1 20.3 fusion.39
  813.5 27.6 %copy.245 = f32[2,8,288,2048,1]{3,2,0,1,4:T(8,128)} copy(f32[2,8,288,2048,1]{3,2,1,0,4:T(8,128)} %fusion.39) | data formatting | bytes 75497472 | tf_op jit(solution)/shard_map/sncgf,ngdf->sncd/dot_general | solution.py:239
  848.7 16.6 convolution_bitcast_fusion
  865.2 27.5 %copy.161 = f32[8,2,288,2048]{3,2,1,0:T(8,128)} copy(f32[8,2,288,2048]{3,2,0,1:T(8,128)} %convolution_bitcast_fusion) | data formatting | bytes 75497472 | tf_op jit(solution)/shard_map/sncf,nfd->sncd/transpose | solution.py:199
  892.8 364.6 %all-to-all-done.3 = f32[8,2,288,2048]{3,2,1,0:T(8,128)} async-done(((f32[8,2,288,2048]{3,2,1,0:T(8,128)}), f32[8,2,288,2048]{3,2,1,0:T(8,128)}, u32[]{:S(2)}, u32[]{:S(2)}) %all-to-all-start.3) | async-done | bytes 37748768 | tf_op jit(solution)/shard_map/all_to_all | solution.py:66
  1265.0 27.4 %concatenate.79 = f32[4609,2048]{1,0:T(8,128)} pad(f32[4608,2048]{1,0:T(8,128)} %bitcast.59, f32[]{:T(128)} %constant.35.clone.1), padding=0_1x0_0 | pad | bytes 75505664 | tf_op jit(solution)/shard_map/concatenate | solution.py:245
  1292.4 43.2 %gather_fusion.4 = f32[4096,2048]{1,0:T(8,128)} fusion(f32[4609,2048]{1,0:T(8,128)} %concatenate.79, s32[4096]{0:T(1024)S(1)} %copy-done.49), kind=kCustom, calls=%fused_computation.4 | custom fusion | bytes 67125248 | tf_op jit(solution)/shard_map/gather | solution.py:245
  1335.7 17.0 bitcast_reduce_fusion
  1354.4 319.2 %all-to-all-done.1 = f32[8,2,288,2048]{3,2,1,0:T(8,128)} async-done(((f32[8,2,288,2048]{3,2,1,0:T(8,128)}), f32[8,2,288,2048]{3,2,1,0:T(8,128)}, u32[]{:S(2)}, u32[]{:S(2)}) %all-to-all-start.1) | async-done | bytes 37748768 | tf_op jit(solution)/shard_map/all_to_all | solution.py:66
  1673.6 27.4 %concatenate.77 = f32[4609,2048]{1,0:T(8,128)} pad(f32[4608,2048]{1,0:T(8,128)} %bitcast.45, f32[]{:T(128)} %constant.35.clone.1), padding=0_1x0_0 | pad | bytes 75505664 | tf_op jit(solution)/shard_map/concatenate | solution.py:206
  1701.0 43.2 %gather_fusion.2 = f32[4096,2048]{1,0:T(8,128)} fusion(f32[4609,2048]{1,0:T(8,128)} %concatenate.77, s32[4096]{0:T(1024)S(1)} %copy-done.49), kind=kCustom, calls=%fused_computation.2 | custom fusion | bytes 67125248 | tf_op jit(solution)/shard_map/gather | solution.py:206
  1744.3 16.7 fusion.2
  1761.0 21.8 psum.53
  1835.3 285.7 %all-reduce.13.cloned.1.call-done = (f32[512,2048]{1,0:T(8,128)}, f32[512,2048]{1,0:T(8,128)}) async-done(((f32[512,2048]{1,0:T(8,128)}, f32[512,2048]{1,0:T(8,128)}), (f32[512,2048]{1,0:T(8,128)}, f32[512,2048]{1,0:T(8,128)})) %all-reduce.13.cloned.1.call-update) | async-done | bytes 8388624 | tf_op jit(solution)/shard_map/psum | solution.py:211
  2141.5 17.3 fusion.23
  2179.9 13.5 reduce-scatter.18.cloned.1.call-done
  2205.1 27.5 %reduce-scatter.16.cloned.1.call-done = f32[256,2]{1,0:T(8,128)} async-done(((f32[2048,2]{1,0:T(8,128)}), f32[256,2]{1,0:T(8,128)}) %reduce-scatter.16.cloned.1.call-update) | async-done | bytes 2064
  2234.1 53.9 %reduce-scatter.12.cloned.1.call-done = f32[256,512]{1,0:T(8,128)} async-done(((f32[2048,512]{1,0:T(8,128)}), f32[256,512]{1,0:T(8,128)}) %reduce-scatter.12.cloned.1.call-update) | async-done | bytes 524304 | tf_op jit(solution)/shard_map/reduce_scatter | solution.py:336
  2287.9 96.8 %reduce-scatter.10.cloned.1.call-done = f32[256,3,512]{2,0,1:T(8,128)} async-done(((f32[2048,3,512]{2,0,1:T(8,128)}), f32[256,3,512]{2,0,1:T(8,128)}) %reduce-scatter.10.cloned.1.call-update) | async-done | bytes 1572880 | tf_op jit(solution)/shard_map/reduce_scatter | solution.py:335
  (334 shorter events, 250.6 us)
Async XLA Ops:
  7.2 771.4 %copy-start = (bf16[2,256,2048]{2,1,0:T(8,128)(2,1)S(1)}, bf16[2,256,2048]{2,1,0:T(8,128)(2,1)}, u32[]{:S(2)}) copy-start(bf16[2,256,2048]{2,1,0:T(8,128)(2,1)} %param.19) | copy-start | bytes 6291460
  7.2 53.0 %all-gather.3.cloned.1.call-start = ((), (), s32[]{:S(2)}) async-start(), calls=%async_computation.9 | async-start | bytes 7077888 | tf_op jit(solution)/shard_map/all_gather | solution.py:100
  9.7 90.2 %all-gather.5.cloned.1.call-start = ((), (), s32[]{:S(2)}) async-start(), calls=%async_computation.10 | async-start | bytes 2359296 | tf_op jit(solution)/shard_map/all_gather | solution.py:101
  10.5 247.0 %all-reduce.9.cloned.1.call-start = ((), (), s32[]{:S(2)}) async-start(), calls=%async_computation.11 | async-start | bytes 8388608 | tf_op jit(solution)/shard_map/psum | solution.py:62
  12.7 53.9 %copy-start.76 = (f32[512]{0:T(512)}, f32[512]{0:T(512)S(1)}, u32[]{:S(2)}) copy-start(f32[512]{0:T(512)S(1)} %add_rsqrt_fusion.1) | copy-start | bytes 6148
  23.2 43.4 %copy-start.54 = (f32[2048,1]{0,1:T(1,128)}, f32[2048,1]{0,1:T(1,128)S(1)}, u32[]{:S(2)}) copy-start(f32[2048,1]{0,1:T(1,128)S(1)} %get-tuple-element.106) | copy-start | bytes 24580
  23.2 237.8 %copy-start.52 = (f32[2048,1]{0,1:T(1,128)}, f32[2048,1]{0,1:T(1,128)S(1)}, u32[]{:S(2)}) copy-start(f32[2048,1]{0,1:T(1,128)S(1)} %get-tuple-element.105) | copy-start | bytes 24580
  32.6 53.9 %copy-start.58 = (f32[4,128]{1,0:T(4,128)}, f32[4,128]{1,0:T(4,128)S(1)}, u32[]{:S(2)}) copy-start(f32[4,128]{1,0:T(4,128)S(1)} %copy.154) | copy-start | bytes 6148
  32.7 58.1 %copy-start.62 = (f32[4,128]{1,0:T(4,128)}, f32[4,128]{1,0:T(4,128)S(1)}, u32[]{:S(2)}) copy-start(f32[4,128]{1,0:T(4,128)S(1)} %copy.149) | copy-start | bytes 6148
  34.7 51.9 %copy-start.23 = (f32[512,128]{1,0:T(8,128)}, f32[512,128]{1,0:T(8,128)S(1)}, u32[]{:S(2)}) copy-start(f32[512,128]{1,0:T(8,128)S(1)} %get-tuple-element.98) | copy-start | bytes 786436
  82.4 12.8 collective-permute-start
  87.6 3.5 collective-permute-start.1
  122.0 44.2 %copy-start.81 = (bf16[256,16]{0,1:T(8,128)(2,1)S(1)}, bf16[256,16]{0,1:T(8,128)(2,1)}, u32[]{:S(2)}) copy-start(bf16[256,16]{0,1:T(8,128)(2,1)} %param.17) | copy-start | bytes 24580
  175.7 85.8 %copy-start.43 = (bf16[2048,16]{0,1:T(8,128)(2,1)}, bf16[2048,16]{0,1:T(8,128)(2,1)S(1)}, u32[]{:S(2)}) copy-start(bf16[2048,16]{0,1:T(8,128)(2,1)S(1)} %all_gather.19) | copy-start | bytes 196612
  297.3 56.4 %copy-start.21 = (f32[4096]{0:T(1024)}, f32[4096]{0:T(1024)S(1)}, u32[]{:S(2)}) copy-start(f32[4096]{0:T(1024)S(1)} %gather_fusion.5) | copy-start | bytes 49156
  297.3 56.4 %copy-start.66 = (pred[4096]{0:T(1024)(128)(4,1)}, pred[4096]{0:T(1024)(128)(4,1)S(1)}, u32[]{:S(2)}) copy-start(pred[4096]{0:T(1024)(128)(4,1)S(1)} %get-tuple-element.75) | copy-start | bytes 12292
  353.7 212.3 %all-to-all-start = ((bf16[8,2,288,2048]{3,2,1,0:T(8,128)(2,1)}), bf16[8,2,288,2048]{3,2,1,0:T(8,128)(2,1)}, u32[]{:S(2)}, u32[]{:S(2)}) async-start(bf16[8,2,288,2048]{3,2,1,0:T(8,128)(2,1)} %bitcast.293), calls=%async_computation | async-start | bytes 37748736 | tf_op jit(solution)/shard_map/all_to_all | solution.py:192
  566.0 212.6 %all-to-all-start.2 = ((bf16[8,2,288,2048]{3,2,1,0:T(8,128)(2,1)}), bf16[8,2,288,2048]{3,2,1,0:T(8,128)(2,1)}, u32[]{:S(2)}, u32[]{:S(2)}) async-start(bf16[8,2,288,2048]{3,2,1,0:T(8,128)(2,1)} %bitcast.294), calls=%async_computation.2 | async-start | bytes 37748736 | tf_op jit(solution)/shard_map/all_to_all | solution.py:227
  841.0 416.3 %all-to-all-start.3 = ((f32[8,2,288,2048]{3,2,1,0:T(8,128)}), f32[8,2,288,2048]{3,2,1,0:T(8,128)}, u32[]{:S(2)}, u32[]{:S(2)}) async-start(f32[8,2,288,2048]{3,2,1,0:T(8,128)} %bitcast.290), calls=%async_computation.3 | async-start | bytes 75497472 | tf_op jit(solution)/shard_map/all_to_all | solution.py:66
  1257.3 416.3 %all-to-all-start.1 = ((f32[8,2,288,2048]{3,2,1,0:T(8,128)}), f32[8,2,288,2048]{3,2,1,0:T(8,128)}, u32[]{:S(2)}, u32[]{:S(2)}) async-start(f32[8,2,288,2048]{3,2,1,0:T(8,128)} %copy.161), calls=%async_computation.1 | async-start | bytes 75497472 | tf_op jit(solution)/shard_map/all_to_all | solution.py:66
  1265.0 518.1 %all-reduce.11.cloned.1.call-start = ((), (), s32[]{:S(2)}) async-start(), calls=%async_computation.12 | async-start | bytes 8388608 | tf_op jit(solution)/shard_map/psum | solution.py:62
  1352.7 768.3 %all-reduce.13.cloned.1.call-start = ((), (), s32[]{:S(2)}) async-start(), calls=%async_computation.18 | async-start | bytes 16777216 | tf_op jit(solution)/shard_map/psum | solution.py:211
  1795.0 27.6 %collective-permute-start.3 = (bf16[1,512,4,128]{1,3,2,0:T(8,128)(2,1)}, bf16[1,512,4,128]{1,3,2,0:T(8,128)(2,1)}, u32[]{:S(2)}, u32[]{:S(2)}) collective-permute-start(bf16[1,512,4,128]{1,3,2,0:T(8,128)(2,1)} %slice.221), channel_id=1, source_target_pairs={{4,0},{5,1},{6,2},{7,3},{12,8},{13,9},{14,10},{15,11},{20,16},{21,... | collective-permute-start | bytes 1572872 | tf_op jit(solution)/shard_map/ppermute | solution.py:15
  1803.0 4.7 collective-permute-start.2
  1831.8 289.2 %copy-start.55 = (f32[2048,1]{0,1:T(1,128)S(1)}, f32[2048,1]{0,1:T(1,128)}, u32[]{:S(2)}) copy-start(f32[2048,1]{0,1:T(1,128)} %copy-done.54) | copy-start | bytes 24580
  1831.8 289.2 %copy-start.77 = (f32[512]{0:T(512)S(1)}, f32[512]{0:T(512)}, u32[]{:S(2)}) copy-start(f32[512]{0:T(512)} %copy-done.76) | copy-start | bytes 6148
  1831.8 346.8 %reduce-scatter.14.cloned.1.call-start = ((), (), s32[]{:S(2)}) async-start(), calls=%async_computation.15 | async-start | bytes 147456 | tf_op jit(solution)/shard_map/reduce_scatter | solution.py:339
  1834.4 359.0 %reduce-scatter.18.cloned.1.call-start = ((), (), s32[]{:S(2)}) async-start(), calls=%async_computation.17 | async-start | bytes 73728
  1835.2 397.4 %reduce-scatter.16.cloned.1.call-start = ((), (), s32[]{:S(2)}) async-start(), calls=%async_computation.16 | async-start | bytes 1179648
  2126.4 161.5 %reduce-scatter.12.cloned.1.call-start = ((), (), s32[]{:S(2)}) async-start(), calls=%async_computation.14 | async-start | bytes 4718592 | tf_op jit(solution)/shard_map/reduce_scatter | solution.py:336
  2132.1 252.6 %reduce-scatter.10.cloned.1.call-start = ((), (), s32[]{:S(2)}) async-start(), calls=%async_computation.13 | async-start | bytes 14155776 | tf_op jit(solution)/shard_map/reduce_scatter | solution.py:335
  2194.8 189.9 %copy-start.1 = (bf16[2,256,2048]{2,1,0:T(8,128)(2,1)S(1)}, bf16[2,256,2048]{2,1,0:T(8,128)(2,1)}, u32[]{:S(2)}) copy-start(bf16[2,256,2048]{2,1,0:T(8,128)(2,1)} %param.19) | copy-start | bytes 6291460
  (73 other events, 618.7 us)
Sparse Core Ops, SparseCore 0:
  10.5 49.6 all-gather.2
  62.1 27.8 all-gather.4
  105.2 152.2 all-reduce.8
  1352.8 154.3 all-reduce.10
  1831.9 289.0 all-reduce.12
  2124.5 32.3 reduce-scatter.13
  2160.1 33.2 reduce-scatter.17
  2196.6 36.0 reduce-scatter.15
  2236.6 51.2 reduce-scatter.11
  2292.3 92.4 reduce-scatter.9
where the time goes:
time: 2400 us; the launch traced here: 2390 us
  waiting for transfers between devices  1610 us (67%)
  local copies, waits for them, and re-layouts  429 us (18%)
  matrix products  151 us (6%)
  other arithmetic  82.8 us (3%)
  blocking collectives  71.5 us (3%)
  starting transfers between devices  34.2 us (1%)
    all_to_all x2, waiting for transfers between devices, to_owners(): lax.all_to_all(slot_rows, ('weights', 'context'), split_axis=0, concat_ax...  684 us
    psum x1, waiting for transfers between devices, per_device(): moe_total, dot_total = lax.psum((moe_partial, dot_partial), 'tensor')  286 us
    all_to_all x1, waiting for transfers between devices, per_device(): lax.all_to_all(d_slots, ('weights', 'context'), split_axis=0, concat_axis...  189 us
    all_to_all x1, waiting for transfers between devices, per_device(): lax.all_to_all(dispatch_rows, ('weights', 'context'), split_axis=0, conca...  150 us
    reduce_scatter x1, waiting for transfers between devices, per_device(): lax.psum_scatter(d_qkv, ('weights', 'context'), scatter_dimension=0, tile...  96.8 us
    psum x2, waiting for transfers between devices, tensor_sum(): return lax.psum(partial_rows, 'tensor')  81.8 us
    reduce_scatter x1, waiting for transfers between devices, per_device(): lax.psum_scatter(d_out_weight, ('weights', 'context'), scatter_dimension=...  53.9 us
  transfers between devices with their start and end apart: 18, of which 12 were waited for; matrix products, arithmetic and copies ran while one was open for 20% of the time, Pallas kernels for 0%

commit v1 on v0

--- a/solution.py
+++ b/solution.py
@@ -1,12 +1,22 @@
+import functools
 import math
 
 import jax
 import jax.numpy as jnp
 from jax import lax
+from jax.experimental import pallas as pl
+from jax.experimental.pallas import tpu as pltpu
 from jax.sharding import PartitionSpec as P
 
 epsilon = 1e-05
 rotary_base = 10000.0
+WEIGHTS, CONTEXT, TENSOR = ("weights", "context", "tensor")
+GROUP = (WEIGHTS, CONTEXT)
+EVERYONE = (WEIGHTS, CONTEXT, TENSOR)
+MESH = pl.DeviceIdType.MESH
+BY_SCORE = "sqhd,skhd->shqk"
+BY_QUERY = "shqk,skhd->sqhd"
+BY_KEY = "shqk,sqhd->skhd"
 
 
 def passed_along(value, axis, steps):
@@ -32,18 +42,19 @@
     return (jnp.cos(angle_table), jnp.sin(angle_table))
 
 
-def place_pairs(pair_expert, rank, expert_total, capacity):
+def pair_slots(token_routes, token_ranks, expert_total):
+    unused = token_routes.size
+    hot = token_routes.T[None] == jnp.arange(expert_total, dtype=jnp.int32)[:, None, None]
+    rank_of = jnp.min(jnp.where(hot, token_ranks.T[None], unused), axis=1)
+    slot_of = jnp.sum((rank_of[:, :, None] < rank_of[:, None, :]).astype(jnp.int32), axis=1)
+    return (rank_of < unused, slot_of)
+
+
+def place_pairs(pair_expert, rank, expert_total, capacity, top_count):
     pair_count = pair_expert.shape[0]
-    by_rank = (
-        jnp.zeros((pair_count,), jnp.int32).at[rank].set(jnp.arange(pair_count, dtype=jnp.int32))
-    )
-    sorted_expert = pair_expert[by_rank]
-    onehot = (sorted_expert[:, None] == jnp.arange(expert_total, dtype=jnp.int32)[None, :]).astype(
-        jnp.int32
-    )
-    running = jnp.cumsum(onehot, axis=0)
-    sorted_slot = jnp.sum(running * onehot, axis=1) - 1
-    slot_index = jnp.zeros((pair_count,), jnp.int32).at[by_rank].set(sorted_slot)
+    token_routes = pair_expert.reshape(-1, top_count)
+    slot_of = pair_slots(token_routes, rank.reshape(-1, top_count), expert_total)[1]
+    slot_index = jnp.take_along_axis(slot_of.T, token_routes, axis=1).reshape(pair_count)
     kept_pair = slot_index < capacity
     dest_row = jnp.where(kept_pair, pair_expert * capacity + slot_index, expert_total * capacity)
     slot_pair = (
@@ -55,16 +66,16 @@
 
 
 def row_sums(partial_rows):
-    return lax.psum(partial_rows, "tensor")
+    return lax.psum(partial_rows, TENSOR)
 
 
 def tensor_sum(partial_rows):
-    return lax.psum(partial_rows, "tensor")
+    return lax.psum(partial_rows, TENSOR)
 
 
 def to_owners(slot_rows):
     return lax.all_to_all(
-        slot_rows, ("weights", "context"), split_axis=0, concat_axis=0, tiled=True
+        slot_rows, GROUP, split_axis=0, concat_axis=0, tiled=True
     )
 
 
@@ -75,7 +86,7 @@
     return (both_pre[..., 0, :], both_pre[..., 1, :])
 
 
-def per_device(
+def per_device_slots(
     layer_in,
     norm_gains,
     qkv_weight,
@@ -89,19 +100,19 @@
     routes,
     route_order,
 ):
-    group_count = lax.axis_size(("weights", "context"))
-    tensor_count = lax.axis_size("tensor")
-    context_rank = lax.axis_index("context")
-    tensor_rank = lax.axis_index("tensor")
+    group_count = lax.axis_size(GROUP)
+    tensor_count = lax.axis_size(TENSOR)
+    context_rank = lax.axis_index(CONTEXT)
+    tensor_rank = lax.axis_index(TENSOR)
     seq_count, half_len, model_width = layer_in.shape
     token_count = seq_count * half_len
     top_count = routes.shape[2]
     qkv_full, out_full, qk_gain_full, gain_full, router_full = (
-        lax.all_gather(qkv_weight, ("weights", "context"), axis=0, tiled=True),
-        lax.all_gather(out_weight, ("weights", "context"), axis=0, tiled=True),
-        lax.all_gather(qk_gains, ("weights", "context"), axis=0, tiled=True),
-        lax.all_gather(norm_gains, ("weights", "context"), axis=0, tiled=True),
-        lax.all_gather(router, ("weights", "context"), axis=0, tiled=True),
+        lax.all_gather(qkv_weight, GROUP, axis=0, tiled=True),
+        lax.all_gather(out_weight, GROUP, axis=0, tiled=True),
+        lax.all_gather(qk_gains, GROUP, axis=0, tiled=True),
+        lax.all_gather(norm_gains, GROUP, axis=0, tiled=True),
+        lax.all_gather(router, GROUP, axis=0, tiled=True),
     )
     head_size = qk_gain_full.shape[0]
     local_heads = qk_gain_full.shape[2]
@@ -138,7 +149,7 @@
     )
     key_rot = (key_hat * cosine_table + rotate_half(key_hat) * sine_table).astype(jnp.bfloat16)
     value_low = value_raw.astype(jnp.bfloat16).reshape(heads_shape)
-    key_prev, value_prev = passed_along((key_rot, value_low), "context", 1)
+    key_prev, value_prev = passed_along((key_rot, value_low), CONTEXT, 1)
     all_keys = jnp.concatenate([key_prev, key_rot], axis=1)
     all_values = jnp.concatenate([value_prev, value_low], axis=1)
     key_pos = jnp.concatenate([query_pos - half_len, query_pos])
@@ -152,7 +163,7 @@
 
     def score_block(queries, key_rows):
         raw_scores = (
-            jnp.einsum("sqhd,skhd->shqk", queries, key_rows, preferred_element_type=jnp.float32)
+            jnp.einsum(BY_SCORE, queries, key_rows, preferred_element_type=jnp.float32)
             * inv_root
         )
         return jnp.where(allowed[:, None], raw_scores, -1e30)
@@ -164,7 +175,7 @@
     log_total = row_max + jnp.log(row_total)
     attn_probs = (exponent / row_total).astype(jnp.bfloat16)
     attended = jnp.einsum(
-        "shqk,skhd->sqhd", attn_probs, all_values, preferred_element_type=jnp.float32
+        BY_QUERY, attn_probs, all_values, preferred_element_type=jnp.float32
     )
     attended_low = attended.reshape(token_count, -1).astype(jnp.bfloat16)
     attn_partial = jnp.einsum(
@@ -181,7 +192,7 @@
     pair_count = token_count * top_count
     token_routes = routes.reshape(token_count, top_count)
     kept_pair, dest_row, slot_pair = place_pairs(
-        token_routes.reshape(pair_count), route_order.reshape(pair_count), expert_total, capacity
+        token_routes.reshape(pair_count), route_order.reshape(pair_count), expert_total, capacity, top_count
     )
     zero_row = jnp.zeros((1, model_width), jnp.bfloat16)
     zero_wide = jnp.zeros((1, model_width), jnp.float32)
@@ -190,7 +201,7 @@
         slot_shape
     )
     received = lax.all_to_all(
-        dispatch_rows, ("weights", "context"), split_axis=0, concat_axis=0, tiled=True
+        dispatch_rows, GROUP, split_axis=0, concat_axis=0, tiled=True
     )
     gate_pre, up_pre = expert_front(received, expert_in)
     sigmoid_gate = jax.nn.sigmoid(gate_pre)
@@ -208,7 +219,7 @@
     )
     moe_partial = jnp.sum(gate_weight[:, :, None] * picked, axis=1)
     dot_partial = jnp.sum(upstream[:, None, :] * picked, axis=2)
-    moe_total, dot_total = lax.psum((moe_partial, dot_partial), "tensor")
+    moe_total, dot_total = lax.psum((moe_partial, dot_partial), TENSOR)
     layer_out = (hidden + moe_total).astype(jnp.bfloat16).reshape(layer_in.shape)
     d_gate = dot_total * kept_float
     route_hot = (
@@ -225,7 +236,7 @@
     )
     d_slots = jnp.concatenate([d_pair, zero_row], axis=0)[slot_pair].reshape(slot_shape)
     d_received = lax.all_to_all(
-        d_slots, ("weights", "context"), split_axis=0, concat_axis=0, tiled=True
+        d_slots, GROUP, split_axis=0, concat_axis=0, tiled=True
     )
     d_activated = jnp.einsum(
         "sncd,nfd->sncf", d_received, expert_out, preferred_element_type=jnp.float32
@@ -268,26 +279,26 @@
     probs_again = jnp.exp(score_block(query_rot, all_keys) - log_total)
     probs_again_low = probs_again.astype(jnp.bfloat16)
     d_probs_att = jnp.einsum(
-        "sqhd,skhd->shqk", d_attended, all_values, preferred_element_type=jnp.float32
+        BY_SCORE, d_attended, all_values, preferred_element_type=jnp.float32
     )
     d_values_all = jnp.einsum(
-        "shqk,sqhd->skhd", probs_again_low, d_attended, preferred_element_type=jnp.float32
+        BY_KEY, probs_again_low, d_attended, preferred_element_type=jnp.float32
     )
     row_dot = jnp.sum(probs_again * d_probs_att, axis=-1, keepdims=True)
     d_scores = (probs_again * (d_probs_att - row_dot)).astype(jnp.bfloat16)
     d_query_rot = (
-        jnp.einsum("shqk,skhd->sqhd", d_scores, all_keys, preferred_element_type=jnp.float32)
+        jnp.einsum(BY_QUERY, d_scores, all_keys, preferred_element_type=jnp.float32)
         * inv_root
     )
     d_keys_all = (
-        jnp.einsum("shqk,sqhd->skhd", d_scores, query_rot, preferred_element_type=jnp.float32)
+        jnp.einsum(BY_KEY, d_scores, query_rot, preferred_element_type=jnp.float32)
         * inv_root
     )
     back_key, back_value = (
-        passed_along(d_keys_all[:, :half_len].astype(jnp.bfloat16), "context", -1).astype(
+        passed_along(d_keys_all[:, :half_len].astype(jnp.bfloat16), CONTEXT, -1).astype(
             jnp.float32
         ),
-        passed_along(d_values_all[:, :half_len].astype(jnp.bfloat16), "context", -1).astype(
+        passed_along(d_values_all[:, :half_len].astype(jnp.bfloat16), CONTEXT, -1).astype(
             jnp.float32
         ),
     )
@@ -332,11 +343,11 @@
     )
     d_norm_gains = jnp.stack([d_gain_attn, d_gain_ffn], axis=1)
     grad_qkv, grad_out_weight, grad_qk_gains, gain_rows, router_rows = (
-        lax.psum_scatter(d_qkv, ("weights", "context"), scatter_dimension=0, tiled=True),
-        lax.psum_scatter(d_out_weight, ("weights", "context"), scatter_dimension=0, tiled=True),
-        lax.psum_scatter(d_qk_gains, ("weights", "context"), scatter_dimension=0, tiled=True),
-        lax.psum_scatter(d_norm_gains, ("weights", "context"), scatter_dimension=0, tiled=True),
-        lax.psum_scatter(d_router, ("weights", "context"), scatter_dimension=0, tiled=True),
+        lax.psum_scatter(d_qkv, GROUP, scatter_dimension=0, tiled=True),
+        lax.psum_scatter(d_out_weight, GROUP, scatter_dimension=0, tiled=True),
+        lax.psum_scatter(d_qk_gains, GROUP, scatter_dimension=0, tiled=True),
+        lax.psum_scatter(d_norm_gains, GROUP, scatter_dimension=0, tiled=True),
+        lax.psum_scatter(d_router, GROUP, scatter_dimension=0, tiled=True),
     )
     gain_share = gain_rows.shape[0] // tensor_count
     grad_norm_gains = lax.dynamic_slice_in_dim(gain_rows, tensor_rank * gain_share, gain_share, 0)
@@ -355,35 +366,655 @@
     )
 
 
+def contract_last(left, right):
+    return lax.dot_general(
+        left, right, (((1,), (1,)), ((), ())), preferred_element_type=jnp.float32
+    )
+
+
+def share_order(z):
+    upper, odd = (z // 2, z % 2)
+    return (z, z + 1 - 2 * upper, 2 + upper - 2 * odd, 3 - 3 * upper)
+
+
+def experts_kernel(
+    experts,
+    x_ref,
+    grads_ref,
+    kept_ref,
+    router_ref,
+    in_ref,
+    out_w_ref,
+    x_out,
+    dx_out,
+    moe_out,
+    gated_out,
+    both_out,
+    x_all,
+    w_in,
+    w_out,
+    grads,
+    dx_buf,
+    moe_buf,
+    gated,
+    both,
+    own_sem,
+    weight_sem,
+    grads_sem,
+    store_sem,
+    send_z,
+    send_x,
+    send_y,
+    send_c,
+    recv,
+):
+    w, c, z = (lax.axis_index(a) for a in (WEIGHTS, CONTEXT, TENSOR))
+    wx, wy = (w + 1 - 2 * (w % 2), (w + 2) % 4)
+    wd = wx + wy - w
+    share, width = x_ref.shape
+    half = width // 2
+    lo, hi = (pl.ds(0, half), pl.ds(half, half))
+    dev_x, dev_y, dev_c = ((wx, c, z), (wy, c, z), (w, 1 - c, z))
+    order = share_order(z)
+    hidden = out_w_ref.shape[1]
+    group = w * 2 + c
+
+    def loads():
+        return [
+        pltpu.make_async_copy(
+            in_ref.at[n, g], w_in.at[:, pl.ds((2 * n + g) * hidden, hidden)], weight_sem.at[2 * n + g]
+        )
+        for n in range(2)
+        for g in range(2)
+    ] + [
+        pltpu.make_async_copy(
+            out_w_ref.at[n], w_out.at[pl.ds(n * hidden, hidden)], weight_sem.at[4 + n]
+        )
+        for n in range(2)
+    ]
+
+    for load in loads():
+        load.start()
+
+    def grads_load(zj, cc, slot):
+        return pltpu.make_async_copy(grads_ref.at[:, cc, zj], grads.at[slot], grads_sem.at[slot])
+
+    grads_load(z, c, 0).start()
+    keep = lambda: pltpu.make_async_copy(x_ref, x_all.at[z, c, w], own_sem)
+    keep().start()
+
+    barrier = pltpu.get_barrier_semaphore()
+    around = [(w, c, (z + 1) % 4), (w, c, (z + 3) % 4)]
+    for device in [dev_x, dev_y, dev_c] + around:
+        pl.semaphore_signal(barrier, inc=1, device_id=device, device_id_type=MESH)
+    pl.semaphore_wait(barrier, 5)
+
+    def view(chunk, cols):
+        return x_all.at[chunk] if cols is None else x_all.at[chunk[0], chunk[1], chunk[2], :, cols]
+
+    def copy(src, chunk, cols, slot, sem, device):
+        return pltpu.make_async_remote_copy(
+            src_ref=src,
+            dst_ref=view(chunk, cols),
+            send_sem=sem[0].at[sem[1:]],
+            recv_sem=recv.at[chunk[0], chunk[1], slot],
+            device_id=device,
+            device_id_type=MESH,
+        )
+
+    sent = []
+    devices_z = ((w, c, z + 1), (w, c, z - 1))
+
+    def start(chunk, cols, slot, sem, device, src=None):
+        copy(view(chunk, cols) if src is None else src, chunk, cols, slot, sem, device).start()
+        sent.append((chunk, cols, slot, sem, device))
+
+    def arrived(chunk, cols, slot):
+        copy(view(chunk, cols), chunk, cols, slot, (send_c, 0, 0), dev_c).wait_recv()
+
+    def spread(j):
+        chunk = (order[j], c, w)
+        src = x_ref if j == 0 else None
+        start(chunk, None, 1, (send_x, j, 0), dev_x, src)
+        start(chunk, None, 2, (send_y, j, 0), dev_y, src)
+        start(chunk, None, 0, (send_c, j, 0), dev_c, src)
+
+    def onward(j):
+        chunk = (order[j], c, w)
+
+        def moved(side):
+            src = x_ref if j == 0 else view(chunk, None)
+            return copy(src, chunk, None, 0, (send_z, j, side), devices_z[side])
+
+        return (
+            ((order[j] <= z) & (z < 3), functools.partial(moved, 0)),
+            ((order[j] >= z) & (z > 0), functools.partial(moved, 1)),
+        )
+
+    def along(j):
+        for there, moved in onward(j):
+            pl.when(there)(lambda: moved().start())
+
+    def share_in(j):
+        arrived((order[j], c, w), None, 0)
+        along(j)
+        spread(j)
+
+    def relay(j):
+        from_x, from_y = ((order[j], c, wx), (order[j], c, wy))
+        arrived(from_x, None, 1)
+        start(from_x, lo, 3, (send_y, j, 1), dev_y)
+        start(from_x, None, 1, (send_c, j, 1), dev_c)
+        arrived(from_y, None, 2)
+        start(from_y, hi, 4, (send_x, j, 1), dev_x)
+        start(from_y, None, 2, (send_c, j, 2), dev_c)
+
+    def across(j):
+        chunk = (order[j], c, wd)
+        for cols, slot in ((lo, 3), (hi, 4)):
+            arrived(chunk, cols, slot)
+            start(chunk, cols, slot, (send_c, j, slot), dev_c)
+
+    def sibling(j):
+        for ww, cols, slot in ((w, None, 0), (wx, None, 1), (wy, None, 2), (wd, lo, 3), (wd, hi, 4)):
+            arrived((order[j], 1 - c, ww), cols, slot)
+
+    def before(step):
+        j = step // 2
+        if step == 0:
+            along(0)
+            spread(0)
+            share_in(1)
+            relay(0)
+            across(0)
+            keep().wait()
+            for load in loads():
+                load.wait()
+        elif step % 2 == 0:
+            across(j)
+        else:
+            if j + 2 < 4:
+                share_in(j + 2)
+            if j + 1 < 4:
+                relay(j + 1)
+            sibling(j)
+
+    code = order[0] + 4 * order[1] + 16 * order[2] + 64 * order[3]
+
+    def tile_of(step):
+        j = step // 2
+        power = 1 + 3 * j + (9 * j * (j - 1)) // 2 + (27 * j * (j - 1) * (j - 2)) // 6
+        return ((code // power) % 4, (c + step) % 2)
+
+    lanes = lax.broadcasted_iota(jnp.int32, (4 * share, 128), 1)
+
+    def stores(step):
+        zj, cc = tile_of(step)
+        return [
+            pltpu.make_async_copy(src, dst.at[:, cc, zj], store_sem.at[i])
+            for i, (src, dst) in enumerate(
+                (
+                    (x_all.at[zj, cc], x_out),
+                    (dx_buf, dx_out),
+                    (moe_buf, moe_out),
+                    (gated, gated_out),
+                    (both, both_out),
+                )
+            )
+        ]
+
+    def one_tile(step, carry):
+        for k in range(8):
+            pl.when(step == k)(functools.partial(before, k))
+        zj, cc = tile_of(step)
+        slot = step % 2
+        grads_load(zj, cc, slot).wait()
+
+        @pl.when(step < 7)
+        def _():
+            zn, cn = tile_of(step + 1)
+            grads_load(zn, cn, 1 - slot).start()
+
+        rows = x_all[zj, cc].reshape(4 * share, width)
+        upstream = grads[slot].reshape(4 * share, width)
+        logits = jnp.dot(rows, router_ref[...], preferred_element_type=jnp.float32)
+        logits = jnp.where(lanes < experts, logits, -1e30)
+        raised = jnp.exp(logits - jnp.max(logits, axis=1, keepdims=True))
+        gates = raised / jnp.sum(raised, axis=1, keepdims=True)
+        gates = gates * kept_ref[:, cc, zj].reshape(4 * share, 128).astype(jnp.float32)
+
+        @pl.when(step > 0)
+        def _():
+            for store in stores(step - 1):
+                store.wait()
+
+        d_gate = jnp.zeros((4 * share, 128), jnp.float32)
+        for n in range(2):
+            here = lanes == group * 2 + n
+            gate = jnp.sum(jnp.where(here, gates, 0.0), axis=1, keepdims=True)
+            at = 2 * n * hidden
+            gate_pre = jnp.dot(
+                rows, w_in[:, at : at + hidden], preferred_element_type=jnp.float32
+            )
+            up_pre = jnp.dot(
+                rows, w_in[:, at + hidden : at + 2 * hidden], preferred_element_type=jnp.float32
+            )
+            back = contract_last(upstream, w_out[n * hidden : (n + 1) * hidden, :])
+            sigmoid = 1.0 / (1.0 + jnp.exp(-gate_pre))
+            silu = gate_pre * sigmoid
+            activated = silu * up_pre
+            d_gate = jnp.where(here, jnp.sum(activated * back, axis=1, keepdims=True), d_gate)
+            back = gate * back
+            d_pre = back * up_pre * sigmoid * (1.0 + gate_pre * (1.0 - sigmoid))
+            shape = (4, share, hidden)
+            gated[:, :, n * hidden : (n + 1) * hidden] = (
+                (gate * activated).astype(jnp.bfloat16).reshape(shape)
+            )
+            both[:, :, at : at + hidden] = d_pre.astype(jnp.bfloat16).reshape(shape)
+            both[:, :, at + hidden : at + 2 * hidden] = (
+                (back * silu).astype(jnp.bfloat16).reshape(shape)
+            )
+        dx_buf[:, :, width:] = d_gate.astype(jnp.bfloat16).reshape(4, share, 128)
+        d_rows = both[...].reshape(4 * share, 4 * hidden)
+        g_rows = gated[...].reshape(4 * share, 2 * hidden)
+
+        def columns(m, carried):
+            cols = pl.ds(pl.multiple_of(m * 256, 256), 256)
+            dx_buf[:, :, cols] = (
+                contract_last(d_rows, w_in[cols, :]).astype(jnp.bfloat16).reshape(4, share, 256)
+            )
+            moe_buf[:, :, cols] = (
+                jnp.dot(g_rows, w_out[:, cols], preferred_element_type=jnp.float32)
+                .astype(jnp.bfloat16)
+                .reshape(4, share, 256)
+            )
+            return carried
+
+        lax.fori_loop(0, width // 256, columns, None)
+        for store in stores(step):
+            store.start()
+        return carry
+
+    lax.fori_loop(0, 8, one_tile, None)
+    for store in stores(7):
+        store.wait()
+    for chunk, cols, slot, sem, device in sent:
+        copy(view(chunk, cols), chunk, cols, slot, sem, device).wait_send()
+    for j in range(4):
+        for there, moved in onward(j):
+            pl.when(there)(lambda: moved().wait_send())
+
+
+def experts_call(rows, grads, kept, router, expert_in, expert_out, experts):
+    share, width = rows.shape
+    hidden = expert_out.shape[1]
+    blocks = (4, 2, 4, share)
+    bf16 = jnp.bfloat16
+    dma = pltpu.SemaphoreType.DMA
+    anywhere, vmem = (pl.BlockSpec(memory_space=pl.ANY), pl.BlockSpec(memory_space=pltpu.VMEM))
+    outs = (width, width + 128, width, 2 * hidden, 4 * hidden)
+    return pl.pallas_call(
+        functools.partial(experts_kernel, experts),
+        out_shape=tuple(jax.ShapeDtypeStruct(blocks + (n,), bf16) for n in outs),
+        in_specs=[anywhere, anywhere, vmem, vmem, anywhere, anywhere],
+        out_specs=(anywhere,) * 5,
+        scratch_shapes=[
+            pltpu.VMEM((4, 2, 4, share, width), bf16),
+            pltpu.VMEM((width, 4 * hidden), bf16),
+            pltpu.VMEM((2 * hidden, width), bf16),
+            pltpu.VMEM((2, 4, share, width), bf16),
+            pltpu.VMEM((4, share, width + 128), bf16),
+            pltpu.VMEM((4, share, width), bf16),
+            pltpu.VMEM((4, share, 2 * hidden), bf16),
+            pltpu.VMEM((4, share, 4 * hidden), bf16),
+            dma,
+            dma((6,)),
+            dma((2,)),
+            dma((5,)),
+            dma((4, 2)),
+            dma((4, 2)),
+            dma((4, 2)),
+            dma((4, 5)),
+            dma((4, 2, 5)),
+        ],
+        compiler_params=pltpu.CompilerParams(
+            collective_id=0, has_side_effects=True, vmem_limit_bytes=62 << 20
+        ),
+    )(rows, grads, kept, router, expert_in, expert_out)
+
+
+def gathered(rows, axes):
+    return lax.all_gather(rows, axes, axis=0, tiled=True)
+
+
+def scattered(rows, axes):
+    return lax.psum_scatter(rows, axes, scatter_dimension=0, tiled=True)
+
+
+def fit_rows(values, rows):
+    flat = values.reshape(-1)
+    columns = -(-flat.shape[0] // rows)
+    return jnp.pad(flat, (0, rows * columns - flat.shape[0])).reshape(rows, columns)
+
+
+def per_device_dense(
+    layer_in,
+    norm_gains,
+    qkv_weight,
+    qk_gains,
+    out_weight,
+    router,
+    expert_in,
+    expert_out,
+    grad_out,
+    segments,
+    routes,
+    route_order,
+):
+    group = GROUP
+    everyone = EVERYONE
+    group_count = lax.axis_size(group)
+    tensor_count = lax.axis_size(TENSOR)
+    context_rank = lax.axis_index(CONTEXT)
+    tensor_rank = lax.axis_index(TENSOR)
+    seq_count, half_len, model_width = layer_in.shape
+    token_count = seq_count * half_len
+    top_count = routes.shape[2]
+    weight_rows, _, head_width = qkv_weight.shape
+    expert_total = router.shape[1]
+    local_experts = expert_in.shape[0]
+    hidden_width = expert_in.shape[3]
+    head_rows, _, local_heads = qk_gains.shape
+    head_size = head_rows * group_count
+    share = token_count // tensor_count
+    bf16, f32 = jnp.bfloat16, jnp.float32
+
+    capacity = token_count * top_count * 9 // (8 * expert_total)
+    routed, slot_of = pair_slots(
+        routes.reshape(token_count, top_count),
+        route_order.reshape(token_count, top_count),
+        expert_total,
+    )
+    kept = routed & (slot_of < capacity)
+
+    front_small = jnp.concatenate(
+        [norm_gains, fit_rows(qk_gains, weight_rows)], axis=1
+    )
+    front = gathered(
+        jnp.concatenate([qkv_weight.reshape(weight_rows, -1), front_small], axis=1), group
+    )
+    back_small = jnp.concatenate(
+        [router, fit_rows(kept.astype(bf16), weight_rows)], axis=1
+    )
+    back = gathered(jnp.concatenate([out_weight, back_small], axis=1), group)
+    qkv_full = front[:, : 3 * head_width]
+    gain_full = front[:, 3 * head_width : 3 * head_width + 2].astype(f32)
+    gain_attn, gain_ffn = (gain_full[:, 0], gain_full[:, 1])
+    qk_gain_full = (
+        front[:, 3 * head_width + 2 :]
+        .reshape(group_count, -1)[:, : head_rows * 2 * local_heads]
+        .reshape(head_size, 2, local_heads)
+        .astype(f32)
+    )
+    query_gain = qk_gain_full[:, 0, :].T.reshape(-1)
+    key_gain = qk_gain_full[:, 1, :].T.reshape(-1)
+    out_full = back[:, :head_width]
+    router_full = back[:, head_width : head_width + expert_total]
+    kept_all = (
+        back[:, head_width + expert_total :]
+        .reshape(group_count, -1)[:, : expert_total * token_count]
+        .reshape(group_count, expert_total, token_count)
+    )
+    grads_all = gathered(grad_out.reshape(token_count, model_width), group)
+
+    inv_root = 1.0 / math.sqrt(head_size)
+    residual = layer_in.reshape(token_count, model_width).astype(f32)
+    scale_one = lax.rsqrt(jnp.mean(residual * residual, axis=1, keepdims=True) + epsilon)
+    normed_one = (residual * scale_one * gain_attn).astype(bf16)
+    projected = jnp.dot(normed_one, qkv_full, preferred_element_type=f32)
+    query_raw = projected[:, :head_width]
+    key_raw = projected[:, head_width : 2 * head_width]
+    value_raw = projected[:, 2 * head_width :]
+    square_sums = row_sums(
+        jnp.stack(
+            [jnp.sum(query_raw * query_raw, axis=1), jnp.sum(key_raw * key_raw, axis=1)], axis=1
+        )
+    )
+    query_scale = lax.rsqrt(square_sums[:, 0:1] / model_width + epsilon)
+    key_scale = lax.rsqrt(square_sums[:, 1:2] / model_width + epsilon)
+    heads_shape = (seq_count, half_len, local_heads, head_size)
+    query_hat = (query_raw * query_scale * query_gain).reshape(heads_shape)
+    key_hat = (key_raw * key_scale * key_gain).reshape(heads_shape)
+    query_pos = context_rank * half_len + jnp.arange(half_len, dtype=jnp.int32)
+    cosine_table, sine_table = rotary_tables(query_pos, head_size)
+    cosine_table = cosine_table[None, :, None, :]
+    sine_table = sine_table[None, :, None, :]
+    query_rot = (query_hat * cosine_table + rotate_half(query_hat) * sine_table).astype(bf16)
+    key_rot = (key_hat * cosine_table + rotate_half(key_hat) * sine_table).astype(bf16)
+    value_low = value_raw.astype(bf16).reshape(heads_shape)
+    key_prev, value_prev = passed_along((key_rot, value_low), CONTEXT, 1)
+    all_keys = jnp.concatenate([key_prev, key_rot], axis=1)
+    all_values = jnp.concatenate([value_prev, value_low], axis=1)
+    key_pos = jnp.concatenate([query_pos - half_len, query_pos])
+    seg_query = lax.dynamic_slice_in_dim(segments, context_rank * half_len, half_len, 1)
+    seg_prev = lax.dynamic_slice_in_dim(
+        segments, jnp.maximum(context_rank - 1, 0) * half_len, half_len, 1
+    )
+    seg_keys = jnp.concatenate([seg_prev, seg_query], axis=1)
+    causal = (key_pos[None, :] >= 0) & (key_pos[None, :] <= query_pos[:, None])
+    allowed = causal[None] & (seg_query[:, :, None] == seg_keys[:, None, :])
+
+    def score_block(queries, key_rows):
+        raw_scores = (
+            jnp.einsum(BY_SCORE, queries, key_rows, preferred_element_type=f32) * inv_root
+        )
+        return jnp.where(allowed[:, None], raw_scores, -1e30)
+
+    scores = score_block(query_rot, all_keys)
+    row_max = jnp.max(scores, axis=-1, keepdims=True)
+    exponent = jnp.exp(scores - row_max)
+    row_total = jnp.sum(exponent, axis=-1, keepdims=True)
+    log_total = row_max + jnp.log(row_total)
+    attn_probs = (exponent / row_total).astype(bf16)
+    attended = jnp.einsum(BY_QUERY, attn_probs, all_values, preferred_element_type=f32)
+    attended_low = attended.reshape(token_count, -1).astype(bf16)
+    attn_partial = jnp.einsum("tf,df->td", attended_low, out_full, preferred_element_type=f32)
+
+    own_rows = lambda rows: lax.dynamic_slice_in_dim(rows, tensor_rank * share, share, 0)
+    residual_own = own_rows(residual)
+    hidden = residual_own + scattered(attn_partial.astype(bf16), TENSOR).astype(f32)
+    scale_two = lax.rsqrt(jnp.mean(hidden * hidden, axis=1, keepdims=True) + epsilon)
+    unit_two = hidden * scale_two
+    normed_two = (unit_two * gain_ffn).astype(bf16)
+    upstream = own_rows(grad_out.reshape(token_count, model_width)).astype(f32)
+
+    blocks = (4, 2, 4, share)
+    pad_experts = lambda rows: jnp.pad(rows, ((0, 0), (0, 128 - expert_total)))
+    kept_rows = kept_all.transpose(0, 2, 1).reshape(-1, expert_total)
+    normed_all, d_sums, moe_partial, gated, d_both = (
+        rows.reshape(group_count * token_count, -1)
+        for rows in experts_call(
+            normed_two,
+            grads_all.reshape(blocks + (model_width,)),
+            pad_experts(kept_rows).reshape(blocks + (128,)),
+            pad_experts(router_full),
+            expert_in,
+            expert_out,
+            expert_total,
+        )
+    )
+    d_sums = scattered(scattered(d_sums, group), TENSOR).astype(f32)
+    moe_own = scattered(scattered(moe_partial, group), TENSOR).astype(f32)
+    layer_out = gathered((hidden + moe_own).astype(bf16), TENSOR).reshape(layer_in.shape)
+    grad_expert_in = jnp.einsum(
+        "td,tngf->ngdf",
+        normed_all,
+        d_both.reshape(-1, local_experts, 2, hidden_width),
+        preferred_element_type=f32,
+    )
+    grad_expert_out = jnp.dot(gated.T, grads_all, preferred_element_type=f32).reshape(
+        expert_out.shape
+    )
+
+    kept_own = own_rows(kept.T).astype(f32)
+    probs_own = jax.nn.softmax(
+        jnp.dot(normed_two, router_full, preferred_element_type=f32), axis=1
+    )
+    d_probs = d_sums[:, model_width : model_width + expert_total] * kept_own
+    d_logits = (
+        probs_own * (d_probs - jnp.sum(probs_own * d_probs, axis=1, keepdims=True))
+    ).astype(bf16)
+    d_normed_two = d_sums[:, :model_width] + jnp.dot(
+        d_logits, router_full.T, preferred_element_type=f32
+    )
+    d_router = jnp.dot(normed_two.T, d_logits, preferred_element_type=f32)
+    d_gain_ffn = jnp.sum(d_normed_two * unit_two, axis=0)
+    scaled_ffn = gain_ffn * d_normed_two
+    d_hidden = upstream + scale_two * (
+        scaled_ffn - unit_two * jnp.mean(scaled_ffn * unit_two, axis=1, keepdims=True)
+    )
+    d_hidden_low = gathered(d_hidden.astype(bf16), TENSOR)
+
+    d_attended = (
+        jnp.dot(d_hidden_low, out_full, preferred_element_type=f32)
+        .astype(bf16)
+        .reshape(heads_shape)
+    )
+    d_out_weight = jnp.einsum("td,tf->df", d_hidden_low, attended_low, preferred_element_type=f32)
+    probs_again = jnp.exp(score_block(query_rot, all_keys) - log_total)
+    probs_again_low = probs_again.astype(bf16)
+    d_probs_att = jnp.einsum(
+        BY_SCORE, d_attended, all_values, preferred_element_type=f32
+    )
+    d_values_all = jnp.einsum(
+        BY_KEY, probs_again_low, d_attended, preferred_element_type=f32
+    )
+    row_dot = jnp.sum(probs_again * d_probs_att, axis=-1, keepdims=True)
+    d_scores = (probs_again * (d_probs_att - row_dot)).astype(bf16)
+    d_query_rot = (
+        jnp.einsum(BY_QUERY, d_scores, all_keys, preferred_element_type=f32) * inv_root
+    )
+    d_keys_all = (
+        jnp.einsum(BY_KEY, d_scores, query_rot, preferred_element_type=f32) * inv_root
+    )
+    back_key, back_value = (
+        passed_along(d_keys_all[:, :half_len].astype(bf16), CONTEXT, -1).astype(f32),
+        passed_along(d_values_all[:, :half_len].astype(bf16), CONTEXT, -1).astype(f32),
+    )
+    d_key_rot = d_keys_all[:, half_len:] + back_key
+    d_value = (d_values_all[:, half_len:] + back_value).reshape(token_count, -1)
+    d_query_hat = (d_query_rot * cosine_table + rotate_back(d_query_rot * sine_table)).reshape(
+        token_count, -1
+    )
+    d_key_hat = (d_key_rot * cosine_table + rotate_back(d_key_rot * sine_table)).reshape(
+        token_count, -1
+    )
+    centre = row_sums(
+        jnp.stack(
+            [
+                jnp.sum(query_gain * d_query_hat * query_raw, axis=1),
+                jnp.sum(key_gain * d_key_hat * key_raw, axis=1),
+            ],
+            axis=1,
+        )
+    )
+    d_query_raw = (
+        query_scale * query_gain * d_query_hat
+        - query_raw * (query_scale**3 / model_width) * centre[:, 0:1]
+    )
+    d_key_raw = (
+        key_scale * key_gain * d_key_hat - key_raw * (key_scale**3 / model_width) * centre[:, 1:2]
+    )
+    d_query_gain = (
+        jnp.sum(d_query_hat * query_raw * query_scale, axis=0).reshape(local_heads, head_size).T
+    )
+    d_key_gain = jnp.sum(d_key_hat * key_raw * key_scale, axis=0).reshape(local_heads, head_size).T
+    d_qk_gains = jnp.stack([d_query_gain, d_key_gain], axis=1)
+    d_projected = jnp.concatenate([d_query_raw, d_key_raw, d_value], axis=1).astype(bf16)
+    d_normed_one = scattered(
+        jnp.einsum("tf,df->td", d_projected, qkv_full, preferred_element_type=f32).astype(bf16),
+        TENSOR,
+    ).astype(f32)
+    d_qkv = jnp.einsum("td,tf->df", normed_one, d_projected, preferred_element_type=f32)
+
+    scale_own = own_rows(scale_one)
+    unit_one = residual_own * scale_own
+    d_gain_attn = jnp.sum(d_normed_one * unit_one, axis=0)
+    scaled_attn = gain_attn * d_normed_one
+    grad_in = d_hidden + scale_own * (
+        scaled_attn - unit_one * jnp.mean(scaled_attn * unit_one, axis=1, keepdims=True)
+    )
+    grad_in = gathered(grad_in.astype(bf16), TENSOR).astype(f32).reshape(layer_in.shape)
+
+    grad_qkv = (
+        scattered(d_qkv.astype(bf16), group)
+        .astype(f32)
+        .reshape(weight_rows, 3, head_width)
+    )
+    grad_out_weight = scattered(d_out_weight.astype(bf16), group).astype(f32)
+    gain_share = weight_rows // tensor_count
+    router_share = expert_total // tensor_count
+    own_slot = (jnp.arange(tensor_count) == tensor_rank).astype(f32)[None, :, None]
+    small = jnp.concatenate(
+        [
+            jnp.stack([d_gain_attn, d_gain_ffn], axis=1).reshape(group_count, tensor_count, -1),
+            d_router.reshape(group_count, weight_rows, tensor_count, router_share)
+            .transpose(0, 2, 1, 3)
+            .reshape(group_count, tensor_count, -1),
+            d_qk_gains.reshape(group_count, 1, -1) * own_slot,
+        ],
+        axis=2,
+    ).reshape(group_count * tensor_count, -1)
+    small = scattered(small, everyone)[0]
+    ends = (gain_share * 2, gain_share * 2 + weight_rows * router_share)
+    return (
+        layer_out,
+        grad_in,
+        small[: ends[0]].reshape(gain_share, 2),
+        grad_qkv,
+        small[ends[1] :].reshape(head_rows, 2, local_heads),
+        grad_out_weight,
+        small[ends[0] : ends[1]].reshape(weight_rows, router_share),
+        grad_expert_in,
+        grad_expert_out,
+    )
+
+
 def solution(mesh):
     placed = (
-        P("weights", "context", None),
-        P(("weights", "context"), None),
-        P(("weights", "context"), None, "tensor"),
-        P(("weights", "context"), None, "tensor"),
-        P(("weights", "context"), "tensor"),
-        P(("weights", "context"), None),
-        P(("weights", "context"), None, None, "tensor"),
-        P(("weights", "context"), "tensor", None),
-        P("weights", "context", None),
-        P("weights", None),
-        P("weights", "context", None),
-        P("weights", "context", None),
-    )
+        P(WEIGHTS, CONTEXT, None),
+        P(GROUP, None),
+        P(GROUP, None, TENSOR),
+        P(GROUP, None, TENSOR),
+        P(GROUP, TENSOR),
+        P(GROUP, None),
+        P(GROUP, None, None, TENSOR),
+        P(GROUP, TENSOR, None),
+        P(WEIGHTS, CONTEXT, None),
+        P(WEIGHTS, None),
+        P(WEIGHTS, CONTEXT, None),
+        P(WEIGHTS, CONTEXT, None),
+    )
+    axes = tuple(mesh.shape[axis] for axis in EVERYONE)
+
+    def per_device(*blocks):
+        dense = axes == (4, 2, 4) and blocks[5].shape[1] <= 2 * blocks[10].shape[2]
+        return (per_device_dense if dense else per_device_slots)(*blocks)
+
     return jax.shard_map(
         per_device,
         mesh=mesh,
         in_specs=placed,
         out_specs=(
-            P("weights", "context", None),
-            P("weights", "context", None),
-            P(("weights", "context", "tensor"), None),
-            P(("weights", "context"), None, "tensor"),
-            P(("weights", "context"), None, "tensor"),
-            P(("weights", "context"), "tensor"),
-            P(("weights", "context"), "tensor"),
-            P(("weights", "context"), None, None, "tensor"),
-            P(("weights", "context"), "tensor", None),
+            P(WEIGHTS, CONTEXT, None),
+            P(WEIGHTS, CONTEXT, None),
+            P(EVERYONE, None),
+            P(GROUP, None, TENSOR),
+            P(GROUP, None, TENSOR),
+            P(GROUP, TENSOR),
+            P(GROUP, TENSOR),
+            P(GROUP, None, None, TENSOR),
+            P(GROUP, TENSOR, None),
         ),
         check_vma=False,
     )

time: 2400 us -> 1180 us (0.49)
  waiting for transfers between devices: 1610 us -> 748 us
  local copies, waits for them, and re-layouts: 429 us -> 88.6 us
  Pallas kernels: 0 us -> 147 us
  matrix products: 151 us -> 94.5 us
  blocking collectives: 71.5 us -> 21.7 us
  other arithmetic: 82.8 us -> 50.2 us
  starting transfers between devices: 34.2 us -> 7.93 us
    all_to_all x4 -> x0, waiting for transfers between devices: 1020 us -> none  [the longest x2 684 us: to_owners(): lax.all_to_all(slot_rows, ('weights', 'context'), split_axis=0, concat_ax...]
    psum x3 -> x0, waiting for transfers between devices: 368 us -> none  [the longest x1 286 us: per_device(): moe_total, dot_total = lax.psum((moe_partial, dot_partial), 'tensor')]
    reduce_scatter x3 -> x8, waiting for transfers between devices: 151 us -> 395 us  [scattered(): return lax.psum_scatter(rows, axes, scatter_dimension=0, tiled=True)]
    all_gather x2 -> x6, waiting for transfers between devices: 22.5 us -> 261 us  [gathered(): return lax.all_gather(rows, axes, axis=0, tiled=True)]
    gather x9 -> x0, local copies, waits for them, and re-layouts: 223 us -> none  [the longest x1 43.2 us: per_device(): jnp.concatenate([d_returned, zero_wide], axis=0)[dest_row]]
    pallas_call x0 -> x1, Pallas kernels: none -> 147 us  [experts_call(): pl.pallas_call(functools.partial(experts_kernel, experts), out_shape=tupl...]
    dot_general x21 -> x17, matrix products: 151 us -> 94.5 us  [the longest x1 24.3 us: per_device_dense(): jnp.einsum('td,tngf->ngdf', normed_all, d_both.reshape(-1, local_experts,...]
    concatenate x4 -> x3, local copies, waits for them, and re-layouts: 65.4 us -> 10.3 us  [the longest x2 6.9 us: per_device_dense(): jnp.concatenate([jnp.stack([d_gain_attn, d_gain_ffn], axis=1).reshape(gro...]
  transfers between devices with their start and end apart: 18 -> 19, of which waited for: 12 -> 13; matrix products, arithmetic and copies ran while one was open for 20% -> 17% of each run, Pallas kernels for 0% -> 0%
where the time goes in v1:
time: 1180 us; the launch traced here: 1170 us
  waiting for transfers between devices  748 us (63%)
  Pallas kernels  147 us (12%)
  matrix products  94.5 us (8%)
  local copies, waits for them, and re-layouts  88.6 us (8%)
  other arithmetic  50.2 us (4%)
  blocking collectives  21.7 us (2%)
  between operations  15.2 us (1%)
    reduce_scatter x8, waiting for transfers between devices, scattered(): return lax.psum_scatter(rows, axes, scatter_dimension=0, tiled=True)  395 us
    all_gather x6, waiting for transfers between devices, gathered(): return lax.all_gather(rows, axes, axis=0, tiled=True)  261 us
    pallas_call x1, Pallas kernels, experts_call(): pl.pallas_call(functools.partial(experts_kernel, experts), out_shape=tupl...  147 us
    unnamed x16, waiting for transfers between devices  91.7 us
    unnamed x125, local copies, waits for them, and re-layouts  28.1 us
    dot_general x1, matrix products, per_device_dense(): jnp.einsum('td,tngf->ngdf', normed_all, d_both.reshape(-1, local_experts,...  24.3 us
  transfers between devices with their start and end apart: 19, of which 13 were waited for; matrix products, arithmetic and copies ran while one was open for 17% of the time, Pallas kernels for 0%

profile of v1, /device:TPU:0, one launch (start us, length us, event | category | flops | bytes accessed | tf_op | source)
XLA Modules:
  0.0 1173.3 jit_solution(10330738366801502237)
XLA Ops:
  9.7 3.4 concatenate.72
  25.5 37.3 %all-gather.8.cloned.1.call-done = bf16[2048,1539]{0,1:T(8,128)(2,1)} async-done(((bf16[256,1539]{0,1:T(8,128)(2,1)}), bf16[2048,1539]{0,1:T(8,128)(2,1)}) %all-gather.8.cloned.1.call-update) | async-done | bytes 6303760 | tf_op jit(solution)/shard_map/all_gather | solution.py:687
  64.8 6.3 fusion.8
  74.4 11.7 psum.14
  100.5 3.7 fusion.86
  112.2 4.2 convolution_convert_fusion.2
  124.9 32.8 %reduce-scatter.9.cloned.1.call-done = bf16[128,2048]{1,0:T(8,128)(2,1)} async-done(((bf16[512,2048]{1,0:T(8,128)(2,1)}), bf16[128,2048]{1,0:T(8,128)(2,1)}) %reduce-scatter.9.cloned.1.call-update) | async-done | bytes 524304 | tf_op jit(solution)/shard_map/reduce_scatter | solution.py:691
  160.5 88.3 %all-gather.18.cloned.1.call-done = bf16[1,4096,2048]{2,1,0:T(8,128)(2,1)} async-done(((bf16[1,512,2048]{2,1,0:T(8,128)(2,1)}), bf16[1,4096,2048]{2,1,0:T(8,128)(2,1)}) %all-gather.18.cloned.1.call-update) | async-done | bytes 16777232 | tf_op jit(solution)/shard_map/all_gather | solution.py:687
  248.9 147.5 %shard_map.187 = (bf16[4,2,4,128,2048]{4,3,2,1,0:T(8,128)(2,1)}, bf16[4,2,4,128,2176]{4,3,2,1,0:T(8,128)(2,1)}, bf16[4,2,4,128,2048]{4,3,2,1,0:T(8,128)(2,1)}, b...) custom-call(bf16[128,2048]{1,0:T(8,128)(2,1)} %multiply_convert_fusion.1.x_ref, ...), custom_call_target="tpu_custom_call" | custom-call | tf_op jit(solution)/shard_map/pallas_call | solution.py:656
  396.4 119.1 %reduce-scatter.15.cloned.1.call-done = bf16[512,2176]{1,0:T(8,128)(2,1)} async-done(((bf16[4096,2176]{1,0:T(8,128)(2,1)}), bf16[512,2176]{1,0:T(8,128)(2,1)}) %reduce-scatter.15.cloned.1.call-update) | async-done | bytes 2228240 | tf_op jit(solution)/shard_map/reduce_scatter | solution.py:691
  518.0 45.8 %reduce-scatter.17.cloned.1.call-done = bf16[128,2176]{1,0:T(8,128)(2,1)} async-done(((bf16[512,2176]{1,0:T(8,128)(2,1)}), bf16[128,2176]{1,0:T(8,128)(2,1)}) %reduce-scatter.17.cloned.1.call-update) | async-done | bytes 557072 | tf_op jit(solution)/shard_map/reduce_scatter | solution.py:691
  574.0 42.8 %all-gather.14.cloned.1.call-done = bf16[512,2048]{1,0:T(8,128)(2,1)} async-done(((bf16[128,2048]{1,0:T(8,128)(2,1)}), bf16[512,2048]{1,0:T(8,128)(2,1)}) %all-gather.14.cloned.1.call-update) | async-done | bytes 2097168 | tf_op jit(solution)/shard_map/all_gather | solution.py:687
  619.9 5.1 fusion.26
  628.3 3.4 multiply_reduce_fusion
  651.6 10.0 psum.15
  664.8 7.6 fusion.20
  672.4 63.6 %reduce-scatter.11.cloned.1.call-done = bf16[512,2048]{1,0:T(8,128)(2,1)} async-done(((bf16[4096,2048]{1,0:T(8,128)(2,1)}), bf16[512,2048]{1,0:T(8,128)(2,1)}) %reduce-scatter.11.cloned.1.call-update) | async-done | bytes 2097168 | tf_op jit(solution)/shard_map/reduce_scatter | solution.py:691
  743.2 5.1 concatenate.88
  748.7 34.2 %reduce-scatter.19.cloned.1.call-done = bf16[128,2048]{1,0:T(8,128)(2,1)} async-done(((bf16[512,2048]{1,0:T(8,128)(2,1)}), bf16[128,2048]{1,0:T(8,128)(2,1)}) %reduce-scatter.19.cloned.1.call-update) | async-done | bytes 524304 | tf_op jit(solution)/shard_map/reduce_scatter | solution.py:691
  788.7 39.6 %reduce-scatter.13.cloned.1.call-done = bf16[128,2048]{1,0:T(8,128)(2,1)} async-done(((bf16[512,2048]{1,0:T(8,128)(2,1)}), bf16[128,2048]{1,0:T(8,128)(2,1)}) %reduce-scatter.13.cloned.1.call-update) | async-done | bytes 524304 | tf_op jit(solution)/shard_map/reduce_scatter | solution.py:691
  828.3 3.4 fusion.38
  832.4 7.0 convolution_convert_fusion
  839.4 14.7 %reshape_reshape.7 = bf16[4096,2,2,256]{3,2,1,0:T(2,128)(2,1)} reshape(bf16[4,2,4,128,1024]{4,3,2,1,0:T(8,128)(2,1)} %get-tuple-element.16) | data formatting | bytes 16777216 | tf_op jit(solution)/shard_map/reshape;reshape | solution.py:852
  854.1 24.3 %fusion.10 = f32[2,2,2048,256]{2,3,1,0:T(8,128)} fusion(bf16[4096,2048,1,1]{1,0,3,2:T(8,128)(2,1)} %bitcast.248, bf16[4096,2,2,256]{3,2,1,0:T(2,128)(2,1)} %reshape_reshape.7), kind=kOutput, calls=%fused_computation.18 | convolution fusion | flops 17179869184 | bytes 33554432 | tf_op jit(solution)/shard_map/td,tngf->ngdf/dot_general | solution.py:849
  878.3 8.7 copy.227
  887.0 6.3 copy.222
  893.3 14.9 %fusion = f32[2,256,2048]{2,1,0:T(8,128)} fusion(bf16[2,256,4096]{2,1,0:T(8,128)(2,1)} %bitcast.199, bf16[1,4096,2048]{2,1,0:T(8,128)(2,1)} %all-gather.18.cloned.1.call-done), kind=kOutput, calls=%fused_computation | convolution fusion | flops 8589934592 | bytes 25165824 | tf_op jit(solution)/shard_map/dot_general | solution.py:855
  910.1 89.8 %all-reduce.6.cloned.1.call-done = f32[32,1280]{1,0:T(8,128)} async-done(((f32[32,1280]{1,0:T(8,128)}), f32[32,1280]{1,0:T(8,128)}) %all-reduce.6.cloned.1.call-update) | async-done | bytes 163856
  1003.9 46.1 %all-gather.12.cloned.1.call-done = bf16[512,2048]{1,0:T(8,128)(2,1)} async-done(((bf16[128,2048]{1,0:T(8,128)(2,1)}), bf16[512,2048]{1,0:T(8,128)(2,1)}) %all-gather.12.cloned.1.call-update) | async-done | bytes 2097168 | tf_op jit(solution)/shard_map/all_gather | solution.py:687
  1050.0 46.7 %all-gather.16.cloned.1.call-done = bf16[512,2048]{1,0:T(8,128)(2,1)} async-done(((bf16[128,2048]{1,0:T(8,128)(2,1)}), bf16[512,2048]{1,0:T(8,128)(2,1)}) %all-gather.16.cloned.1.call-update) | async-done | bytes 2097168 | tf_op jit(solution)/shard_map/all_gather | solution.py:687
  1096.7 4.1 bitcast_convert_fusion
  1100.8 59.6 %reduce-scatter.21.cloned.1.call-done = bf16[256,1536]{1,0:T(8,128)(2,1)} async-done(((bf16[2048,1536]{1,0:T(8,128)(2,1)}), bf16[256,1536]{1,0:T(8,128)(2,1)}) %reduce-scatter.21.cloned.1.call-update) | async-done | bytes 786448 | tf_op jit(solution)/shard_map/reduce_scatter | solution.py:691
  (280 shorter events, 121.0 us)
Async XLA Ops:
  7.2 55.6 %all-gather.8.cloned.1.call-start = ((), (), s32[]{:S(2)}) async-start(), calls=%async_computation.8 | async-start | bytes 7114752 | tf_op jit(solution)/shard_map/all_gather | solution.py:687
  13.2 98.3 %all-gather.10.cloned.1.call-start = ((), (), s32[]{:S(2)}) async-start(), calls=%async_computation.9 | async-start | bytes 2949120 | tf_op jit(solution)/shard_map/all_gather | solution.py:687
  19.2 138.5 %reduce-scatter.9.cloned.1.call-start = ((), (), s32[]{:S(2)}) async-start(), calls=%async_computation.10 | async-start | bytes 2621440 | tf_op jit(solution)/shard_map/reduce_scatter | solution.py:691
  22.4 42.3 %copy-start.16 = (f32[512,128]{1,0:T(8,128)}, f32[512,128]{1,0:T(8,128)S(1)}, u32[]{:S(2)}) copy-start(f32[512,128]{1,0:T(8,128)S(1)} %get-tuple-element.102) | copy-start | bytes 786436
  94.1 6.4 collective-permute-start.1
  97.3 8.8 collective-permute-start
  116.5 132.4 %all-gather.18.cloned.1.call-start = ((), (), s32[]{:S(2)}) async-start(), calls=%async_computation.21 | async-start | bytes 18874368 | tf_op jit(solution)/shard_map/all_gather | solution.py:687
  117.1 398.4 %reduce-scatter.15.cloned.1.call-start = ((), (), s32[]{:S(2)}) async-start(), calls=%async_computation.14 | async-start | bytes 20054016 | tf_op jit(solution)/shard_map/reduce_scatter | solution.py:691
  159.4 408.7 %copy-start.3 = (f32[128,2048]{1,0:T(8,128)}, f32[128,2048]{1,0:T(8,128)S(1)}, u32[]{:S(2)}) copy-start(f32[128,2048]{1,0:T(8,128)S(1)} %get-tuple-element.83) | copy-start | bytes 3145732
  159.4 408.7 %copy-start.41 = (f32[128]{0:T(128)}, f32[128]{0:T(128)S(1)}, u32[]{:S(2)}) copy-start(f32[128]{0:T(128)S(1)} %add_rsqrt_fusion.1) | copy-start | bytes 1540
  396.3 120.0 %copy-start.13 = (bf16[128,2048]{1,0:T(8,128)(2,1)S(1)}, bf16[128,2048]{1,0:T(8,128)(2,1)}, u32[]{:S(2)}) copy-start(bf16[128,2048]{1,0:T(8,128)(2,1)} %multiply_convert_fusion.1.x_ref) | copy-start | bytes 1572868
  396.4 167.4 %reduce-scatter.17.cloned.1.call-start = ((), (), s32[]{:S(2)}) async-start(), calls=%async_computation.15 | async-start | bytes 2785280 | tf_op jit(solution)/shard_map/reduce_scatter | solution.py:691
  515.5 101.3 %all-gather.14.cloned.1.call-start = ((), (), s32[]{:S(2)}) async-start(), calls=%async_computation.16 | async-start | bytes 2621440 | tf_op jit(solution)/shard_map/all_gather | solution.py:687
  517.7 53.7 %copy-start.39 = (f32[128]{0:T(128)}, f32[128]{0:T(128)S(1)}, u32[]{:S(2)}) copy-start(f32[128]{0:T(128)S(1)} %get-tuple-element.116) | copy-start | bytes 1540
  518.0 54.1 %copy-start.43 = (f32[128]{0:T(128)}, f32[128]{0:T(128)S(1)}, u32[]{:S(2)}) copy-start(f32[128]{0:T(128)S(1)} %fusion.59) | copy-start | bytes 1540
  571.3 164.7 %reduce-scatter.11.cloned.1.call-start = ((), (), s32[]{:S(2)}) async-start(), calls=%async_computation.11 | async-start | bytes 18874368 | tf_op jit(solution)/shard_map/reduce_scatter | solution.py:691
  571.4 45.4 %copy-start.20 = (bf16[2048,560]{1,0:T(8,128)(2,1)S(1)}, bf16[2048,560]{1,0:T(8,128)(2,1)}, u32[]{:S(2)}) copy-start(bf16[2048,560]{1,0:T(8,128)(2,1)} %all-gather.10.cloned.1.call-done) | copy-start | bytes 6881284
  572.1 210.8 %reduce-scatter.19.cloned.1.call-start = ((), (), s32[]{:S(2)}) async-start(), calls=%async_computation.17 | async-start | bytes 2621440 | tf_op jit(solution)/shard_map/reduce_scatter | solution.py:691
  626.5 15.7 %collective-permute-start.3 = (bf16[1,512,4,128]{1,3,2,0:T(8,128)(2,1)}, bf16[1,512,4,128]{1,3,2,0:T(8,128)(2,1)}, u32[]{:S(2)}, u32[]{:S(2)}) collective-permute-start(bf16[1,512,4,128]{1,3,2,0:T(8,128)(2,1)} %slice.241), channel_id=1, source_target_pairs={{4,0},{5,1},{6,2},{7,3},{12,8},{13,9},{14,10},{15,11},{20,16},{21,... | collective-permute-start | bytes 1572872 | tf_op jit(solution)/shard_map/ppermute | solution.py:25
  636.1 8.9 collective-permute-start.2
  672.4 63.8 %copy-start.51 = (bf16[512,2048]{1,0:T(8,128)(2,1)S(1)}, bf16[512,2048]{1,0:T(8,128)(2,1)}, u32[]{:S(2)}) copy-start(bf16[512,2048]{1,0:T(8,128)(2,1)} %all-gather.14.cloned.1.call-done) | copy-start | bytes 6291460
  672.4 63.8 %copy-start.53 = (bf16[4,128,512]{2,1,0:T(8,128)(2,1)S(1)}, bf16[4,128,512]{2,1,0:T(8,128)(2,1)}, u32[]{:S(2)}) copy-start(bf16[4,128,512]{2,1,0:T(8,128)(2,1)} %copy-done.52) | copy-start | bytes 1572868
  672.4 155.9 %reduce-scatter.13.cloned.1.call-start = ((), (), s32[]{:S(2)}) async-start(), calls=%async_computation.12 | async-start | bytes 2621440 | tf_op jit(solution)/shard_map/reduce_scatter | solution.py:691
  736.1 172.1 %reduce-scatter.23.cloned.1.call-start = ((), (), s32[]{:S(2)}) async-start(), calls=%async_computation.20 | async-start | bytes 2359296 | tf_op jit(solution)/shard_map/reduce_scatter | solution.py:691
  738.8 261.0 %all-reduce.6.cloned.1.call-start = ((), (), s32[]{:S(2)}) async-start(), calls=%async_computation.22 | async-start | bytes 327680
  743.2 85.1 %copy-start.4 = (f32[128,2048]{1,0:T(8,128)S(1)}, f32[128,2048]{1,0:T(8,128)}, u32[]{:S(2)}) copy-start(f32[128,2048]{1,0:T(8,128)} %copy-done.3) | copy-start | bytes 3145732
  743.2 85.1 %copy-start.42 = (f32[128]{0:T(128)S(1)}, f32[128]{0:T(128)}, u32[]{:S(2)}) copy-start(f32[128]{0:T(128)} %copy-done.41) | copy-start | bytes 1540
  743.2 85.1 %copy-start.47 = (f32[128]{0:T(128)S(1)}, f32[128]{0:T(128)}, u32[]{:S(2)}) copy-start(f32[128]{0:T(128)} %copy-done.46) | copy-start | bytes 1540
  786.1 46.3 %copy-start.12 = (bf16[1,512,2048]{2,1,0:T(8,128)(2,1)S(1)}, bf16[1,512,2048]{2,1,0:T(8,128)(2,1)}, u32[]{:S(2)}) copy-start(bf16[1,512,2048]{2,1,0:T(8,128)(2,1)} %param.12) | copy-start | bytes 6291460
  788.7 261.3 %all-gather.12.cloned.1.call-start = ((), (), s32[]{:S(2)}) async-start(), calls=%async_computation.13 | async-start | bytes 2621440 | tf_op jit(solution)/shard_map/all_gather | solution.py:687
  831.8 264.9 %all-gather.16.cloned.1.call-start = ((), (), s32[]{:S(2)}) async-start(), calls=%async_computation.18 | async-start | bytes 2621440 | tf_op jit(solution)/shard_map/all_gather | solution.py:687
  832.3 328.0 %reduce-scatter.21.cloned.1.call-start = ((), (), s32[]{:S(2)}) async-start(), calls=%async_computation.19 | async-start | bytes 7077888 | tf_op jit(solution)/shard_map/reduce_scatter | solution.py:691
  (44 other events, 242.6 us)
Sparse Core Ops, SparseCore 0:
  13.3 49.5 all-gather.7
  64.7 30.1 all-gather.9
  116.6 41.0 reduce-scatter.8
  159.7 89.1 all-gather.17
  396.5 118.9 reduce-scatter.14
  517.8 45.9 reduce-scatter.16
  571.4 45.3 all-gather.13
  620.8 115.1 reduce-scatter.10
  739.0 43.8 reduce-scatter.18
  785.1 43.1 reduce-scatter.12
  831.9 40.5 reduce-scatter.22
  877.9 121.8 all-reduce.5
  1002.0 47.9 all-gather.11
  1052.0 44.6 all-gather.15
  1099.9 60.4 reduce-scatter.20

commit v2 on v1

--- a/solution.py
+++ b/solution.py
@@ -377,40 +377,65 @@
     return (z, z + 1 - 2 * upper, 2 + upper - 2 * odd, 3 - 3 * upper)
 
 
+def neighbours(w):
+    wx, wy = (w + 1 - 2 * (w % 2), (w + 2) % 4)
+    return (wx, wy, wx + wy - w)
+
+
 def experts_kernel(
     experts,
     x_ref,
-    grads_ref,
+    grad_own,
+    grad_x,
+    grad_y,
+    grad_low,
+    grad_high,
     kept_ref,
     router_ref,
     in_ref,
     out_w_ref,
     x_out,
-    dx_out,
-    moe_out,
+    grads_out,
     gated_out,
     both_out,
-    x_all,
+    dx_own,
+    moe_own,
+    x_tile,
     w_in,
     w_out,
     grads,
-    dx_buf,
-    moe_buf,
     gated,
     both,
-    own_sem,
-    weight_sem,
-    grads_sem,
-    store_sem,
-    send_z,
-    send_x,
-    send_y,
-    send_c,
-    recv,
+    *scratch,
 ):
+    others, mine, sibs, from_x1, from_y1, from_y2, from_x2, from_z = (
+        (scratch[2 * k], scratch[2 * k + 1]) for k in range(8)
+    )
+    (
+        own_sem,
+        tile_sem,
+        weight_sem,
+        grads_sem,
+        store_sem,
+        send_z,
+        send_x,
+        send_y,
+        send_c,
+        recv,
+        over_send,
+        over_recv,
+        sib_send,
+        sib_recv,
+        credit,
+        one_send,
+        one_recv,
+        two_send,
+        two_recv,
+        end_send,
+        end_recv,
+    ) = scratch[16:]
     w, c, z = (lax.axis_index(a) for a in (WEIGHTS, CONTEXT, TENSOR))
-    wx, wy = (w + 1 - 2 * (w % 2), (w + 2) % 4)
-    wd = wx + wy - w
+    wx, wy, wd = neighbours(w)
     share, width = x_ref.shape
     half = width // 2
     lo, hi = (pl.ds(0, half), pl.ds(half, half))
@@ -418,39 +443,62 @@
     order = share_order(z)
     hidden = out_w_ref.shape[1]
     group = w * 2 + c
+    bf16, f32 = (jnp.bfloat16, jnp.float32)
+    wides = (width + 128, width)
 
     def loads():
         return [
-        pltpu.make_async_copy(
-            in_ref.at[n, g], w_in.at[:, pl.ds((2 * n + g) * hidden, hidden)], weight_sem.at[2 * n + g]
-        )
-        for n in range(2)
-        for g in range(2)
-    ] + [
-        pltpu.make_async_copy(
-            out_w_ref.at[n], w_out.at[pl.ds(n * hidden, hidden)], weight_sem.at[4 + n]
-        )
-        for n in range(2)
-    ]
+            pltpu.make_async_copy(
+                in_ref.at[n, g],
+                w_in.at[:, pl.ds((2 * n + g) * hidden, hidden)],
+                weight_sem.at[2 * n + g],
+            )
+            for n in range(2)
+            for g in range(2)
+        ] + [
+            pltpu.make_async_copy(
+                out_w_ref.at[n], w_out.at[pl.ds(n * hidden, hidden)], weight_sem.at[4 + n]
+            )
+            for n in range(2)
+        ]
 
     for load in loads():
         load.start()
-
-    def grads_load(zj, cc, slot):
-        return pltpu.make_async_copy(grads_ref.at[:, cc, zj], grads.at[slot], grads_sem.at[slot])
-
-    grads_load(z, c, 0).start()
-    keep = lambda: pltpu.make_async_copy(x_ref, x_all.at[z, c, w], own_sem)
+    keep = lambda: pltpu.make_async_copy(x_ref, x_out.at[w, c, z], own_sem)
     keep().start()
 
+    grad_parts = (
+        (grad_own, w, None),
+        (grad_x, wx, None),
+        (grad_y, wy, None),
+        (grad_low, wd, lo),
+        (grad_high, wd, hi),
+    )
+
+    def grad_place(cc, ww, cols):
+        return grads_out.at[ww, cc] if cols is None else grads_out.at[ww, cc, :, :, cols]
+
+    def over(i, cc):
+        src, ww, cols = grad_parts[i]
+        return pltpu.make_async_remote_copy(
+            src_ref=src,
+            dst_ref=grad_place(cc, ww, cols),
+            send_sem=over_send.at[i],
+            recv_sem=over_recv.at[i],
+            device_id=dev_c,
+            device_id_type=MESH,
+        )
+
     barrier = pltpu.get_barrier_semaphore()
-    around = [(w, c, (z + 1) % 4), (w, c, (z + 3) % 4)]
+    around = [(w, c, (z + k) % 4) for k in range(1, 4)]
     for device in [dev_x, dev_y, dev_c] + around:
         pl.semaphore_signal(barrier, inc=1, device_id=device, device_id_type=MESH)
-    pl.semaphore_wait(barrier, 5)
+    pl.semaphore_wait(barrier, 6)
+
 
     def view(chunk, cols):
-        return x_all.at[chunk] if cols is None else x_all.at[chunk[0], chunk[1], chunk[2], :, cols]
+        zz, cc, ww = chunk
+        return x_out.at[ww, cc, zz] if cols is None else x_out.at[ww, cc, zz, :, cols]
 
     def copy(src, chunk, cols, slot, sem, device):
         return pltpu.make_async_remote_copy(
@@ -519,85 +567,179 @@
         for ww, cols, slot in ((w, None, 0), (wx, None, 1), (wy, None, 2), (wd, lo, 3), (wd, hi, 4)):
             arrived((order[j], 1 - c, ww), cols, slot)
 
-    def before(step):
-        j = step // 2
-        if step == 0:
-            along(0)
-            spread(0)
-            share_in(1)
-            relay(0)
-            across(0)
-            keep().wait()
-            for load in loads():
-                load.wait()
-        elif step % 2 == 0:
-            across(j)
-        else:
-            if j + 2 < 4:
-                share_in(j + 2)
-            if j + 1 < 4:
-                relay(j + 1)
-            sibling(j)
+
+    def parts_of(a):
+        return (pl.ds(0, half), pl.ds(half, wides[a] - half))
+
+    def to_sibling(a):
+        return pltpu.make_async_remote_copy(
+            src_ref=others[a],
+            dst_ref=sibs[a],
+            send_sem=sib_send.at[a],
+            recv_sem=sib_recv.at[a],
+            device_id=dev_c,
+            device_id_type=MESH,
+        )
+
+    def first_hops(a, j):
+        low, high = parts_of(a)
+        moves = (
+            (wx, low, from_x1[a].at[j, 0], dev_x),
+            (wd, low, from_x1[a].at[j, 1], dev_x),
+            (wy, high, from_y1[a].at[j, 0], dev_y),
+            (wd, high, from_y1[a].at[j, 1], dev_y),
+        )
+        return [
+            pltpu.make_async_remote_copy(
+                src_ref=mine[a].at[j % 2, ww, :, cols],
+                dst_ref=dst,
+                send_sem=one_send.at[a, j, i],
+                recv_sem=one_recv.at[a, j, i],
+                device_id=device,
+                device_id_type=MESH,
+            )
+            for i, (ww, cols, dst, device) in enumerate(moves)
+        ]
+
+    def second_hops(a, j):
+        low, high = parts_of(a)
+        moves = ((wy, low, from_y2[a].at[j], dev_y), (wx, high, from_x2[a].at[j], dev_x))
+        return [
+            pltpu.make_async_remote_copy(
+                src_ref=mine[a].at[j % 2, ww, :, cols],
+                dst_ref=dst,
+                send_sem=two_send.at[a, j, i],
+                recv_sem=two_recv.at[a, j, i],
+                device_id=device,
+                device_id_type=MESH,
+            )
+            for i, (ww, cols, dst, device) in enumerate(moves)
+        ]
+
+    def last_hop(a, source, j):
+        return pltpu.make_async_remote_copy(
+            src_ref=mine[a].at[j % 2, w],
+            dst_ref=from_z[a].at[source],
+            send_sem=end_send.at[a, j],
+            recv_sem=end_recv.at[a, source],
+            device_id=(w, c, order[j]),
+            device_id_type=MESH,
+        )
+
+    def total(*terms):
+        added = terms[0].astype(f32)
+        for term in terms[1:]:
+            added = added + term.astype(f32)
+        return added
+
+    def after_first(j):
+        p = j % 2
+        for a in range(2):
+            low, high = parts_of(a)
+            for moved in first_hops(a, j):
+                moved.wait_recv()
+            mine[a][p, wy, :, low] = total(mine[a][p, wy, :, low], from_x1[a][j, 1]).astype(bf16)
+            mine[a][p, wx, :, high] = total(mine[a][p, wx, :, high], from_y1[a][j, 1]).astype(bf16)
+            for moved in second_hops(a, j):
+                moved.start()
+
+    def after_second(j):
+        p = j % 2
+        for a in range(2):
+            low, high = parts_of(a)
+            for moved in second_hops(a, j):
+                moved.wait_recv()
+            mine[a][p, w, :, low] = total(
+                mine[a][p, w, :, low], from_x1[a][j, 0], from_y2[a][j]
+            ).astype(bf16)
+            mine[a][p, w, :, high] = total(
+                mine[a][p, w, :, high], from_y1[a][j, 0], from_x2[a][j]
+            ).astype(bf16)
+            if j == 0:
+                from_z[a][z] = mine[a][p, w]
+            else:
+                last_hop(a, z, j).start()
+
+    def all_sent(j):
+        for a in range(2):
+            for moved in first_hops(a, j) + second_hops(a, j):
+                moved.wait_send()
+            if j > 0:
+                last_hop(a, z, j).wait_send()
+
 
     code = order[0] + 4 * order[1] + 16 * order[2] + 64 * order[3]
 
     def tile_of(step):
         j = step // 2
         power = 1 + 3 * j + (9 * j * (j - 1)) // 2 + (27 * j * (j - 1) * (j - 2)) // 6
-        return ((code // power) % 4, (c + step) % 2)
-
-    lanes = lax.broadcasted_iota(jnp.int32, (4 * share, 128), 1)
-
-    def stores(step):
+        return ((code // power) % 4, (c + 1 + step) % 2)
+
+    def other_grads(step):
+        zj, cc = tile_of(step)
+        return pltpu.make_async_copy(grads_out.at[:, cc, zj], grads.at[0], grads_sem.at[5])
+
+    def my_grads(step):
         zj, cc = tile_of(step)
         return [
+            pltpu.make_async_copy(
+                src.at[zj],
+                grads.at[1, ww] if cols is None else grads.at[1, ww, :, cols],
+                grads_sem.at[i],
+            )
+            for i, (src, ww, cols) in enumerate(grad_parts)
+        ]
+
+    def stores(step, own_tile):
+        zj, cc = tile_of(step)
+        pairs = [(gated, gated_out), (both, both_out)]
+        pairs += [(grads.at[1], grads_out)] if own_tile else []
+        return [
             pltpu.make_async_copy(src, dst.at[:, cc, zj], store_sem.at[i])
-            for i, (src, dst) in enumerate(
-                (
-                    (x_all.at[zj, cc], x_out),
-                    (dx_buf, dx_out),
-                    (moe_buf, moe_out),
-                    (gated, gated_out),
-                    (both, both_out),
-                )
-            )
+            for i, (src, dst) in enumerate(pairs)
         ]
 
-    def one_tile(step, carry):
-        for k in range(8):
-            pl.when(step == k)(functools.partial(before, k))
+    lanes = lax.broadcasted_iota(jnp.int32, (4 * share, 128), 1)
+
+    def tile(step, own_tile, parity):
         zj, cc = tile_of(step)
-        slot = step % 2
-        grads_load(zj, cc, slot).wait()
-
-        @pl.when(step < 7)
-        def _():
-            zn, cn = tile_of(step + 1)
-            grads_load(zn, cn, 1 - slot).start()
-
-        rows = x_all[zj, cc].reshape(4 * share, width)
-        upstream = grads[slot].reshape(4 * share, width)
-        logits = jnp.dot(rows, router_ref[...], preferred_element_type=jnp.float32)
+        load = pltpu.make_async_copy(x_out.at[:, cc, zj], x_tile, tile_sem)
+        load.start()
+        if own_tile:
+            for store in stores(step - 1, False):
+                store.wait()
+            for part in my_grads(step):
+                part.wait()
+
+            @pl.when(step < 7)
+            def _():
+                other_grads(step + 1).start()
+        else:
+
+            @pl.when(step > 0)
+            def _():
+                for store in stores(step - 1, True):
+                    store.wait()
+
+            for part in my_grads(step + 1):
+                part.start()
+            other_grads(step).wait()
+        load.wait()
+        rows = x_tile[...].reshape(4 * share, width)
+        upstream = grads[1 if own_tile else 0].reshape(4 * share, width)
+        logits = jnp.dot(rows, router_ref[...], preferred_element_type=f32)
         logits = jnp.where(lanes < experts, logits, -1e30)
         raised = jnp.exp(logits - jnp.max(logits, axis=1, keepdims=True))
         gates = raised / jnp.sum(raised, axis=1, keepdims=True)
-        gates = gates * kept_ref[:, cc, zj].reshape(4 * share, 128).astype(jnp.float32)
-
-        @pl.when(step > 0)
-        def _():
-            for store in stores(step - 1):
-                store.wait()
-
-        d_gate = jnp.zeros((4 * share, 128), jnp.float32)
+        gates = gates * kept_ref[:, cc, zj].reshape(4 * share, 128).astype(f32)
+        d_gate = jnp.zeros((4 * share, 128), f32)
         for n in range(2):
             here = lanes == group * 2 + n
             gate = jnp.sum(jnp.where(here, gates, 0.0), axis=1, keepdims=True)
             at = 2 * n * hidden
-            gate_pre = jnp.dot(
-                rows, w_in[:, at : at + hidden], preferred_element_type=jnp.float32
-            )
+            gate_pre = jnp.dot(rows, w_in[:, at : at + hidden], preferred_element_type=f32)
             up_pre = jnp.dot(
-                rows, w_in[:, at + hidden : at + 2 * hidden], preferred_element_type=jnp.float32
+                rows, w_in[:, at + hidden : at + 2 * hidden], preferred_element_type=f32
             )
             back = contract_last(upstream, w_out[n * hidden : (n + 1) * hidden, :])
             sigmoid = 1.0 / (1.0 + jnp.exp(-gate_pre))
@@ -608,36 +750,115 @@
             d_pre = back * up_pre * sigmoid * (1.0 + gate_pre * (1.0 - sigmoid))
             shape = (4, share, hidden)
             gated[:, :, n * hidden : (n + 1) * hidden] = (
-                (gate * activated).astype(jnp.bfloat16).reshape(shape)
+                (gate * activated).astype(bf16).reshape(shape)
             )
-            both[:, :, at : at + hidden] = d_pre.astype(jnp.bfloat16).reshape(shape)
-            both[:, :, at + hidden : at + 2 * hidden] = (
-                (back * silu).astype(jnp.bfloat16).reshape(shape)
-            )
-        dx_buf[:, :, width:] = d_gate.astype(jnp.bfloat16).reshape(4, share, 128)
+            both[:, :, at : at + hidden] = d_pre.astype(bf16).reshape(shape)
+            both[:, :, at + hidden : at + 2 * hidden] = (back * silu).astype(bf16).reshape(shape)
+        for store in stores(step, own_tile):
+            store.start()
+        if own_tile:
+            for a in range(2):
+                to_sibling(a).wait_recv()
+        else:
+
+            @pl.when(step > 0)
+            def _():
+                for a in range(2):
+                    to_sibling(a).wait_send()
+
+        def put(a, cols, count, value):
+            value = value.reshape(4, share, count)
+            if own_tile:
+                value = value + sibs[a][:, :, cols].astype(f32)
+                mine[a][parity, :, :, cols] = value.astype(bf16)
+            else:
+                others[a][:, :, cols] = value.astype(bf16)
+
+        put(0, pl.ds(width, 128), 128, d_gate)
         d_rows = both[...].reshape(4 * share, 4 * hidden)
         g_rows = gated[...].reshape(4 * share, 2 * hidden)
 
         def columns(m, carried):
             cols = pl.ds(pl.multiple_of(m * 256, 256), 256)
-            dx_buf[:, :, cols] = (
-                contract_last(d_rows, w_in[cols, :]).astype(jnp.bfloat16).reshape(4, share, 256)
-            )
-            moe_buf[:, :, cols] = (
-                jnp.dot(g_rows, w_out[:, cols], preferred_element_type=jnp.float32)
-                .astype(jnp.bfloat16)
-                .reshape(4, share, 256)
-            )
+            put(0, cols, 256, contract_last(d_rows, w_in[cols, :]))
+            put(1, cols, 256, jnp.dot(g_rows, w_out[:, cols], preferred_element_type=f32))
             return carried
 
         lax.fori_loop(0, width // 256, columns, None)
-        for store in stores(step):
-            store.start()
+
+    def before_other(j):
+        if j == 0:
+            for i in range(5):
+                over(i, c).start()
+            along(0)
+            spread(0)
+            share_in(1)
+            relay(0)
+            keep().wait()
+            for load in loads():
+                load.wait()
+            for i in range(5):
+                over(i, 1 - c).wait_recv()
+            other_grads(0).start()
+        if j >= 2:
+            after_second(j - 2)
+        across(j)
+        sibling(j)
+
+    def before_mine(j):
+        if j + 2 < 4:
+            share_in(j + 2)
+        if j + 1 < 4:
+            relay(j + 1)
+        if j >= 1:
+            after_first(j - 1)
+        if j >= 2:
+            all_sent(j - 2)
+
+    def round_of(j, carry):
+        for k in range(4):
+            pl.when(j == k)(functools.partial(before_other, k))
+        tile(2 * j, False, None)
+
+        @pl.when(j > 0)
+        def _():
+            pl.semaphore_wait(credit, 1)
+
+        for a in range(2):
+            to_sibling(a).start()
+        for k in range(4):
+            pl.when(j == k)(functools.partial(before_mine, k))
+        tile(2 * j + 1, True, j % 2)
+
+        @pl.when(j < 3)
+        def _():
+            pl.semaphore_signal(credit, inc=1, device_id=dev_c, device_id_type=MESH)
+
+        for k in range(4):
+
+            @pl.when(j == k)
+            def _():
+                for a in range(2):
+                    for moved in first_hops(a, k):
+                        moved.start()
+
         return carry
 
-    lax.fori_loop(0, 8, one_tile, None)
-    for store in stores(7):
+    lax.fori_loop(0, 4, round_of, None)
+    after_second(2)
+    after_first(3)
+    after_second(3)
+    for store in stores(7, True):
         store.wait()
+    for a, result in ((0, dx_own), (1, moe_own)):
+        to_sibling(a).wait_send()
+        for k in range(1, 4):
+            last_hop(a, (z + k) % 4, 1).wait_recv()
+        result[...] = total(*(from_z[a][k] for k in range(4)))
+    all_sent(2)
+    all_sent(3)
+    for i in range(5):
+        over(i, c).wait_send()
     for chunk, cols, slot, sem, device in sent:
         copy(view(chunk, cols), chunk, cols, slot, sem, device).wait_send()
     for j in range(4):
@@ -649,38 +870,73 @@
     share, width = rows.shape
     hidden = expert_out.shape[1]
     blocks = (4, 2, 4, share)
-    bf16 = jnp.bfloat16
+    bf16, f32 = (jnp.bfloat16, jnp.float32)
     dma = pltpu.SemaphoreType.DMA
     anywhere, vmem = (pl.BlockSpec(memory_space=pl.ANY), pl.BlockSpec(memory_space=pltpu.VMEM))
-    outs = (width, width + 128, width, 2 * hidden, 4 * hidden)
+    wides = (width + 128, width)
+    half = width // 2
+    both = lambda shape: [pltpu.VMEM(shape(wide), bf16) for wide in wides]
     return pl.pallas_call(
         functools.partial(experts_kernel, experts),
-        out_shape=tuple(jax.ShapeDtypeStruct(blocks + (n,), bf16) for n in outs),
-        in_specs=[anywhere, anywhere, vmem, vmem, anywhere, anywhere],
-        out_specs=(anywhere,) * 5,
+        out_shape=tuple(
+            jax.ShapeDtypeStruct(blocks + (n,), bf16)
+            for n in (width, width, 2 * hidden, 4 * hidden)
+        )
+        + tuple(jax.ShapeDtypeStruct((share, wide), f32) for wide in wides),
+        in_specs=[anywhere] * 6 + [vmem, vmem, anywhere, anywhere],
+        out_specs=(anywhere,) * 4 + (vmem, vmem),
         scratch_shapes=[
-            pltpu.VMEM((4, 2, 4, share, width), bf16),
+            pltpu.VMEM((4, share, width), bf16),
             pltpu.VMEM((width, 4 * hidden), bf16),
             pltpu.VMEM((2 * hidden, width), bf16),
             pltpu.VMEM((2, 4, share, width), bf16),
-            pltpu.VMEM((4, share, width + 128), bf16),
-            pltpu.VMEM((4, share, width), bf16),
             pltpu.VMEM((4, share, 2 * hidden), bf16),
             pltpu.VMEM((4, share, 4 * hidden), bf16),
+            *both(lambda wide: (4, share, wide)),
+            *both(lambda wide: (2, 4, share, wide)),
+            *both(lambda wide: (4, share, wide)),
+            *both(lambda wide: (4, 2, share, half)),
+            *both(lambda wide: (4, 2, share, wide - half)),
+            *both(lambda wide: (4, share, half)),
+            *both(lambda wide: (4, share, wide - half)),
+            *both(lambda wide: (4, share, wide)),
+            dma,
             dma,
             dma((6,)),
-            dma((2,)),
-            dma((5,)),
+            dma((6,)),
+            dma((3,)),
             dma((4, 2)),
             dma((4, 2)),
             dma((4, 2)),
             dma((4, 5)),
             dma((4, 2, 5)),
+            dma((5,)),
+            dma((5,)),
+            dma((2,)),
+            dma((2,)),
+            pltpu.SemaphoreType.REGULAR,
+            dma((2, 4, 4)),
+            dma((2, 4, 4)),
+            dma((2, 4, 2)),
+            dma((2, 4, 2)),
+            dma((2, 4)),
+            dma((2, 4)),
         ],
         compiler_params=pltpu.CompilerParams(
             collective_id=0, has_side_effects=True, vmem_limit_bytes=62 << 20
         ),
-    )(rows, grads, kept, router, expert_in, expert_out)
+    )(rows, *grads, kept, router, expert_in, expert_out)
+
+
+def swapped(rows, flip):
+    return lax.ppermute(rows, WEIGHTS, [(k, k ^ flip) for k in range(4)])
+
+
+def grads_around(rows, share):
+    half = rows.shape[1] // 2
+    from_x, from_y = (swapped(rows, 1), swapped(rows, 2))
+    parts = (rows, from_x, from_y, swapped(from_x[:, :half], 2), swapped(from_y[:, half:], 1))
+    return [part.reshape(-1, share, part.shape[1]) for part in parts]
 
 
 def gathered(rows, axes):
@@ -743,6 +999,9 @@
     front = gathered(
         jnp.concatenate([qkv_weight.reshape(weight_rows, -1), front_small], axis=1), group
     )
+    own_grads = grad_out.reshape(token_count, model_width)
+    front, own_grads = lax.optimization_barrier((front, own_grads))
+    around = grads_around(own_grads, share)
     back_small = jnp.concatenate(
         [router, fit_rows(kept.astype(bf16), weight_rows)], axis=1
     )
@@ -765,8 +1024,6 @@
         .reshape(group_count, -1)[:, : expert_total * token_count]
         .reshape(group_count, expert_total, token_count)
     )
-    grads_all = gathered(grad_out.reshape(token_count, model_width), group)
-
     inv_root = 1.0 / math.sqrt(head_size)
     residual = layer_in.reshape(token_count, model_width).astype(f32)
     scale_one = lax.rsqrt(jnp.mean(residual * residual, axis=1, keepdims=True) + epsilon)
@@ -828,29 +1085,26 @@
     normed_two = (unit_two * gain_ffn).astype(bf16)
     upstream = own_rows(grad_out.reshape(token_count, model_width)).astype(f32)
 
-    blocks = (4, 2, 4, share)
     pad_experts = lambda rows: jnp.pad(rows, ((0, 0), (0, 128 - expert_total)))
     kept_rows = kept_all.transpose(0, 2, 1).reshape(-1, expert_total)
-    normed_all, d_sums, moe_partial, gated, d_both = (
+    normed_all, grads_all, gated, d_both, d_sums, moe_own = experts_call(
+        normed_two,
+        around,
+        pad_experts(kept_rows).reshape(4, 2, 4, share, 128),
+        pad_experts(router_full),
+        expert_in,
+        expert_out,
+        expert_total,
+    )
+    normed_all, grads_all, gated, d_both = (
         rows.reshape(group_count * token_count, -1)
-        for rows in experts_call(
-            normed_two,
-            grads_all.reshape(blocks + (model_width,)),
-            pad_experts(kept_rows).reshape(blocks + (128,)),
-            pad_experts(router_full),
-            expert_in,
-            expert_out,
-            expert_total,
-        )
-    )
-    d_sums = scattered(scattered(d_sums, group), TENSOR).astype(f32)
-    moe_own = scattered(scattered(moe_partial, group), TENSOR).astype(f32)
+        for rows in (normed_all, grads_all, gated, d_both)
+    )
     layer_out = gathered((hidden + moe_own).astype(bf16), TENSOR).reshape(layer_in.shape)
-    grad_expert_in = jnp.einsum(
-        "td,tngf->ngdf",
-        normed_all,
-        d_both.reshape(-1, local_experts, 2, hidden_width),
-        preferred_element_type=f32,
+    grad_expert_in = (
+        jnp.dot(normed_all.T, d_both, preferred_element_type=f32)
+        .reshape(model_width, local_experts, 2, hidden_width)
+        .transpose(1, 2, 0, 3)
     )
     grad_expert_out = jnp.dot(gated.T, grads_all, preferred_element_type=f32).reshape(
         expert_out.shape

time: 1180 us -> 964 us (0.82)
  waiting for transfers between devices: 748 us -> 418 us
  Pallas kernels: 147 us -> 268 us
    reduce_scatter x8 -> x4, waiting for transfers between devices: 395 us -> 90.3 us  [scattered(): return lax.psum_scatter(rows, axes, scatter_dimension=0, tiled=True)]
    pallas_call x1, Pallas kernels: 147 us -> 268 us  [experts_call(): pl.pallas_call(functools.partial(experts_kernel, experts), out_shape=tupl...]
    all_gather x6 -> x5, waiting for transfers between devices: 261 us -> 175 us  [gathered(): return lax.all_gather(rows, axes, axis=0, tiled=True)]
    ppermute x0 -> x4, waiting for transfers between devices: none -> 51.7 us  [swapped(): return lax.ppermute(rows, WEIGHTS, [(k, k ^ flip) for k in range(4)])]
    another operation x3 -> x2, local copies, waits for them, and re-layouts: 15.4 us -> 0.8 us  [the longest x1 14.7 us: per_device_dense(): d_both.reshape(-1, local_experts, 2, hidden_width)]
    dot_general x0 -> x1, local copies, waits for them, and re-layouts: none -> 12 us  [per_device_dense(): jnp.dot(normed_all.T, d_both, preferred_element_type=f32)]
    unnamed x125 -> x128, local copies, waits for them, and re-layouts: 28.1 us -> 16.8 us
    unnamed x16 -> x11, waiting for transfers between devices: 91.7 us -> 100 us
  transfers between devices with their start and end apart: 19 -> 18, of which waited for: 13 -> 10; matrix products, arithmetic and copies ran while one was open for 17% -> 17% of each run, Pallas kernels for 0% -> 0%
where the time goes in v2:
time: 964 us; the launch traced here: 956 us
  waiting for transfers between devices  418 us (43%)
  Pallas kernels  268 us (28%)
  matrix products  95.3 us (10%)
  local copies, waits for them, and re-layouts  77.3 us (8%)
  other arithmetic  49.2 us (5%)
  blocking collectives  21.2 us (2%)
  between operations  15.7 us (2%)
  starting transfers between devices  11.4 us (1%)
    pallas_call x1, Pallas kernels, experts_call(): pl.pallas_call(functools.partial(experts_kernel, experts), out_shape=tupl...  268 us
    all_gather x5, waiting for transfers between devices, gathered(): return lax.all_gather(rows, axes, axis=0, tiled=True)  175 us
    unnamed x11, waiting for transfers between devices  100 us
    reduce_scatter x4, waiting for transfers between devices, scattered(): return lax.psum_scatter(rows, axes, scatter_dimension=0, tiled=True)  90.3 us
    ppermute x4, waiting for transfers between devices, swapped(): return lax.ppermute(rows, WEIGHTS, [(k, k ^ flip) for k in range(4)])  51.7 us
    dot_general x1, matrix products, per_device_dense(): jnp.dot(normed_all.T, d_both, preferred_element_type=f32)  22.2 us
    psum x2, blocking collectives, row_sums(): return lax.psum(partial_rows, TENSOR)  21.2 us
  transfers between devices with their start and end apart: 18, of which 10 were waited for; matrix products, arithmetic and copies ran while one was open for 17% of the time, Pallas kernels for 0%

profile of v2, /device:TPU:0, one launch (start us, length us, event | category | flops | bytes accessed | tf_op | source)
XLA Modules:
  0.0 956.0 jit_solution(7501687375724208846)
XLA Ops:
  9.7 3.4 concatenate.72
  25.5 37.3 %all-gather.6.cloned.1.call-done = bf16[2048,1539]{0,1:T(8,128)(2,1)} async-done(((bf16[256,1539]{0,1:T(8,128)(2,1)}), bf16[2048,1539]{0,1:T(8,128)(2,1)}) %all-gather.6.cloned.1.call-update) | async-done | bytes 6303760 | tf_op jit(solution)/shard_map/all_gather | solution.py:943
  64.8 6.3 fusion.4
  74.4 11.7 %psum.14 = f32[512,2]{0,1:T(2,128)S(1)} all-reduce(f32[512,2]{0,1:T(2,128)S(1)} %pad_maximum_fusion.7), channel_id=1, replica_groups=mesh['weights'=4,'context'=2,'tensor'=4] {'tensor'}, use_global_device_ids=true, to_apply=%region_3.4 | all-reduce | flops 1024 | bytes 8192 | tf_op jit(solution)/shard_map/psum | solution.py:69
  100.6 3.7 fusion.82
  110.9 4.4 convolution_convert_fusion.2
  125.2 35.4 %collective-permute-done.2 = bf16[512,2048]{1,0:T(8,128)(2,1)} collective-permute-done((bf16[512,2048]{1,0:T(8,128)(2,1)}, bf16[512,2048]{1,0:T(8,128)(2,1)}, u32[]{:S(2)}, u32[]{:S(2)}) %collective-permute-start.2) | collective-permute-done | bytes 2097184 | tf_op jit(solution)/shard_map/ppermute | solution.py:932
  170.1 14.2 %collective-permute-done.4 = bf16[512,1024]{1,0:T(8,128)(2,1)} collective-permute-done((bf16[512,1024]{1,0:T(8,128)(2,1)S(1)}, bf16[512,1024]{1,0:T(8,128)(2,1)}, u32[]{:S(2)}, u32[]{:S(2)}) %collective-permute-start.4) | collective-permute-done | bytes 1048608 | tf_op jit(solution)/shard_map/ppermute | solution.py:932
  186.3 268.2 %shard_map.187 = (bf16[4,2,4,128,2048]{4,3,2,1,0:T(8,128)(2,1)}, bf16[4,2,4,128,2048]{4,3,2,1,0:T(8,128)(2,1)}, bf16[4,2,4,128,512]{4,3,2,1,0:T(8,128)(2,1)}, bf...) custom-call(bf16[128,2048]{1,0:T(8,128)(2,1)} %copy-done.13, ...), custom_call_target="tpu_custom_call" | custom-call | tf_op jit(solution)/shard_map/pallas_call | solution.py:879
  463.2 44.9 %all-gather.12.cloned.1.call-done = bf16[512,2048]{1,0:T(8,128)(2,1)} async-done(((bf16[128,2048]{1,0:T(8,128)(2,1)}), bf16[512,2048]{1,0:T(8,128)(2,1)}) %all-gather.12.cloned.1.call-update) | async-done | bytes 2097168 | tf_op jit(solution)/shard_map/all_gather | solution.py:943
  508.1 3.5 fusion.22
  511.7 5.5 multiply_reduce_fusion
  523.6 2.7 broadcast_multiply_fusion
  528.1 5.2 fusion.19
  541.9 9.5 psum.15
  558.8 7.5 fusion.13
  566.5 2.7 convolution_convert_fusion.1
  570.7 2.7 copy.218
  573.3 5.1 concatenate.88
  578.8 30.3 %reduce-scatter.7.cloned.1.call-done = bf16[128,2048]{1,0:T(8,128)(2,1)} async-done(((bf16[512,2048]{1,0:T(8,128)(2,1)}), bf16[128,2048]{1,0:T(8,128)(2,1)}) %reduce-scatter.7.cloned.1.call-update) | async-done | bytes 524304 | tf_op jit(solution)/shard_map/reduce_scatter | solution.py:947
  612.7 3.6 fusion.31
  617.3 7.0 convolution_convert_fusion
  624.4 6.3 copy.223
  630.7 12.0 %copy.221 = bf16[1024,4096]{1,0:T(8,128)(2,1)} copy(bf16[1024,4096]{0,1:T(8,128)(2,1)} %bitcast.196) | data formatting | bytes 16777216 | tf_op jit(solution)/shard_map/dot_general | solution.py:1105
  642.7 15.2 %fusion.85 = f32[2,256,2048]{2,1,0:T(8,128)} fusion(bf16[2,256,4096]{2,1,0:T(8,128)(2,1)} %bitcast.205, bf16[4096,2048,1]{1,0,2:T(8,128)(2,1)} %bitcast.258), kind=kOutput, calls=%fused_computation.170 | convolution fusion | flops 8589934592 | bytes 25165824 | tf_op jit(solution)/shard_map/dot_general | solution.py:1109
  657.9 22.2 %convolution_bitcast_fusion = f32[2,2,2048,256]{3,2,1,0:T(8,128)} fusion(bf16[4096,2048,1,1]{1,0,3,2:T(8,128)(2,1)} %bitcast.257, bf16[2,2,256,4096]{3,2,1,0:T(8,128)(2,1)S(1)} %bitcast.197), kind=kOutput, calls=%fused_computation.14 | convolution fusion | flops 17179869184 | bytes 33554432 | tf_op jit(solution)/shard_map/dot_general | solution.py:1105
  681.9 99.4 %all-reduce.6.cloned.1.call-done = f32[32,1280]{1,0:T(8,128)} async-done(((f32[32,1280]{1,0:T(8,128)}), f32[32,1280]{1,0:T(8,128)}) %all-reduce.6.cloned.1.call-update) | async-done | bytes 163856
  785.3 46.2 %all-gather.10.cloned.1.call-done = bf16[512,2048]{1,0:T(8,128)(2,1)} async-done(((bf16[128,2048]{1,0:T(8,128)(2,1)}), bf16[512,2048]{1,0:T(8,128)(2,1)}) %all-gather.10.cloned.1.call-update) | async-done | bytes 2097168 | tf_op jit(solution)/shard_map/all_gather | solution.py:943
  831.5 46.9 %all-gather.14.cloned.1.call-done = bf16[512,2048]{1,0:T(8,128)(2,1)} async-done(((bf16[128,2048]{1,0:T(8,128)(2,1)}), bf16[512,2048]{1,0:T(8,128)(2,1)}) %all-gather.14.cloned.1.call-update) | async-done | bytes 2097168 | tf_op jit(solution)/shard_map/all_gather | solution.py:943
  878.4 4.1 bitcast_convert_fusion
  882.5 60.0 %reduce-scatter.9.cloned.1.call-done = bf16[256,1536]{1,0:T(8,128)(2,1)} async-done(((bf16[2048,1536]{1,0:T(8,128)(2,1)}), bf16[256,1536]{1,0:T(8,128)(2,1)}) %reduce-scatter.9.cloned.1.call-update) | async-done | bytes 786448 | tf_op jit(solution)/shard_map/reduce_scatter | solution.py:947
  945.5 3.2 copy.255
  (277 shorter events, 109.9 us)
Async XLA Ops:
  7.2 55.6 %all-gather.6.cloned.1.call-start = ((), (), s32[]{:S(2)}) async-start(), calls=%async_computation.4 | async-start | bytes 7114752 | tf_op jit(solution)/shard_map/all_gather | solution.py:943
  13.2 97.7 %all-gather.8.cloned.1.call-start = ((), (), s32[]{:S(2)}) async-start(), calls=%async_computation.5 | async-start | bytes 2949120 | tf_op jit(solution)/shard_map/all_gather | solution.py:943
  19.2 147.1 %reduce-scatter.5.cloned.1.call-start = ((), (), s32[]{:S(2)}) async-start(), calls=%async_computation.6 | async-start | bytes 2621440 | tf_op jit(solution)/shard_map/reduce_scatter | solution.py:947
  22.4 42.4 %copy-start.17 = (f32[512,128]{1,0:T(8,128)}, f32[512,128]{1,0:T(8,128)S(1)}, u32[]{:S(2)}) copy-start(f32[512,128]{1,0:T(8,128)S(1)} %get-tuple-element.108) | copy-start | bytes 786436
  71.1 19.9 %copy-start.1 = (f32[512,1536]{1,0:T(8,128)}, f32[512,1536]{1,0:T(8,128)S(1)}, u32[]{:S(2)}) copy-start(f32[512,1536]{1,0:T(8,128)S(1)} %fusion.4) | copy-start | bytes 9437188
  93.9 6.7 collective-permute-start.1
  97.6 8.6 collective-permute-start
  115.3 392.8 %all-gather.12.cloned.1.call-start = ((), (), s32[]{:S(2)}) async-start(), calls=%async_computation.8 | async-start | bytes 2621440 | tf_op jit(solution)/shard_map/all_gather | solution.py:943
  115.4 45.3 %collective-permute-start.2 = (bf16[512,2048]{1,0:T(8,128)(2,1)}, bf16[512,2048]{1,0:T(8,128)(2,1)}, u32[]{:S(2)}, u32[]{:S(2)}) collective-permute-start(bf16[512,2048]{1,0:T(8,128)(2,1)} %bitcast.199), channel_id=1, source_target_pairs={{0,8},{8,0},{16,24},{24,16},{1,9},{9,1},{17,25},{25,17},{2,10},{10... | collective-permute-start | bytes 6291464 | tf_op jit(solution)/shard_map/ppermute | solution.py:932
  116.9 45.6 %collective-permute-start.3 = (bf16[512,2048]{1,0:T(8,128)(2,1)}, bf16[512,2048]{1,0:T(8,128)(2,1)}, u32[]{:S(2)}, u32[]{:S(2)}) collective-permute-start(bf16[512,2048]{1,0:T(8,128)(2,1)} %bitcast.200), channel_id=1, source_target_pairs={{0,16},{8,24},{16,0},{24,8},{1,17},{9,25},{17,1},{25,9},{2,18},{10... | collective-permute-start | bytes 6291464 | tf_op jit(solution)/shard_map/ppermute | solution.py:932
  161.9 22.4 %collective-permute-start.4 = (bf16[512,1024]{1,0:T(8,128)(2,1)S(1)}, bf16[512,1024]{1,0:T(8,128)(2,1)}, u32[]{:S(2)}, u32[]{:S(2)}) collective-permute-start(bf16[512,1024]{1,0:T(8,128)(2,1)S(1)} %slice.169), channel_id=1, source_target_pairs={{0,16},{8,24},{16,0},{24,8},{1,17},{9,25},{17,1},{25,9},{2,18},{10... | collective-permute-start | bytes 3145736 | tf_op jit(solution)/shard_map/ppermute | solution.py:932
  164.8 21.5 %collective-permute-start.5 = (bf16[512,1024]{1,0:T(8,128)(2,1)}, bf16[512,1024]{1,0:T(8,128)(2,1)}, u32[]{:S(2)}, u32[]{:S(2)}) collective-permute-start(bf16[512,1024]{1,0:T(8,128)(2,1)} %slice.170), channel_id=1, source_target_pairs={{0,8},{8,0},{16,24},{24,16},{1,9},{9,1},{17,25},{25,17},{2,10},{10... | collective-permute-start | bytes 3145736 | tf_op jit(solution)/shard_map/ppermute | solution.py:932
  167.9 290.4 %copy-start.3 = (f32[128,2048]{1,0:T(8,128)}, f32[128,2048]{1,0:T(8,128)S(1)}, u32[]{:S(2)}) copy-start(f32[128,2048]{1,0:T(8,128)S(1)} %get-tuple-element.89) | copy-start | bytes 3145732
  167.9 290.3 %copy-start.43 = (f32[128]{0:T(128)}, f32[128]{0:T(128)S(1)}, u32[]{:S(2)}) copy-start(f32[128]{0:T(128)S(1)} %add_rsqrt_fusion.1) | copy-start | bytes 1540
  168.1 18.2 %copy-start.13 = (bf16[128,2048]{1,0:T(8,128)(2,1)}, bf16[128,2048]{1,0:T(8,128)(2,1)S(1)}, u32[]{:S(2)}) copy-start(bf16[128,2048]{1,0:T(8,128)(2,1)S(1)} %multiply_convert_fusion.1.x_ref) | copy-start | bytes 1572868
  169.8 285.8 %copy-start.41 = (f32[128]{0:T(128)}, f32[128]{0:T(128)S(1)}, u32[]{:S(2)}) copy-start(f32[128]{0:T(128)S(1)} %get-tuple-element.122) | copy-start | bytes 1540
  170.1 285.6 %copy-start.45 = (f32[128]{0:T(128)}, f32[128]{0:T(128)S(1)}, u32[]{:S(2)}) copy-start(f32[128]{0:T(128)S(1)} %fusion.52) | copy-start | bytes 1540
  458.2 53.4 %copy-start.48 = (f32[128]{0:T(128)}, f32[128]{0:T(128)S(1)}, u32[]{:S(2)}) copy-start(f32[128]{0:T(128)S(1)} %broadcast_multiply_fusion.6) | copy-start | bytes 1540
  461.4 147.7 %reduce-scatter.7.cloned.1.call-start = ((), (), s32[]{:S(2)}) async-start(), calls=%async_computation.9 | async-start | bytes 2621440 | tf_op jit(solution)/shard_map/reduce_scatter | solution.py:947
  463.2 48.5 %copy-start.26 = (bf16[512,512]{0,1:T(8,128)(2,1)S(1)}, bf16[512,512]{0,1:T(8,128)(2,1)}, u32[]{:S(2)}) copy-start(bf16[512,512]{0,1:T(8,128)(2,1)} %copy-done.25) | copy-start | bytes 1572868
  463.2 48.5 %copy-start.35 = (bf16[1,512,4,128]{1,3,2,0:T(8,128)(2,1)S(1)}, bf16[1,512,4,128]{1,3,2,0:T(8,128)(2,1)}, u32[]{:S(2)}) copy-start(bf16[1,512,4,128]{1,3,2,0:T(8,128)(2,1)} %copy-done.34) | copy-start | bytes 1572868
  522.2 13.6 %collective-permute-start.6 = (bf16[1,512,4,128]{3,1,2,0:T(8,128)(2,1)}, bf16[1,512,4,128]{3,1,2,0:T(8,128)(2,1)}, u32[]{:S(2)}, u32[]{:S(2)}) collective-permute-start(bf16[1,512,4,128]{3,1,2,0:T(8,128)(2,1)} %slice.249), channel_id=1, source_target_pairs={{4,0},{5,1},{6,2},{7,3},{12,8},{13,9},{14,10},{15,11},{20,16},{21,... | collective-permute-start | bytes 1572872 | tf_op jit(solution)/shard_map/ppermute | solution.py:25
  534.3 17.2 %collective-permute-start.7 = (bf16[1,512,4,128]{1,3,2,0:T(8,128)(2,1)}, bf16[1,512,4,128]{1,3,2,0:T(8,128)(2,1)}, u32[]{:S(2)}, u32[]{:S(2)}) collective-permute-start(bf16[1,512,4,128]{1,3,2,0:T(8,128)(2,1)} %slice.248), channel_id=1, source_target_pairs={{4,0},{5,1},{6,2},{7,3},{12,8},{13,9},{14,10},{15,11},{20,16},{21,... | collective-permute-start | bytes 1572872 | tf_op jit(solution)/shard_map/ppermute | solution.py:25
  566.4 113.7 %reduce-scatter.11.cloned.1.call-start = ((), (), s32[]{:S(2)}) async-start(), calls=%async_computation.12 | async-start | bytes 2359296 | tf_op jit(solution)/shard_map/reduce_scatter | solution.py:947
  569.2 212.1 %all-reduce.6.cloned.1.call-start = ((), (), s32[]{:S(2)}) async-start(), calls=%async_computation.13 | async-start | bytes 327680
  573.3 37.6 %copy-start.40 = (f32[2048]{0:T(1024)S(1)}, f32[2048]{0:T(1024)}, u32[]{:S(2)}) copy-start(f32[2048]{0:T(1024)} %get-tuple-element.80) | copy-start | bytes 24580
  573.3 39.3 %copy-start.4 = (f32[128,2048]{1,0:T(8,128)S(1)}, f32[128,2048]{1,0:T(8,128)}, u32[]{:S(2)}) copy-start(f32[128,2048]{1,0:T(8,128)} %copy-done.3) | copy-start | bytes 3145732
  573.3 39.3 %copy-start.44 = (f32[128]{0:T(128)S(1)}, f32[128]{0:T(128)}, u32[]{:S(2)}) copy-start(f32[128]{0:T(128)} %copy-done.43) | copy-start | bytes 1540
  573.3 39.3 %copy-start.49 = (f32[128]{0:T(128)S(1)}, f32[128]{0:T(128)}, u32[]{:S(2)}) copy-start(f32[128]{0:T(128)} %copy-done.48) | copy-start | bytes 1540
  612.6 218.9 %all-gather.10.cloned.1.call-start = ((), (), s32[]{:S(2)}) async-start(), calls=%async_computation.7 | async-start | bytes 2621440 | tf_op jit(solution)/shard_map/all_gather | solution.py:943
  616.3 262.1 %all-gather.14.cloned.1.call-start = ((), (), s32[]{:S(2)}) async-start(), calls=%async_computation.10 | async-start | bytes 2621440 | tf_op jit(solution)/shard_map/all_gather | solution.py:943
  617.0 325.5 %reduce-scatter.9.cloned.1.call-start = ((), (), s32[]{:S(2)}) async-start(), calls=%async_computation.11 | async-start | bytes 7077888 | tf_op jit(solution)/shard_map/reduce_scatter | solution.py:947
  (45 other events, 240.7 us)
Sparse Core Ops, SparseCore 0:
  13.3 49.5 all-gather.5
  64.7 30.1 all-gather.7
  115.4 41.0 reduce-scatter.4
  461.6 46.5 all-gather.11
  566.5 42.6 reduce-scatter.6
  612.3 40.5 reduce-scatter.10
  659.4 121.8 all-reduce.5
  783.5 47.9 all-gather.9
  833.7 44.6 all-gather.13
  882.0 60.4 reduce-scatter.8

commit v3 on v2

--- a/solution.py
+++ b/solution.py
@@ -928,13 +928,157 @@
     )(rows, *grads, kept, router, expert_in, expert_out)
 
 
+def finish_kernel(
+    rows_ref,
+    small_ref,
+    rows_out,
+    small_out,
+    sums,
+    from_c,
+    from_x,
+    from_y,
+    from_z,
+    send_z,
+    recv_z,
+    small_send,
+    small_recv,
+):
+    w, c, z = (lax.axis_index(a) for a in EVERYONE)
+    wx, wy, wd = neighbours(w)
+    dev_x, dev_y, dev_c = ((wx, c, z), (wy, c, z), (w, 1 - c, z))
+    order = share_order(z)
+    barrier = pltpu.get_barrier_semaphore()
+    around = [(w, c, (z + k) % 4) for k in range(1, 4)]
+    for device in [dev_x, dev_y, dev_c] + around:
+        pl.semaphore_signal(barrier, inc=1, device_id=device, device_id_type=MESH)
+    pl.semaphore_wait(barrier, 6)
+    rows_out[z] = rows_ref[...]
+    sides = ((w, c, z + 1), (w, c, z - 1))
+
+    def moved(j, side):
+        return pltpu.make_async_remote_copy(
+            src_ref=rows_ref if j == 0 else rows_out.at[order[j]],
+            dst_ref=rows_out.at[order[j]],
+            send_sem=send_z.at[j, side],
+            recv_sem=recv_z.at[order[j]],
+            device_id=sides[side],
+            device_id_type=MESH,
+        )
+
+    def onward(j):
+        return (((order[j] <= z) & (z < 3), 0), ((order[j] >= z) & (z > 0), 1))
+
+    def along(j):
+        for there, side in onward(j):
+            pl.when(there)(lambda: moved(j, side).start())
+
+    def passed_on(j):
+        moved(j, 0).wait_recv()
+        along(j)
+
+    def small(i, src, dst, device):
+        return pltpu.make_async_remote_copy(
+            src_ref=src,
+            dst_ref=dst,
+            send_sem=small_send.at[i],
+            recv_sem=small_recv.at[i],
+            device_id=device,
+            device_id_type=MESH,
+        )
+
+    def sibling(k):
+        return small(k, small_ref.at[k, 1 - c], from_c.at[k], dev_c)
+
+    def to_x(k):
+        return small(4 + k, sums.at[(wx, wd)[k]], from_x.at[k], dev_x)
+
+    def to_y():
+        return small(6, sums.at[wy], from_y, dev_y)
+
+    def to_z(target, source):
+        return pltpu.make_async_remote_copy(
+            src_ref=sums.at[w, target],
+            dst_ref=from_z.at[source],
+            send_sem=small_send.at[7 + target],
+            recv_sem=small_recv.at[7 + source],
+            device_id=(w, c, target),
+            device_id_type=MESH,
+        )
+
+    along(0)
+    for k in range(4):
+        sibling(k).start()
+    for k in range(4):
+        sibling(k).wait_recv()
+        sums[k] = small_ref[k, c] + from_c[k]
+    for k in range(2):
+        to_x(k).start()
+    for k in range(2):
+        to_x(k).wait_recv()
+    sums[w] = sums[w] + from_x[0]
+    sums[wy] = sums[wy] + from_x[1]
+    to_y().start()
+    passed_on(1)
+    to_y().wait_recv()
+    sums[w] = sums[w] + from_y[...]
+    for k in range(1, 4):
+        to_z((z + k) % 4, z).start()
+    passed_on(2)
+    added = sums[w, z]
+    for k in range(1, 4):
+        to_z(z, (z + k) % 4).wait_recv()
+    for k in range(1, 4):
+        added = added + from_z[(z + k) % 4]
+    small_out[...] = added
+    passed_on(3)
+    for k in range(4):
+        sibling(k).wait_send()
+    for k in range(2):
+        to_x(k).wait_send()
+    to_y().wait_send()
+    for k in range(1, 4):
+        to_z((z + k) % 4, z).wait_send()
+    for j in range(4):
+        for there, side in onward(j):
+            pl.when(there)(lambda: moved(j, side).wait_send())
+
+
+def finish_call(rows, small):
+    dma = pltpu.SemaphoreType.DMA
+    vmem = pl.BlockSpec(memory_space=pltpu.VMEM)
+    block = small.shape[3:]
+    f32 = jnp.float32
+    return pl.pallas_call(
+        finish_kernel,
+        out_shape=(
+            jax.ShapeDtypeStruct((4,) + rows.shape, rows.dtype),
+            jax.ShapeDtypeStruct(block, f32),
+        ),
+        in_specs=[vmem, vmem],
+        out_specs=(vmem, vmem),
+        scratch_shapes=[
+            pltpu.VMEM((4, 4) + block, f32),
+            pltpu.VMEM((4, 4) + block, f32),
+            pltpu.VMEM((2, 4) + block, f32),
+            pltpu.VMEM((4,) + block, f32),
+            pltpu.VMEM((4,) + block, f32),
+            dma((4, 2)),
+            dma((4,)),
+            dma((11,)),
+            dma((11,)),
+        ],
+        compiler_params=pltpu.CompilerParams(
+            collective_id=1, has_side_effects=True, vmem_limit_bytes=32 << 20
+        ),
+    )(rows, small)
+
+
 def swapped(rows, flip):
     return lax.ppermute(rows, WEIGHTS, [(k, k ^ flip) for k in range(4)])
 
 
-def grads_around(rows, share):
+def grads_around(rows, from_x, from_y, share):
     half = rows.shape[1] // 2
-    from_x, from_y = (swapped(rows, 1), swapped(rows, 2))
     parts = (rows, from_x, from_y, swapped(from_x[:, :half], 2), swapped(from_y[:, half:], 1))
     return [part.reshape(-1, share, part.shape[1]) for part in parts]
 
@@ -1001,7 +1145,7 @@
     )
     own_grads = grad_out.reshape(token_count, model_width)
     front, own_grads = lax.optimization_barrier((front, own_grads))
-    around = grads_around(own_grads, share)
+    from_x, from_y = (swapped(own_grads, 1), swapped(own_grads, 2))
     back_small = jnp.concatenate(
         [router, fit_rows(kept.astype(bf16), weight_rows)], axis=1
     )
@@ -1075,6 +1219,8 @@
     attn_probs = (exponent / row_total).astype(bf16)
     attended = jnp.einsum(BY_QUERY, attn_probs, all_values, preferred_element_type=f32)
     attended_low = attended.reshape(token_count, -1).astype(bf16)
+    from_x, from_y, attended_low = lax.optimization_barrier((from_x, from_y, attended_low))
+    around = grads_around(own_grads, from_x, from_y, share)
     attn_partial = jnp.einsum("tf,df->td", attended_low, out_full, preferred_element_type=f32)
 
     own_rows = lambda rows: lax.dynamic_slice_in_dim(rows, tensor_rank * share, share, 0)
@@ -1101,15 +1247,6 @@
         for rows in (normed_all, grads_all, gated, d_both)
     )
     layer_out = gathered((hidden + moe_own).astype(bf16), TENSOR).reshape(layer_in.shape)
-    grad_expert_in = (
-        jnp.dot(normed_all.T, d_both, preferred_element_type=f32)
-        .reshape(model_width, local_experts, 2, hidden_width)
-        .transpose(1, 2, 0, 3)
-    )
-    grad_expert_out = jnp.dot(gated.T, grads_all, preferred_element_type=f32).reshape(
-        expert_out.shape
-    )
-
     kept_own = own_rows(kept.T).astype(f32)
     probs_own = jax.nn.softmax(
         jnp.dot(normed_two, router_full, preferred_element_type=f32), axis=1
@@ -1128,6 +1265,12 @@
         scaled_ffn - unit_two * jnp.mean(scaled_ffn * unit_two, axis=1, keepdims=True)
     )
     d_hidden_low = gathered(d_hidden.astype(bf16), TENSOR)
+    grad_expert_in = (
+        jnp.dot(normed_all.T, d_both, preferred_element_type=f32)
+        .reshape(model_width, local_experts, 2, hidden_width)
+        .transpose(1, 2, 0, 3)
+    )
+    d_hidden_low, grad_expert_in = lax.optimization_barrier((d_hidden_low, grad_expert_in))
 
     d_attended = (
         jnp.dot(d_hidden_low, out_full, preferred_element_type=f32)
@@ -1185,11 +1328,17 @@
     d_key_gain = jnp.sum(d_key_hat * key_raw * key_scale, axis=0).reshape(local_heads, head_size).T
     d_qk_gains = jnp.stack([d_query_gain, d_key_gain], axis=1)
     d_projected = jnp.concatenate([d_query_raw, d_key_raw, d_value], axis=1).astype(bf16)
+    d_projected, layer_out = lax.optimization_barrier((d_projected, layer_out))
     d_normed_one = scattered(
         jnp.einsum("tf,df->td", d_projected, qkv_full, preferred_element_type=f32).astype(bf16),
         TENSOR,
     ).astype(f32)
     d_qkv = jnp.einsum("td,tf->df", normed_one, d_projected, preferred_element_type=f32)
+
+    grad_expert_out = jnp.dot(gated.T, grads_all, preferred_element_type=f32).reshape(
+        expert_out.shape
+    )
+    d_normed_one, grad_expert_out = lax.optimization_barrier((d_normed_one, grad_expert_out))
 
     scale_own = own_rows(scale_one)
     unit_one = residual_own * scale_own
@@ -1198,7 +1347,6 @@
     grad_in = d_hidden + scale_own * (
         scaled_attn - unit_one * jnp.mean(scaled_attn * unit_one, axis=1, keepdims=True)
     )
-    grad_in = gathered(grad_in.astype(bf16), TENSOR).astype(f32).reshape(layer_in.shape)
 
     grad_qkv = (
         scattered(d_qkv.astype(bf16), group)
@@ -1218,15 +1366,22 @@
             d_qk_gains.reshape(group_count, 1, -1) * own_slot,
         ],
         axis=2,
-    ).reshape(group_count * tensor_count, -1)
-    small = scattered(small, everyone)[0]
+    )
+    small = jnp.pad(small, ((0, 0), (0, 0), (0, -small.shape[2] % 128)))
+    grad_in, small = finish_call(
+        grad_in.astype(bf16), small.reshape(4, 2, tensor_count, -1, 128)
+    )
+    grad_in = grad_in.astype(f32).reshape(layer_in.shape)
+    small = small.reshape(-1)
     ends = (gain_share * 2, gain_share * 2 + weight_rows * router_share)
     return (
         layer_out,
         grad_in,
         small[: ends[0]].reshape(gain_share, 2),
         grad_qkv,
-        small[ends[1] :].reshape(head_rows, 2, local_heads),
+        small[ends[1] : ends[1] + d_qk_gains.size // group_count].reshape(
+            head_rows, 2, local_heads
+        ),
         grad_out_weight,
         small[ends[0] : ends[1]].reshape(weight_rows, router_share),
         grad_expert_in,

time: 964 us -> 742 us (0.77)
  waiting for transfers between devices: 418 us -> 155 us
  Pallas kernels: 268 us -> 308 us
    all_gather x5 -> x4, waiting for transfers between devices: 175 us -> 59.4 us  [gathered(): return lax.all_gather(rows, axes, axis=0, tiled=True)]
    unnamed x11 -> x8, waiting for transfers between devices: 100 us -> 0.13 us
    pallas_call x0 -> x1, Pallas kernels: none -> 37.8 us  [finish_call(): pl.pallas_call(finish_kernel, out_shape=(jax.ShapeDtypeStruct((4,) + rows...]
    ppermute x4, waiting for transfers between devices: 51.7 us -> 16.4 us  [swapped(): return lax.ppermute(rows, WEIGHTS, [(k, k ^ flip) for k in range(4)])]
    reduce_scatter x4, waiting for transfers between devices: 90.3 us -> 78.7 us  [scattered(): return lax.psum_scatter(rows, axes, scatter_dimension=0, tiled=True)]
  transfers between devices with their start and end apart: 18 -> 16, of which waited for: 10 -> 7; matrix products, arithmetic and copies ran while one was open for 17% -> 25% of each run, Pallas kernels for 0% -> 5%
where the time goes in v3:
time: 742 us; the launch traced here: 733 us
  Pallas kernels  308 us (42%)
  waiting for transfers between devices  155 us (21%)
  matrix products  97.1 us (13%)
  local copies, waits for them, and re-layouts  74.8 us (10%)
  other arithmetic  51.2 us (7%)
  blocking collectives  20.9 us (3%)
  between operations  15.5 us (2%)
  starting transfers between devices  10.8 us (1%)
    pallas_call x1, Pallas kernels, experts_call(): pl.pallas_call(functools.partial(experts_kernel, experts), out_shape=tupl...  271 us
    reduce_scatter x4, waiting for transfers between devices, scattered(): return lax.psum_scatter(rows, axes, scatter_dimension=0, tiled=True)  78.7 us
    all_gather x4, waiting for transfers between devices, gathered(): return lax.all_gather(rows, axes, axis=0, tiled=True)  59.4 us
    pallas_call x1, Pallas kernels, finish_call(): pl.pallas_call(finish_kernel, out_shape=(jax.ShapeDtypeStruct((4,) + rows...  37.8 us
    dot_general x1, matrix products, per_device_dense(): jnp.dot(normed_all.T, d_both, preferred_element_type=f32)  24.4 us
    psum x2, blocking collectives, row_sums(): return lax.psum(partial_rows, TENSOR)  20.9 us
    ppermute x4, waiting for transfers between devices, swapped(): return lax.ppermute(rows, WEIGHTS, [(k, k ^ flip) for k in range(4)])  16.4 us
    dot_general x1, matrix products, per_device_dense(): jnp.dot(gated.T, grads_all, preferred_element_type=f32)  15.1 us
  transfers between devices with their start and end apart: 16, of which 7 were waited for; matrix products, arithmetic and copies ran while one was open for 25% of the time, Pallas kernels for 5%

profile of v3, /device:TPU:0, one launch (start us, length us, event | category | flops | bytes accessed | tf_op | source)
XLA Modules:
  0.0 733.4 jit_solution(3928979099499664322)
XLA Ops:
  9.7 3.4 concatenate.67
  25.0 37.9 %all-gather.5.cloned.1.call-done = bf16[2048,1539]{0,1:T(8,128)(2,1)} async-done(((bf16[256,1539]{0,1:T(8,128)(2,1)}), bf16[2048,1539]{0,1:T(8,128)(2,1)}) %all-gather.5.cloned.1.call-update) | async-done | bytes 6303760 | tf_op jit(solution)/shard_map/all_gather | solution.py:1087
  64.4 6.3 fusion.4
  79.4 11.7 %psum.14 = f32[512,2]{0,1:T(2,128)S(1)} all-reduce(f32[512,2]{0,1:T(2,128)S(1)} %pad_maximum_fusion.5), channel_id=1, replica_groups=mesh['weights'=4,'context'=2,'tensor'=4] {'tensor'}, use_global_device_ids=true, to_apply=%region_3.4 | all-reduce | flops 1024 | bytes 8192 | tf_op jit(solution)/shard_map/psum | solution.py:69
  92.7 2.5 reshape.539
  105.0 3.7 fusion.73
  114.2 16.2 %collective-permute-done.1 = bf16[512,2048]{1,0:T(8,128)(2,1)} collective-permute-done((bf16[512,2048]{1,0:T(8,128)(2,1)}, bf16[512,2048]{1,0:T(8,128)(2,1)}, u32[]{:S(2)}, u32[]{:S(2)}) %collective-permute-start.1) | collective-permute-done | bytes 2097184 | tf_op jit(solution)/shard_map/ppermute | solution.py:1077
  130.6 4.4 convolution_convert_fusion.2
  135.1 2.5 convert_element_type.148
  151.1 27.9 %reduce-scatter.5.cloned.1.call-done = bf16[128,2048]{1,0:T(8,128)(2,1)} async-done(((bf16[512,2048]{1,0:T(8,128)(2,1)}), bf16[128,2048]{1,0:T(8,128)(2,1)}) %reduce-scatter.5.cloned.1.call-update) | async-done | bytes 524304 | tf_op jit(solution)/shard_map/reduce_scatter | solution.py:1091
  181.8 270.5 %shard_map.187 = (bf16[4,2,4,128,2048]{4,3,2,1,0:T(8,128)(2,1)}, bf16[4,2,4,128,2048]{4,3,2,1,0:T(8,128)(2,1)}, bf16[4,2,4,128,512]{4,3,2,1,0:T(8,128)(2,1)}, bf...) custom-call(bf16[128,2048]{1,0:T(8,128)(2,1)} %multiply_convert_fusion.1.x_ref, ...), custom_call_target="tpu_custom_call" | custom-call | tf_op jit(solution)/shard_map/pallas_call | solution.py:879
  452.3 11.8 %copy.219 = bf16[1024,4096]{1,0:T(8,128)(2,1)} copy(bf16[1024,4096]{0,1:T(8,128)(2,1)} %bitcast.201) | data formatting | bytes 16777216 | tf_op jit(solution)/shard_map/dot_general | solution.py:1269
  466.9 2.6 multiply_reduce_fusion.2
  469.4 3.1 add_convert_fusion.1
  472.6 24.4 %convolution_bitcast_fusion = f32[2,2,2048,256]{3,2,1,0:T(8,128)} fusion(bf16[4096,2048,1,1]{1,0,3,2:T(8,128)(2,1)} %bitcast.259, bf16[2,2,256,4096]{3,2,1,0:T(8,128)(2,1)} %bitcast.200), kind=kOutput, calls=%fused_computation.14 | convolution fusion | flops 17179869184 | bytes 33554432 | tf_op jit(solution)/shard_map/dot_general | solution.py:1269
  497.1 21.6 %all-gather.9.cloned.1.call-done = bf16[512,2048]{1,0:T(8,128)(2,1)} async-done(((bf16[128,2048]{1,0:T(8,128)(2,1)}), bf16[512,2048]{1,0:T(8,128)(2,1)}) %all-gather.9.cloned.1.call-update) | async-done | bytes 2097168 | tf_op jit(solution)/shard_map/all_gather | solution.py:1087
  518.6 2.9 fusion.22
  521.6 5.9 multiply_reduce_fusion
  533.6 2.8 broadcast_multiply_fusion
  536.5 2.9 fusion.19
  544.6 4.3 convolution_convert_fusion.1
  561.2 9.2 %psum.15 = f32[512,2]{0,1:T(2,128)S(1)} all-reduce(f32[512,2]{0,1:T(2,128)S(1)} %pad_maximum_fusion.6), channel_id=1, replica_groups=mesh['weights'=4,'context'=2,'tensor'=4] {'tensor'}, use_global_device_ids=true, to_apply=%region_17.18 | all-reduce | flops 1024 | bytes 8192 | tf_op jit(solution)/shard_map/psum | solution.py:69
  573.9 8.6 %fusion.13 = bf16[512,2048]{1,0:T(8,128)(2,1)} fusion(bf16[512,1536]{1,0:T(8,128)(2,1)} %pad_maximum_fusion, bf16[2048,1539]{0,1:T(8,128)(2,1)} %all-gather.5.cloned.1.call-done), kind=kOutput, calls=%fused_computation.23 | convolution fusion | flops 3222274048 | bytes 9961472 | tf_op jit(solution)/shard_map/tf,df->td/dot_general | solution.py:1333
  582.5 7.0 convolution_convert_fusion
  589.6 6.5 copy.230
  598.7 15.1 %fusion.76 = f32[2,256,2048]{2,1,0:T(8,128)} fusion(bf16[2,256,4096]{2,1,0:T(8,128)(2,1)} %bitcast.207, bf16[4096,2048,1]{1,0,2:T(8,128)(2,1)} %bitcast.258), kind=kOutput, calls=%fused_computation.161 | convolution fusion | flops 8589934592 | bytes 25165824 | tf_op jit(solution)/shard_map/dot_general | solution.py:1338
  616.3 38.7 %reduce-scatter.7.cloned.1.call-done = bf16[128,2048]{1,0:T(8,128)(2,1)} async-done(((bf16[512,2048]{1,0:T(8,128)(2,1)}), bf16[128,2048]{1,0:T(8,128)(2,1)}) %reduce-scatter.7.cloned.1.call-update) | async-done | bytes 524304 | tf_op jit(solution)/shard_map/reduce_scatter | solution.py:1091
  662.6 2.4 add_convert_fusion.rows_ref
  665.0 37.8 %shard_map.188 = (bf16[4,128,2048]{2,1,0:T(8,128)(2,1)S(1)}, f32[10,128]{1,0:T(8,128)S(1)}) custom-call(bf16[128,2048]{1,0:T(8,128)(2,1)S(1)} %add_convert_fusion.rows_ref, f32[4,2,4,10,128]{4,3,2,1,0:T(8,128)S(1)} %copy.236.small_ref), custom_call_target="tpu_custom_call" | custom-call | tf_op jit(solution)/shard_map/pallas_call | solution.py:1051
  705.3 2.5 bitcast_convert_fusion
  707.8 12.1 %reduce-scatter.9.cloned.1.call-done = bf16[256,1536]{1,0:T(8,128)(2,1)} async-done(((bf16[2048,1536]{1,0:T(8,128)(2,1)}), bf16[256,1536]{1,0:T(8,128)(2,1)}) %reduce-scatter.9.cloned.1.call-update) | async-done | bytes 786448 | tf_op jit(solution)/shard_map/reduce_scatter | solution.py:1091
  722.9 3.2 copy.268
  (256 shorter events, 105.6 us)
Async XLA Ops:
  7.2 55.6 %all-gather.5.cloned.1.call-start = ((), (), s32[]{:S(2)}) async-start(), calls=%async_computation.4 | async-start | bytes 7114752 | tf_op jit(solution)/shard_map/all_gather | solution.py:1087
  13.2 117.5 %all-gather.7.cloned.1.call-start = ((), (), s32[]{:S(2)}) async-start(), calls=%async_computation.5 | async-start | bytes 2949120 | tf_op jit(solution)/shard_map/all_gather | solution.py:1087
  19.2 159.8 %reduce-scatter.5.cloned.1.call-start = ((), (), s32[]{:S(2)}) async-start(), calls=%async_computation.6 | async-start | bytes 2621440 | tf_op jit(solution)/shard_map/reduce_scatter | solution.py:1091
  19.9 50.8 %copy-start.42 = (f32[512]{0:T(512)}, f32[512]{0:T(512)S(1)}, u32[]{:S(2)}) copy-start(f32[512]{0:T(512)S(1)} %add_rsqrt_fusion) | copy-start | bytes 6148
  21.8 42.6 %copy-start.16 = (f32[512,128]{1,0:T(8,128)}, f32[512,128]{1,0:T(8,128)S(1)}, u32[]{:S(2)}) copy-start(f32[512,128]{1,0:T(8,128)S(1)} %get-tuple-element.130) | copy-start | bytes 786436
  70.7 24.6 %copy-start.1 = (f32[512,1536]{1,0:T(8,128)}, f32[512,1536]{1,0:T(8,128)S(1)}, u32[]{:S(2)}) copy-start(f32[512,1536]{1,0:T(8,128)S(1)} %fusion.4) | copy-start | bytes 9437188
  72.6 57.9 %collective-permute-start.1 = (bf16[512,2048]{1,0:T(8,128)(2,1)}, bf16[512,2048]{1,0:T(8,128)(2,1)}, u32[]{:S(2)}, u32[]{:S(2)}) collective-permute-start(bf16[512,2048]{1,0:T(8,128)(2,1)} %bitcast.2), channel_id=1, source_target_pairs={{0,8},{8,0},{16,24},{24,16},{1,9},{9,1},{17,25},{25,17},{2,10},{10... | collective-permute-start | bytes 6291464 | tf_op jit(solution)/shard_map/ppermute | solution.py:1077
  74.0 56.6 %collective-permute-start.2 = (bf16[512,2048]{1,0:T(8,128)(2,1)}, bf16[512,2048]{1,0:T(8,128)(2,1)}, u32[]{:S(2)}, u32[]{:S(2)}) collective-permute-start(bf16[512,2048]{1,0:T(8,128)(2,1)} %bitcast.2), channel_id=1, source_target_pairs={{0,16},{8,24},{16,0},{24,8},{1,17},{9,25},{17,1},{25,9},{2,18},{10... | collective-permute-start | bytes 6291464 | tf_op jit(solution)/shard_map/ppermute | solution.py:1077
  98.2 6.8 collective-permute-start
  102.0 8.6 %collective-permute-start.3 = (bf16[1,512,4,128]{1,3,2,0:T(8,128)(2,1)S(1)}, bf16[1,512,4,128]{1,3,2,0:T(8,128)(2,1)S(1)}, u32[]{:S(2)}, u32[]{:S(2)}) collective-permute-start(bf16[1,512,4,128]{1,3,2,0:T(8,128)(2,1)S(1)} %bitcast.214), channel_id=1, source_target_pairs={{0,4},{1,5},{2,6},{3,7},{8,12},{9,13},{10,14},{11,15},{16,20},{17,... | collective-permute-start | bytes 1572872 | tf_op jit(solution)/shard_map/ppermute | solution.py:25
  114.2 20.8 %copy-start.46 = (bf16[4,128,512]{2,1,0:T(8,128)(2,1)}, bf16[4,128,512]{2,1,0:T(8,128)(2,1)S(1)}, u32[]{:S(2)}) copy-start(bf16[4,128,512]{2,1,0:T(8,128)(2,1)S(1)} %fusion.25) | copy-start | bytes 1572868
  135.0 383.6 %all-gather.9.cloned.1.call-start = ((), (), s32[]{:S(2)}) async-start(), calls=%async_computation.7 | async-start | bytes 2621440 | tf_op jit(solution)/shard_map/all_gather | solution.py:1087
  146.8 35.0 %collective-permute-start.4 = (bf16[512,1024]{1,0:T(8,128)(2,1)S(1)}, bf16[512,1024]{1,0:T(8,128)(2,1)}, u32[]{:S(2)}, u32[]{:S(2)}) collective-permute-start(bf16[512,1024]{1,0:T(8,128)(2,1)S(1)} %slice.135), channel_id=1, source_target_pairs={{0,16},{8,24},{16,0},{24,8},{1,17},{9,25},{17,1},{25,9},{2,18},{10... | collective-permute-start | bytes 3145736 | tf_op jit(solution)/shard_map/ppermute | solution.py:1077
  150.2 31.6 %collective-permute-start.5 = (bf16[512,1024]{1,0:T(8,128)(2,1)}, bf16[512,1024]{1,0:T(8,128)(2,1)}, u32[]{:S(2)}, u32[]{:S(2)}) collective-permute-start(bf16[512,1024]{1,0:T(8,128)(2,1)} %slice.136), channel_id=1, source_target_pairs={{0,8},{8,0},{16,24},{24,16},{1,9},{9,1},{17,25},{25,17},{2,10},{10... | collective-permute-start | bytes 3145736 | tf_op jit(solution)/shard_map/ppermute | solution.py:1077
  180.6 288.8 %copy-start.3 = (f32[128,2048]{1,0:T(8,128)}, f32[128,2048]{1,0:T(8,128)S(1)}, u32[]{:S(2)}) copy-start(f32[128,2048]{1,0:T(8,128)S(1)} %get-tuple-element.111) | copy-start | bytes 3145732
  180.7 288.8 %copy-start.35 = (f32[128]{0:T(128)}, f32[128]{0:T(128)S(1)}, u32[]{:S(2)}) copy-start(f32[128]{0:T(128)S(1)} %add_rsqrt_fusion.1) | copy-start | bytes 1540
  465.8 31.2 %copy-start.37 = (f32[128]{0:T(128)}, f32[128]{0:T(128)S(1)}, u32[]{:S(2)}) copy-start(f32[128]{0:T(128)S(1)} %fusion.45) | copy-start | bytes 1540
  469.4 27.6 %copy-start.40 = (f32[128]{0:T(128)}, f32[128]{0:T(128)S(1)}, u32[]{:S(2)}) copy-start(f32[128]{0:T(128)S(1)} %broadcast_multiply_fusion.6) | copy-start | bytes 1540
  472.6 101.3 %all-gather.11.cloned.1.call-start = ((), (), s32[]{:S(2)}) async-start(), calls=%async_computation.8 | async-start | bytes 2621440 | tf_op jit(solution)/shard_map/all_gather | solution.py:1087
  472.6 46.0 %copy-start.20 = (bf16[2048,560]{1,0:T(8,128)(2,1)S(1)}, bf16[2048,560]{1,0:T(8,128)(2,1)}, u32[]{:S(2)}) copy-start(bf16[2048,560]{1,0:T(8,128)(2,1)} %all-gather.7.cloned.1.call-done) | copy-start | bytes 6881284
  497.0 24.6 %copy-start.25 = (bf16[512,512]{0,1:T(8,128)(2,1)S(1)}, bf16[512,512]{0,1:T(8,128)(2,1)}, u32[]{:S(2)}) copy-start(bf16[512,512]{0,1:T(8,128)(2,1)} %copy-done.24) | copy-start | bytes 1572868
  497.0 117.3 %reduce-scatter.11.cloned.1.call-start = ((), (), s32[]{:S(2)}) async-start(), calls=%async_computation.11 | async-start | bytes 2359296 | tf_op jit(solution)/shard_map/reduce_scatter | solution.py:1091
  531.4 17.6 %copy-start.5 = (f32[1,1024,4,128]{3,1,2,0:T(8,128)}, f32[1,1024,4,128]{3,1,2,0:T(8,128)S(1)}, u32[]{:S(2)}) copy-start(f32[1,1024,4,128]{3,1,2,0:T(8,128)S(1)} %multiply_bitcast_fusion) | copy-start | bytes 6291460
  532.4 16.6 %collective-permute-start.6 = (bf16[1,512,4,128]{3,1,2,0:T(8,128)(2,1)}, bf16[1,512,4,128]{3,1,2,0:T(8,128)(2,1)}, u32[]{:S(2)}, u32[]{:S(2)}) collective-permute-start(bf16[1,512,4,128]{3,1,2,0:T(8,128)(2,1)} %slice.249), channel_id=1, source_target_pairs={{4,0},{5,1},{6,2},{7,3},{12,8},{13,9},{14,10},{15,11},{20,16},{21,... | collective-permute-start | bytes 1572872 | tf_op jit(solution)/shard_map/ppermute | solution.py:25
  543.2 11.8 %collective-permute-start.7 = (bf16[1,512,4,128]{1,3,2,0:T(8,128)(2,1)}, bf16[1,512,4,128]{1,3,2,0:T(8,128)(2,1)}, u32[]{:S(2)}, u32[]{:S(2)}) collective-permute-start(bf16[1,512,4,128]{1,3,2,0:T(8,128)(2,1)} %slice.248), channel_id=1, source_target_pairs={{4,0},{5,1},{6,2},{7,3},{12,8},{13,9},{14,10},{15,11},{20,16},{21,... | collective-permute-start | bytes 1572872 | tf_op jit(solution)/shard_map/ppermute | solution.py:25
  548.9 106.1 %reduce-scatter.7.cloned.1.call-start = ((), (), s32[]{:S(2)}) async-start(), calls=%async_computation.9 | async-start | bytes 2621440 | tf_op jit(solution)/shard_map/reduce_scatter | solution.py:1091
  582.5 137.4 %reduce-scatter.9.cloned.1.call-start = ((), (), s32[]{:S(2)}) async-start(), calls=%async_computation.10 | async-start | bytes 7077888 | tf_op jit(solution)/shard_map/reduce_scatter | solution.py:1091
  613.8 43.9 %copy-start.34 = (f32[2048]{0:T(1024)S(1)}, f32[2048]{0:T(1024)}, u32[]{:S(2)}) copy-start(f32[2048]{0:T(1024)} %get-tuple-element.102) | copy-start | bytes 24580
  613.8 48.7 %copy-start.4 = (f32[128,2048]{1,0:T(8,128)S(1)}, f32[128,2048]{1,0:T(8,128)}, u32[]{:S(2)}) copy-start(f32[128,2048]{1,0:T(8,128)} %copy-done.3) | copy-start | bytes 3145732
  613.8 48.8 %copy-start.15 = (f32[128,2048]{1,0:T(8,128)S(1)}, f32[128,2048]{1,0:T(8,128)}, u32[]{:S(2)}) copy-start(f32[128,2048]{1,0:T(8,128)} %copy-done.14) | copy-start | bytes 3145732
  613.8 48.8 %copy-start.36 = (f32[128]{0:T(128)S(1)}, f32[128]{0:T(128)}, u32[]{:S(2)}) copy-start(f32[128]{0:T(128)} %copy-done.35) | copy-start | bytes 1540
  613.8 48.8 %copy-start.41 = (f32[128]{0:T(128)S(1)}, f32[128]{0:T(128)}, u32[]{:S(2)}) copy-start(f32[128]{0:T(128)} %copy-done.40) | copy-start | bytes 1540
  (34 other events, 194.4 us)
Sparse Core Ops, SparseCore 0:
  13.3 49.5 all-gather.4
  64.7 40.6 all-gather.6
  135.1 43.8 reduce-scatter.4
  472.7 45.9 all-gather.8
  520.1 44.6 all-gather.10
  568.3 39.9 reduce-scatter.10
  611.1 43.8 reduce-scatter.6
  658.8 61.0 reduce-scatter.8

commit v4 on v3

--- a/solution.py
+++ b/solution.py
@@ -377,6 +377,10 @@
     return (z, z + 1 - 2 * upper, 2 + upper - 2 * odd, 3 - 3 * upper)
 
 
+def share_turns(z):
+    return (z, (z + 2) % 4, 3 - z, z + 1 - 2 * (z % 2))
+
+
 def neighbours(w):
     wx, wy = (w + 1 - 2 * (w % 2), (w + 2) % 4)
     return (wx, wy, wx + wy - w)
@@ -398,20 +402,23 @@
     grads_out,
     gated_out,
     both_out,
+    moe_out,
     dx_own,
-    moe_own,
     x_tile,
     w_in,
     w_out,
     grads,
     gated,
     both,
-    *scratch,
-):
-    others, mine, sibs, from_x1, from_y1, from_y2, from_x2, from_z = (
-        (scratch[2 * k], scratch[2 * k + 1]) for k in range(8)
-    )
-    (
+    moe_tile,
+    others,
+    mine,
+    sibs,
+    from_x1,
+    from_y1,
+    from_y2,
+    from_x2,
+    from_z,
         own_sem,
         tile_sem,
         weight_sem,
@@ -433,18 +440,18 @@
         two_recv,
         end_send,
         end_recv,
-    ) = scratch[16:]
+):
     w, c, z = (lax.axis_index(a) for a in (WEIGHTS, CONTEXT, TENSOR))
     wx, wy, wd = neighbours(w)
     share, width = x_ref.shape
     half = width // 2
     lo, hi = (pl.ds(0, half), pl.ds(half, half))
     dev_x, dev_y, dev_c = ((wx, c, z), (wy, c, z), (w, 1 - c, z))
-    order = share_order(z)
+    turns = share_turns(z)
     hidden = out_w_ref.shape[1]
     group = w * 2 + c
     bf16, f32 = (jnp.bfloat16, jnp.float32)
-    wides = (width + 128, width)
+    low, high = (pl.ds(0, half), pl.ds(half, half + 128))
 
     def loads():
         return [
@@ -521,35 +528,34 @@
         copy(view(chunk, cols), chunk, cols, slot, (send_c, 0, 0), dev_c).wait_recv()
 
     def spread(j):
-        chunk = (order[j], c, w)
+        chunk = (turns[j], c, w)
         src = x_ref if j == 0 else None
         start(chunk, None, 1, (send_x, j, 0), dev_x, src)
         start(chunk, None, 2, (send_y, j, 0), dev_y, src)
         start(chunk, None, 0, (send_c, j, 0), dev_c, src)
 
     def onward(j):
-        chunk = (order[j], c, w)
+        chunk = (turns[j], c, w)
 
         def moved(side):
             src = x_ref if j == 0 else view(chunk, None)
             return copy(src, chunk, None, 0, (send_z, j, side), devices_z[side])
 
         return (
-            ((order[j] <= z) & (z < 3), functools.partial(moved, 0)),
-            ((order[j] >= z) & (z > 0), functools.partial(moved, 1)),
+            ((turns[j] <= z) & (z < 3), functools.partial(moved, 0)),
+            ((turns[j] >= z) & (z > 0), functools.partial(moved, 1)),
         )
 
     def along(j):
         for there, moved in onward(j):
             pl.when(there)(lambda: moved().start())
 
-    def share_in(j):
-        arrived((order[j], c, w), None, 0)
+    def pass_on(j):
+        arrived((turns[j], c, w), None, 0)
         along(j)
-        spread(j)
 
     def relay(j):
-        from_x, from_y = ((order[j], c, wx), (order[j], c, wy))
+        from_x, from_y = ((turns[j], c, wx), (turns[j], c, wy))
         arrived(from_x, None, 1)
         start(from_x, lo, 3, (send_y, j, 1), dev_y)
         start(from_x, None, 1, (send_c, j, 1), dev_c)
@@ -558,72 +564,59 @@
         start(from_y, None, 2, (send_c, j, 2), dev_c)
 
     def across(j):
-        chunk = (order[j], c, wd)
+        chunk = (turns[j], c, wd)
         for cols, slot in ((lo, 3), (hi, 4)):
             arrived(chunk, cols, slot)
             start(chunk, cols, slot, (send_c, j, slot), dev_c)
 
     def sibling(j):
         for ww, cols, slot in ((w, None, 0), (wx, None, 1), (wy, None, 2), (wd, lo, 3), (wd, hi, 4)):
-            arrived((order[j], 1 - c, ww), cols, slot)
-
-
-    def parts_of(a):
-        return (pl.ds(0, half), pl.ds(half, wides[a] - half))
-
-    def to_sibling(a):
+            arrived((turns[j], 1 - c, ww), cols, slot)
+
+
+    def remote(src, dst, send, got, device):
         return pltpu.make_async_remote_copy(
-            src_ref=others[a],
-            dst_ref=sibs[a],
-            send_sem=sib_send.at[a],
-            recv_sem=sib_recv.at[a],
-            device_id=dev_c,
+            src_ref=src,
+            dst_ref=dst,
+            send_sem=send,
+            recv_sem=got,
+            device_id=device,
             device_id_type=MESH,
         )
 
-    def first_hops(a, j):
-        low, high = parts_of(a)
+    def to_sibling():
+        return remote(others, sibs, sib_send, sib_recv, dev_c)
+
+    def first_hops(j):
         moves = (
-            (wx, low, from_x1[a].at[j, 0], dev_x),
-            (wd, low, from_x1[a].at[j, 1], dev_x),
-            (wy, high, from_y1[a].at[j, 0], dev_y),
-            (wd, high, from_y1[a].at[j, 1], dev_y),
+            (wx, low, from_x1.at[j, 0], dev_x),
+            (wd, low, from_x1.at[j, 1], dev_x),
+            (wy, high, from_y1.at[j, 0], dev_y),
+            (wd, high, from_y1.at[j, 1], dev_y),
         )
         return [
-            pltpu.make_async_remote_copy(
-                src_ref=mine[a].at[j % 2, ww, :, cols],
-                dst_ref=dst,
-                send_sem=one_send.at[a, j, i],
-                recv_sem=one_recv.at[a, j, i],
-                device_id=device,
-                device_id_type=MESH,
+            remote(
+                mine.at[j % 2, ww, :, cols], dst, one_send.at[j, i], one_recv.at[j, i], device
             )
             for i, (ww, cols, dst, device) in enumerate(moves)
         ]
 
-    def second_hops(a, j):
-        low, high = parts_of(a)
-        moves = ((wy, low, from_y2[a].at[j], dev_y), (wx, high, from_x2[a].at[j], dev_x))
+    def second_hops(j):
+        moves = ((wy, low, from_y2.at[j], dev_y), (wx, high, from_x2.at[j], dev_x))
         return [
-            pltpu.make_async_remote_copy(
-                src_ref=mine[a].at[j % 2, ww, :, cols],
-                dst_ref=dst,
-                send_sem=two_send.at[a, j, i],
-                recv_sem=two_recv.at[a, j, i],
-                device_id=device,
-                device_id_type=MESH,
+            remote(
+                mine.at[j % 2, ww, :, cols], dst, two_send.at[j, i], two_recv.at[j, i], device
             )
             for i, (ww, cols, dst, device) in enumerate(moves)
         ]
 
-    def last_hop(a, source, j):
-        return pltpu.make_async_remote_copy(
-            src_ref=mine[a].at[j % 2, w],
-            dst_ref=from_z[a].at[source],
-            send_sem=end_send.at[a, j],
-            recv_sem=end_recv.at[a, source],
-            device_id=(w, c, order[j]),
-            device_id_type=MESH,
+    def last_hop(source, j):
+        return remote(
+            mine.at[j % 2, w],
+            from_z.at[source],
+            end_send.at[j],
+            end_recv.at[source],
+            (w, c, turns[j]),
         )
 
     def total(*terms):
@@ -634,41 +627,32 @@
 
     def after_first(j):
         p = j % 2
-        for a in range(2):
-            low, high = parts_of(a)
-            for moved in first_hops(a, j):
-                moved.wait_recv()
-            mine[a][p, wy, :, low] = total(mine[a][p, wy, :, low], from_x1[a][j, 1]).astype(bf16)
-            mine[a][p, wx, :, high] = total(mine[a][p, wx, :, high], from_y1[a][j, 1]).astype(bf16)
-            for moved in second_hops(a, j):
-                moved.start()
+        for moved in first_hops(j):
+            moved.wait_recv()
+        mine[p, wy, :, low] = total(mine[p, wy, :, low], from_x1[j, 1]).astype(bf16)
+        mine[p, wx, :, high] = total(mine[p, wx, :, high], from_y1[j, 1]).astype(bf16)
+        for moved in second_hops(j):
+            moved.start()
 
     def after_second(j):
         p = j % 2
-        for a in range(2):
-            low, high = parts_of(a)
-            for moved in second_hops(a, j):
-                moved.wait_recv()
-            mine[a][p, w, :, low] = total(
-                mine[a][p, w, :, low], from_x1[a][j, 0], from_y2[a][j]
-            ).astype(bf16)
-            mine[a][p, w, :, high] = total(
-                mine[a][p, w, :, high], from_y1[a][j, 0], from_x2[a][j]
-            ).astype(bf16)
-            if j == 0:
-                from_z[a][z] = mine[a][p, w]
-            else:
-                last_hop(a, z, j).start()
+        for moved in second_hops(j):
+            moved.wait_recv()
+        mine[p, w, :, low] = total(mine[p, w, :, low], from_x1[j, 0], from_y2[j]).astype(bf16)
+        mine[p, w, :, high] = total(mine[p, w, :, high], from_y1[j, 0], from_x2[j]).astype(bf16)
+        if j == 0:
+            from_z[z] = mine[p, w]
+        else:
+            last_hop(z, j).start()
 
     def all_sent(j):
-        for a in range(2):
-            for moved in first_hops(a, j) + second_hops(a, j):
-                moved.wait_send()
-            if j > 0:
-                last_hop(a, z, j).wait_send()
-
-
-    code = order[0] + 4 * order[1] + 16 * order[2] + 64 * order[3]
+        for moved in first_hops(j) + second_hops(j):
+            moved.wait_send()
+        if j > 0:
+            last_hop(z, j).wait_send()
+
+
+    code = turns[0] + 4 * turns[1] + 16 * turns[2] + 64 * turns[3]
 
     def tile_of(step):
         j = step // 2
@@ -698,6 +682,10 @@
             pltpu.make_async_copy(src, dst.at[:, cc, zj], store_sem.at[i])
             for i, (src, dst) in enumerate(pairs)
         ]
+
+    def moe_store(step):
+        zj, cc = tile_of(step)
+        return pltpu.make_async_copy(moe_tile, moe_out.at[:, cc, zj], store_sem.at[3])
 
     lanes = lax.broadcasted_iota(jnp.int32, (4 * share, 128), 1)
 
@@ -757,34 +745,39 @@
         for store in stores(step, own_tile):
             store.start()
         if own_tile:
-            for a in range(2):
-                to_sibling(a).wait_recv()
+            to_sibling().wait_recv()
+            moe_store(step - 1).wait()
         else:
 
             @pl.when(step > 0)
             def _():
-                for a in range(2):
-                    to_sibling(a).wait_send()
-
-        def put(a, cols, count, value):
+                to_sibling().wait_send()
+                moe_store(step - 1).wait()
+
+        def put(cols, count, value):
             value = value.reshape(4, share, count)
             if own_tile:
-                value = value + sibs[a][:, :, cols].astype(f32)
-                mine[a][parity, :, :, cols] = value.astype(bf16)
+                value = value + sibs[:, :, cols].astype(f32)
+                mine[parity, :, :, cols] = value.astype(bf16)
             else:
-                others[a][:, :, cols] = value.astype(bf16)
-
-        put(0, pl.ds(width, 128), 128, d_gate)
+                others[:, :, cols] = value.astype(bf16)
+
+        put(pl.ds(width, 128), 128, d_gate)
         d_rows = both[...].reshape(4 * share, 4 * hidden)
         g_rows = gated[...].reshape(4 * share, 2 * hidden)
 
         def columns(m, carried):
             cols = pl.ds(pl.multiple_of(m * 256, 256), 256)
-            put(0, cols, 256, contract_last(d_rows, w_in[cols, :]))
-            put(1, cols, 256, jnp.dot(g_rows, w_out[:, cols], preferred_element_type=f32))
+            put(cols, 256, contract_last(d_rows, w_in[cols, :]))
+            moe_tile[:, :, cols] = (
+                jnp.dot(g_rows, w_out[:, cols], preferred_element_type=f32)
+                .astype(bf16)
+                .reshape(4, share, 256)
+            )
             return carried
 
         lax.fori_loop(0, width // 256, columns, None)
+        moe_store(step).start()
 
     def before_other(j):
         if j == 0:
@@ -792,8 +785,11 @@
                 over(i, c).start()
             along(0)
             spread(0)
-            share_in(1)
+            pass_on(3)
+            pl.when((z > 0) & (z < 3))(lambda: pass_on(2))
             relay(0)
+            pass_on(1)
+            spread(1)
             keep().wait()
             for load in loads():
                 load.wait()
@@ -806,8 +802,10 @@
         sibling(j)
 
     def before_mine(j):
+        if j == 0:
+            pl.when((z == 0) | (z == 3))(lambda: pass_on(2))
         if j + 2 < 4:
-            share_in(j + 2)
+            spread(j + 2)
         if j + 1 < 4:
             relay(j + 1)
         if j >= 1:
@@ -824,8 +822,7 @@
         def _():
             pl.semaphore_wait(credit, 1)
 
-        for a in range(2):
-            to_sibling(a).start()
+        to_sibling().start()
         for k in range(4):
             pl.when(j == k)(functools.partial(before_mine, k))
         tile(2 * j + 1, True, j % 2)
@@ -838,9 +835,8 @@
 
             @pl.when(j == k)
             def _():
-                for a in range(2):
-                    for moved in first_hops(a, k):
-                        moved.start()
+                for moved in first_hops(k):
+                    moved.start()
 
         return carry
 
@@ -850,11 +846,11 @@
     after_second(3)
     for store in stores(7, True):
         store.wait()
-    for a, result in ((0, dx_own), (1, moe_own)):
-        to_sibling(a).wait_send()
-        for k in range(1, 4):
-            last_hop(a, (z + k) % 4, 1).wait_recv()
-        result[...] = total(*(from_z[a][k] for k in range(4)))
+    moe_store(7).wait()
+    to_sibling().wait_send()
+    for k in range(1, 4):
+        last_hop((z + k) % 4, 1).wait_recv()
+    dx_own[...] = total(*(from_z[k] for k in range(4)))
     all_sent(2)
     all_sent(3)
     for i in range(5):
@@ -873,18 +869,16 @@
     bf16, f32 = (jnp.bfloat16, jnp.float32)
     dma = pltpu.SemaphoreType.DMA
     anywhere, vmem = (pl.BlockSpec(memory_space=pl.ANY), pl.BlockSpec(memory_space=pltpu.VMEM))
-    wides = (width + 128, width)
-    half = width // 2
-    both = lambda shape: [pltpu.VMEM(shape(wide), bf16) for wide in wides]
+    wide, half = (width + 128, width // 2)
     return pl.pallas_call(
         functools.partial(experts_kernel, experts),
         out_shape=tuple(
             jax.ShapeDtypeStruct(blocks + (n,), bf16)
-            for n in (width, width, 2 * hidden, 4 * hidden)
-        )
-        + tuple(jax.ShapeDtypeStruct((share, wide), f32) for wide in wides),
+            for n in (width, width, 2 * hidden, 4 * hidden, width)
+        )
+        + (jax.ShapeDtypeStruct((share, wide), f32),),
         in_specs=[anywhere] * 6 + [vmem, vmem, anywhere, anywhere],
-        out_specs=(anywhere,) * 4 + (vmem, vmem),
+        out_specs=(anywhere,) * 5 + (vmem,),
         scratch_shapes=[
             pltpu.VMEM((4, share, width), bf16),
             pltpu.VMEM((width, 4 * hidden), bf16),
@@ -892,19 +886,20 @@
             pltpu.VMEM((2, 4, share, width), bf16),
             pltpu.VMEM((4, share, 2 * hidden), bf16),
             pltpu.VMEM((4, share, 4 * hidden), bf16),
-            *both(lambda wide: (4, share, wide)),
-            *both(lambda wide: (2, 4, share, wide)),
-            *both(lambda wide: (4, share, wide)),
-            *both(lambda wide: (4, 2, share, half)),
-            *both(lambda wide: (4, 2, share, wide - half)),
-            *both(lambda wide: (4, share, half)),
-            *both(lambda wide: (4, share, wide - half)),
-            *both(lambda wide: (4, share, wide)),
+            pltpu.VMEM((4, share, width), bf16),
+            pltpu.VMEM((4, share, wide), bf16),
+            pltpu.VMEM((2, 4, share, wide), bf16),
+            pltpu.VMEM((4, share, wide), bf16),
+            pltpu.VMEM((4, 2, share, half), bf16),
+            pltpu.VMEM((4, 2, share, wide - half), bf16),
+            pltpu.VMEM((4, share, half), bf16),
+            pltpu.VMEM((4, share, wide - half), bf16),
+            pltpu.VMEM((4, share, wide), bf16),
             dma,
             dma,
             dma((6,)),
             dma((6,)),
-            dma((3,)),
+            dma((4,)),
             dma((4, 2)),
             dma((4, 2)),
             dma((4, 2)),
@@ -912,15 +907,15 @@
             dma((4, 2, 5)),
             dma((5,)),
             dma((5,)),
-            dma((2,)),
-            dma((2,)),
+            dma,
+            dma,
             pltpu.SemaphoreType.REGULAR,
-            dma((2, 4, 4)),
-            dma((2, 4, 4)),
-            dma((2, 4, 2)),
-            dma((2, 4, 2)),
-            dma((2, 4)),
-            dma((2, 4)),
+            dma((4, 4)),
+            dma((4, 4)),
+            dma((4, 2)),
+            dma((4, 2)),
+            dma((4,)),
+            dma((4,)),
         ],
         compiler_params=pltpu.CompilerParams(
             collective_id=0, has_side_effects=True, vmem_limit_bytes=62 << 20
@@ -929,40 +924,186 @@
 
 
 def finish_kernel(
-    rows_ref,
+    parts_ref,
+    x_ref,
+    scale_ref,
+    gain_ref,
+    d_hidden_ref,
+    qkv_ref,
+    out_ref,
     small_ref,
     rows_out,
+    qkv_out,
+    out_out,
     small_out,
+    own_rows,
+    right_in,
+    left_in,
     sums,
     from_c,
     from_x,
     from_y,
     from_z,
+    mine,
+    sibs,
+    from_x1,
+    from_y1,
+    from_y2,
+    from_x2,
+    right_send,
+    right_recv,
+    left_send,
+    left_recv,
     send_z,
     recv_z,
     small_send,
     small_recv,
+    load_sem,
+    sib_send,
+    sib_recv,
+    one_send,
+    one_recv,
+    two_send,
+    two_recv,
 ):
     w, c, z = (lax.axis_index(a) for a in EVERYONE)
     wx, wy, wd = neighbours(w)
     dev_x, dev_y, dev_c = ((wx, c, z), (wy, c, z), (w, 1 - c, z))
+    sides = ((w, c, z + 1), (w, c, z - 1))
     order = share_order(z)
+    bf16, f32 = (jnp.bfloat16, jnp.float32)
+    half = x_ref.shape[1] // 2
+    lo, hi = (slice(0, half), slice(half, 2 * half))
+    heads = out_ref.shape[3]
+    both = ((qkv_ref, pl.ds(0, 3 * heads)), (out_ref, pl.ds(3 * heads, heads)))
+
+    def loads():
+        return [
+            pltpu.make_async_copy(ref.at[:, c], mine.at[:, :, cols], load_sem.at[i])
+            for i, (ref, cols) in enumerate(both)
+        ]
+
+    for load in loads():
+        load.start()
     barrier = pltpu.get_barrier_semaphore()
     around = [(w, c, (z + k) % 4) for k in range(1, 4)]
     for device in [dev_x, dev_y, dev_c] + around:
         pl.semaphore_signal(barrier, inc=1, device_id=device, device_id_type=MESH)
     pl.semaphore_wait(barrier, 6)
-    rows_out[z] = rows_ref[...]
-    sides = ((w, c, z + 1), (w, c, z - 1))
+
+    def remote(src, dst, send, got, device):
+        return pltpu.make_async_remote_copy(
+            src_ref=src,
+            dst_ref=dst,
+            send_sem=send,
+            recv_sem=got,
+            device_id=device,
+            device_id_type=MESH,
+        )
+
+
+    def to_right(s):
+        return remote(
+            parts_ref.at[s], right_in.at[s], right_send.at[s], right_recv.at[s], sides[0]
+        )
+
+    def to_left(s):
+        return remote(parts_ref.at[s], left_in.at[s], left_send.at[s], left_recv.at[s], sides[1])
+
+    def pass_right(s):
+        @pl.when(z < s)
+        def _():
+            @pl.when(z > 0)
+            def _():
+                to_right(s).wait_recv()
+                parts_ref[s] = (parts_ref[s].astype(f32) + right_in[s].astype(f32)).astype(bf16)
+
+            to_right(s).start()
+
+    def pass_left(s):
+        @pl.when(z > s)
+        def _():
+            @pl.when(z < 3)
+            def _():
+                to_left(s).wait_recv()
+                parts_ref[s] = (parts_ref[s].astype(f32) + left_in[s].astype(f32)).astype(bf16)
+
+            to_left(s).start()
+
+
+    def to_sibling():
+        return [
+            remote(
+                ref.at[:, 1 - c], sibs.at[:, :, cols], sib_send.at[i], sib_recv.at[i], dev_c
+            )
+            for i, (ref, cols) in enumerate(both)
+        ]
+
+    def first_hops():
+        moves = (
+            (wx, lo, from_x1.at[0], dev_x),
+            (wd, lo, from_x1.at[1], dev_x),
+            (wy, hi, from_y1.at[0], dev_y),
+            (wd, hi, from_y1.at[1], dev_y),
+        )
+        return [
+            remote(mine.at[ww, :, cols], dst, one_send.at[i], one_recv.at[i], device)
+            for i, (ww, cols, dst, device) in enumerate(moves)
+        ]
+
+    def second_hops():
+        moves = ((wy, lo, from_y2, dev_y), (wx, hi, from_x2, dev_x))
+        return [
+            remote(mine.at[ww, :, cols], dst, two_send.at[i], two_recv.at[i], device)
+            for i, (ww, cols, dst, device) in enumerate(moves)
+        ]
+
+    def add(*terms):
+        added = terms[0].astype(f32)
+        for term in terms[1:]:
+            added = added + term.astype(f32)
+        return added
+
+    def weights_first():
+        for load in loads():
+            load.wait()
+        for part in to_sibling():
+            part.wait_recv()
+        for k in range(4):
+            mine[k] = add(mine[k], sibs[k]).astype(bf16)
+        for hop in first_hops():
+            hop.start()
+
+    def weights_second():
+        for hop in first_hops():
+            hop.wait_recv()
+        mine[wy, :, lo] = add(mine[wy, :, lo], from_x1[1]).astype(bf16)
+        mine[wx, :, hi] = add(mine[wx, :, hi], from_y1[1]).astype(bf16)
+        for hop in second_hops():
+            hop.start()
+
+    def weights_last():
+        for hop in second_hops():
+            hop.wait_recv()
+        low = add(mine[w, :, lo], from_x1[0], from_y2[...])
+        high = add(mine[w, :, hi], from_y1[0], from_x2[...])
+        for k in range(4):
+            part = (low if (k + 1) * heads <= half else high)[
+                :, k * heads % half : k * heads % half + heads
+            ]
+            if k < 3:
+                qkv_out[k] = part
+            else:
+                out_out[...] = part
+
 
     def moved(j, side):
-        return pltpu.make_async_remote_copy(
-            src_ref=rows_ref if j == 0 else rows_out.at[order[j]],
-            dst_ref=rows_out.at[order[j]],
-            send_sem=send_z.at[j, side],
-            recv_sem=recv_z.at[order[j]],
-            device_id=sides[side],
-            device_id_type=MESH,
+        return remote(
+            own_rows if j == 0 else rows_out.at[order[j]],
+            rows_out.at[order[j]],
+            send_z.at[j, side],
+            recv_z.at[order[j]],
+            sides[side],
         )
 
     def onward(j):
@@ -976,101 +1117,173 @@
         moved(j, 0).wait_recv()
         along(j)
 
+
     def small(i, src, dst, device):
-        return pltpu.make_async_remote_copy(
-            src_ref=src,
-            dst_ref=dst,
-            send_sem=small_send.at[i],
-            recv_sem=small_recv.at[i],
-            device_id=device,
-            device_id_type=MESH,
-        )
-
-    def sibling(k):
+        return remote(src, dst, small_send.at[i], small_recv.at[i], device)
+
+    def small_sibling(k):
         return small(k, small_ref.at[k, 1 - c], from_c.at[k], dev_c)
 
-    def to_x(k):
+    def small_x(k):
         return small(4 + k, sums.at[(wx, wd)[k]], from_x.at[k], dev_x)
 
-    def to_y():
+    def small_y():
         return small(6, sums.at[wy], from_y, dev_y)
 
-    def to_z(target, source):
-        return pltpu.make_async_remote_copy(
-            src_ref=sums.at[w, target],
-            dst_ref=from_z.at[source],
-            send_sem=small_send.at[7 + target],
-            recv_sem=small_recv.at[7 + source],
-            device_id=(w, c, target),
-            device_id_type=MESH,
-        )
-
+    def small_z(target, source):
+        return remote(
+            sums.at[w],
+            from_z.at[source],
+            small_send.at[7 + target],
+            small_recv.at[7 + source],
+            (w, c, target),
+        )
+
+    for part in to_sibling():
+        part.start()
+    for s in range(3):
+        pass_right(3 - s)
+        pass_left(s)
+        if s == 1:
+            weights_first()
+    d_normed = parts_ref[z].astype(f32)
+    right_in[0] = jnp.zeros(right_in.shape[1:], bf16)
+    left_in[3] = jnp.zeros(left_in.shape[1:], bf16)
+
+    @pl.when(z > 0)
+    def _():
+        to_right(z).wait_recv()
+
+    @pl.when(z < 3)
+    def _():
+        to_left(z).wait_recv()
+
+    d_normed = d_normed + right_in[z].astype(f32) + left_in[z].astype(f32)
+    scale = scale_ref[...]
+    unit = x_ref[...].astype(f32) * scale
+    scaled = gain_ref[...] * d_normed
+    shift = jnp.mean(scaled * unit, axis=1, keepdims=True)
+    own_rows[...] = (d_hidden_ref[...] + scale * (scaled - unit * shift)).astype(bf16)
     along(0)
+    rows_out[z] = own_rows[...]
+    d_gain = jnp.sum(d_normed * unit, axis=0, keepdims=True)
+    for k in range(8):
+        for i in range(2):
+            at = (2 * k + i) * 128
+            small_ref[k // 2, k % 2, i : i + 1, :] = d_gain[:, at : at + 128]
     for k in range(4):
-        sibling(k).start()
+        small_sibling(k).start()
     for k in range(4):
-        sibling(k).wait_recv()
+        small_sibling(k).wait_recv()
         sums[k] = small_ref[k, c] + from_c[k]
     for k in range(2):
-        to_x(k).start()
+        small_x(k).start()
+    weights_second()
     for k in range(2):
-        to_x(k).wait_recv()
+        small_x(k).wait_recv()
     sums[w] = sums[w] + from_x[0]
     sums[wy] = sums[wy] + from_x[1]
-    to_y().start()
+    small_y().start()
     passed_on(1)
-    to_y().wait_recv()
+    small_y().wait_recv()
     sums[w] = sums[w] + from_y[...]
     for k in range(1, 4):
-        to_z((z + k) % 4, z).start()
+        small_z((z + k) % 4, z).start()
     passed_on(2)
-    added = sums[w, z]
+    weights_last()
     for k in range(1, 4):
-        to_z(z, (z + k) % 4).wait_recv()
+        small_z(z, (z + k) % 4).wait_recv()
+    from_z[z] = sums[w]
+    small_out[...] = add(*(from_z[k] for k in range(4)))
+    passed_on(3)
+    for s in range(3):
+
+        @pl.when(z < 3 - s)
+        def _():
+            to_right(3 - s).wait_send()
+
+        @pl.when(z > s)
+        def _():
+            to_left(s).wait_send()
+
+    for hop in to_sibling() + first_hops() + second_hops():
+        hop.wait_send()
+    for k in range(4):
+        small_sibling(k).wait_send()
+    for k in range(2):
+        small_x(k).wait_send()
+    small_y().wait_send()
     for k in range(1, 4):
-        added = added + from_z[(z + k) % 4]
-    small_out[...] = added
-    passed_on(3)
-    for k in range(4):
-        sibling(k).wait_send()
-    for k in range(2):
-        to_x(k).wait_send()
-    to_y().wait_send()
-    for k in range(1, 4):
-        to_z((z + k) % 4, z).wait_send()
+        small_z((z + k) % 4, z).wait_send()
     for j in range(4):
         for there, side in onward(j):
             pl.when(there)(lambda: moved(j, side).wait_send())
 
 
-def finish_call(rows, small):
+def finish_call(parts, rows, scale, gain, d_hidden, d_qkv, d_out, small):
     dma = pltpu.SemaphoreType.DMA
-    vmem = pl.BlockSpec(memory_space=pltpu.VMEM)
-    block = small.shape[3:]
-    f32 = jnp.float32
+    anywhere, vmem = (pl.BlockSpec(memory_space=pl.ANY), pl.BlockSpec(memory_space=pltpu.VMEM))
+    share, width = rows.shape
+    count, heads = d_out.shape[2:]
+    half = width // 2
+    block = small.shape[2:]
+    bf16, f32 = (jnp.bfloat16, jnp.float32)
+
+    def body(*refs):
+        ins, outs, rest = (refs[:8], refs[8:12], refs[12:])
+        parts_in, small_in = (ins[0], ins[7])
+        parts_own, small_own = rest[:2]
+        parts_own[...] = parts_in[...]
+        small_own[...] = small_in[...]
+        finish_kernel(parts_own, *ins[1:7], small_own, *outs, *rest[2:])
+
     return pl.pallas_call(
-        finish_kernel,
+        body,
         out_shape=(
-            jax.ShapeDtypeStruct((4,) + rows.shape, rows.dtype),
+            jax.ShapeDtypeStruct((4, share, width), bf16),
+            jax.ShapeDtypeStruct((3, count, heads), f32),
+            jax.ShapeDtypeStruct((count, heads), f32),
             jax.ShapeDtypeStruct(block, f32),
         ),
-        in_specs=[vmem, vmem],
-        out_specs=(vmem, vmem),
+        in_specs=[vmem, vmem, vmem, vmem, vmem, anywhere, anywhere, vmem],
+        out_specs=(vmem, vmem, vmem, vmem),
         scratch_shapes=[
-            pltpu.VMEM((4, 4) + block, f32),
-            pltpu.VMEM((4, 4) + block, f32),
-            pltpu.VMEM((2, 4) + block, f32),
+            pltpu.VMEM((4, share, width), bf16),
+            pltpu.VMEM((4, 2) + block, f32),
+            pltpu.VMEM((share, width), bf16),
+            pltpu.VMEM((4, share, width), bf16),
+            pltpu.VMEM((4, share, width), bf16),
             pltpu.VMEM((4,) + block, f32),
             pltpu.VMEM((4,) + block, f32),
+            pltpu.VMEM((2,) + block, f32),
+            pltpu.VMEM(block, f32),
+            pltpu.VMEM((4,) + block, f32),
+            pltpu.VMEM((4, count, width), bf16),
+            pltpu.VMEM((4, count, width), bf16),
+            pltpu.VMEM((2, count, half), bf16),
+            pltpu.VMEM((2, count, half), bf16),
+            pltpu.VMEM((count, half), bf16),
+            pltpu.VMEM((count, half), bf16),
+            dma((4,)),
+            dma((4,)),
+            dma((4,)),
+            dma((4,)),
             dma((4, 2)),
             dma((4,)),
             dma((11,)),
             dma((11,)),
+            dma((2,)),
+            dma((2,)),
+            dma((2,)),
+            dma((4,)),
+            dma((4,)),
+            dma((2,)),
+            dma((2,)),
         ],
         compiler_params=pltpu.CompilerParams(
-            collective_id=1, has_side_effects=True, vmem_limit_bytes=32 << 20
+            collective_id=1, has_side_effects=True, vmem_limit_bytes=48 << 20
         ),
-    )(rows, small)
+    )(parts, rows, scale, gain, d_hidden, d_qkv, d_out, small)
 
 
 def swapped(rows, flip):
@@ -1081,6 +1294,17 @@
     half = rows.shape[1] // 2
     parts = (rows, from_x, from_y, swapped(from_x[:, :half], 2), swapped(from_y[:, half:], 1))
     return [part.reshape(-1, share, part.shape[1]) for part in parts]
+
+
+def shares_around(rows):
+    z = lax.axis_index(TENSOR)
+    parts = [rows] + [
+        lax.ppermute(rows, TENSOR, [(k, (k + step) % 4) for k in range(4)]) for step in (1, 3, 2)
+    ]
+    whole = jnp.zeros((4,) + rows.shape, rows.dtype)
+    for part, step in zip(parts, (0, 1, 3, 2)):
+        whole = lax.dynamic_update_index_in_dim(whole, part, (z + 4 - step) % 4, 0)
+    return whole.reshape((-1,) + rows.shape[1:])
 
 
 def gathered(rows, axes):
@@ -1233,7 +1457,7 @@
 
     pad_experts = lambda rows: jnp.pad(rows, ((0, 0), (0, 128 - expert_total)))
     kept_rows = kept_all.transpose(0, 2, 1).reshape(-1, expert_total)
-    normed_all, grads_all, gated, d_both, d_sums, moe_own = experts_call(
+    normed_all, grads_all, gated, d_both, moe_all, d_sums = experts_call(
         normed_two,
         around,
         pad_experts(kept_rows).reshape(4, 2, 4, share, 128),
@@ -1242,11 +1466,11 @@
         expert_out,
         expert_total,
     )
-    normed_all, grads_all, gated, d_both = (
+    normed_all, grads_all, gated, d_both, moe_all = (
         rows.reshape(group_count * token_count, -1)
-        for rows in (normed_all, grads_all, gated, d_both)
-    )
-    layer_out = gathered((hidden + moe_own).astype(bf16), TENSOR).reshape(layer_in.shape)
+        for rows in (normed_all, grads_all, gated, d_both, moe_all)
+    )
+    moe_plane = scattered(moe_all, group)
     kept_own = own_rows(kept.T).astype(f32)
     probs_own = jax.nn.softmax(
         jnp.dot(normed_two, router_full, preferred_element_type=f32), axis=1
@@ -1264,13 +1488,21 @@
     d_hidden = upstream + scale_two * (
         scaled_ffn - unit_two * jnp.mean(scaled_ffn * unit_two, axis=1, keepdims=True)
     )
-    d_hidden_low = gathered(d_hidden.astype(bf16), TENSOR)
+    d_hidden_own, normed_all, grads_all, gated, d_both = lax.optimization_barrier(
+        (d_hidden.astype(bf16), normed_all, grads_all, gated, d_both)
+    )
+    d_hidden_low = shares_around(d_hidden_own)
     grad_expert_in = (
         jnp.dot(normed_all.T, d_both, preferred_element_type=f32)
         .reshape(model_width, local_experts, 2, hidden_width)
         .transpose(1, 2, 0, 3)
     )
-    d_hidden_low, grad_expert_in = lax.optimization_barrier((d_hidden_low, grad_expert_in))
+    grad_expert_out = jnp.dot(gated.T, grads_all, preferred_element_type=f32).reshape(
+        expert_out.shape
+    )
+    d_hidden_low, grad_expert_in, grad_expert_out = lax.optimization_barrier(
+        (d_hidden_low, grad_expert_in, grad_expert_out)
+    )
 
     d_attended = (
         jnp.dot(d_hidden_low, out_full, preferred_element_type=f32)
@@ -1306,7 +1538,7 @@
     d_key_hat = (d_key_rot * cosine_table + rotate_back(d_key_rot * sine_table)).reshape(
         token_count, -1
     )
-    centre = row_sums(
+    centre_own = (
         jnp.stack(
             [
                 jnp.sum(query_gain * d_query_hat * query_raw, axis=1),
@@ -1315,6 +1547,8 @@
             axis=1,
         )
     )
+    centre, moe_plane = lax.optimization_barrier((row_sums(centre_own), moe_plane))
+    moe_own = scattered(moe_plane, TENSOR).astype(f32)
     d_query_raw = (
         query_scale * query_gain * d_query_hat
         - query_raw * (query_scale**3 / model_width) * centre[:, 0:1]
@@ -1328,62 +1562,54 @@
     d_key_gain = jnp.sum(d_key_hat * key_raw * key_scale, axis=0).reshape(local_heads, head_size).T
     d_qk_gains = jnp.stack([d_query_gain, d_key_gain], axis=1)
     d_projected = jnp.concatenate([d_query_raw, d_key_raw, d_value], axis=1).astype(bf16)
-    d_projected, layer_out = lax.optimization_barrier((d_projected, layer_out))
-    d_normed_one = scattered(
-        jnp.einsum("tf,df->td", d_projected, qkv_full, preferred_element_type=f32).astype(bf16),
-        TENSOR,
-    ).astype(f32)
+    d_normed_parts = jnp.einsum(
+        "tf,df->td", d_projected, qkv_full, preferred_element_type=f32
+    ).astype(bf16)
     d_qkv = jnp.einsum("td,tf->df", normed_one, d_projected, preferred_element_type=f32)
 
-    grad_expert_out = jnp.dot(gated.T, grads_all, preferred_element_type=f32).reshape(
-        expert_out.shape
-    )
-    d_normed_one, grad_expert_out = lax.optimization_barrier((d_normed_one, grad_expert_out))
-
-    scale_own = own_rows(scale_one)
-    unit_one = residual_own * scale_own
-    d_gain_attn = jnp.sum(d_normed_one * unit_one, axis=0)
-    scaled_attn = gain_attn * d_normed_one
-    grad_in = d_hidden + scale_own * (
-        scaled_attn - unit_one * jnp.mean(scaled_attn * unit_one, axis=1, keepdims=True)
-    )
-
-    grad_qkv = (
-        scattered(d_qkv.astype(bf16), group)
-        .astype(f32)
-        .reshape(weight_rows, 3, head_width)
-    )
-    grad_out_weight = scattered(d_out_weight.astype(bf16), group).astype(f32)
+    own_slot = (jnp.arange(tensor_count) == tensor_rank).astype(f32)[None, :, None]
+    lines = lambda values: values.reshape(group_count, -1, 128)
+    small = jnp.concatenate(
+        [
+            jnp.zeros((group_count, weight_rows // 128, 128), f32),
+            lines(d_gain_ffn),
+            lines(d_router),
+            lines(d_qk_gains) * own_slot,
+        ],
+        axis=1,
+    )
+    d_normed_parts, moe_own = lax.optimization_barrier((d_normed_parts, moe_own))
+    layer_out = gathered((hidden + moe_own).astype(bf16), TENSOR).reshape(layer_in.shape)
+    grad_in, grad_qkv, grad_out_weight, small = finish_call(
+        d_normed_parts.reshape(tensor_count, share, model_width),
+        own_rows(layer_in.reshape(token_count, model_width)),
+        own_rows(scale_one),
+        gain_attn[None],
+        d_hidden,
+        d_qkv.astype(bf16).reshape(4, 2, weight_rows, -1),
+        d_out_weight.astype(bf16).reshape(4, 2, weight_rows, -1),
+        small.reshape((4, 2) + small.shape[1:]),
+    )
+    grad_in = grad_in.astype(f32).reshape(layer_in.shape)
+    grad_qkv = grad_qkv.transpose(1, 0, 2)
+    lines_of = weight_rows // 128
     gain_share = weight_rows // tensor_count
     router_share = expert_total // tensor_count
-    own_slot = (jnp.arange(tensor_count) == tensor_rank).astype(f32)[None, :, None]
-    small = jnp.concatenate(
-        [
-            jnp.stack([d_gain_attn, d_gain_ffn], axis=1).reshape(group_count, tensor_count, -1),
-            d_router.reshape(group_count, weight_rows, tensor_count, router_share)
-            .transpose(0, 2, 1, 3)
-            .reshape(group_count, tensor_count, -1),
-            d_qk_gains.reshape(group_count, 1, -1) * own_slot,
-        ],
-        axis=2,
-    )
-    small = jnp.pad(small, ((0, 0), (0, 0), (0, -small.shape[2] % 128)))
-    grad_in, small = finish_call(
-        grad_in.astype(bf16), small.reshape(4, 2, tensor_count, -1, 128)
-    )
-    grad_in = grad_in.astype(f32).reshape(layer_in.shape)
-    small = small.reshape(-1)
-    ends = (gain_share * 2, gain_share * 2 + weight_rows * router_share)
+    router_lines = weight_rows * expert_total // 128
+    part_of = lambda rows, count, axis: lax.dynamic_slice_in_dim(
+        rows, tensor_rank * count, count, axis
+    )
+    gains = small[: 2 * lines_of].reshape(2, weight_rows)
+    routers = small[2 * lines_of : 2 * lines_of + router_lines].reshape(weight_rows, expert_total)
+    qk_lines = small[2 * lines_of + router_lines :]
     return (
         layer_out,
         grad_in,
-        small[: ends[0]].reshape(gain_share, 2),
+        part_of(gains, gain_share, 1).T,
         grad_qkv,
-        small[ends[1] : ends[1] + d_qk_gains.size // group_count].reshape(
-            head_rows, 2, local_heads
-        ),
+        part_of(qk_lines, 1, 0).reshape(head_rows, 2, local_heads),
         grad_out_weight,
-        small[ends[0] : ends[1]].reshape(weight_rows, router_share),
+        part_of(routers, router_share, 1),
         grad_expert_in,
         grad_expert_out,
     )

time: 742 us -> 703 us (0.947)
  waiting for transfers between devices: 155 us -> 117 us
  other arithmetic: 51.2 us -> 42.2 us
    pallas_call x1, Pallas kernels: 37.8 us -> 114 us  [finish_call(): pl.pallas_call(body, out_shape=(jax.ShapeDtypeStruct((4, share, width), b...]
    pallas_call x1, Pallas kernels: 271 us -> 201 us  [experts_call(): pl.pallas_call(functools.partial(experts_kernel, experts), out_shape=tupl...]
    all_gather x4 -> x3, waiting for transfers between devices: 59.4 us -> 38.6 us  [gathered(): return lax.all_gather(rows, axes, axis=0, tiled=True)]
    reduce_scatter x4 -> x3, waiting for transfers between devices: 78.7 us -> 58.2 us  [scattered(): return lax.psum_scatter(rows, axes, scatter_dimension=0, tiled=True)]
    dot_general x2 -> x0, local copies, waits for them, and re-layouts: 18.3 us -> none  [the longest x1 11.8 us: per_device_dense(): jnp.dot(normed_all.T, d_both, preferred_element_type=f32)]
    dynamic_update_slice x0 -> x4, local copies, waits for them, and re-layouts: none -> 7.73 us  [shares_around(): whole = lax.dynamic_update_index_in_dim(whole, part, (z + 4 - step) % 4, 0)]
    unnamed x110 -> x107, local copies, waits for them, and re-layouts: 13.5 us -> 16.8 us
  transfers between devices with their start and end apart: 16 -> 17, of which waited for: 7 -> 7; matrix products, arithmetic and copies ran while one was open for 25% -> 27% of each run, Pallas kernels for 5% -> 16%
where the time goes in v4:
time: 703 us; the launch traced here: 694 us
  Pallas kernels  315 us (45%)
  waiting for transfers between devices  117 us (17%)
  matrix products  99.5 us (14%)
  local copies, waits for them, and re-layouts  69.1 us (10%)
  other arithmetic  42.2 us (6%)
  blocking collectives  20.9 us (3%)
  between operations  15.5 us (2%)
  starting transfers between devices  14.9 us (2%)
    pallas_call x1, Pallas kernels, experts_call(): pl.pallas_call(functools.partial(experts_kernel, experts), out_shape=tupl...  201 us
    pallas_call x1, Pallas kernels, finish_call(): pl.pallas_call(body, out_shape=(jax.ShapeDtypeStruct((4, share, width), b...  114 us
    reduce_scatter x3, waiting for transfers between devices, scattered(): return lax.psum_scatter(rows, axes, scatter_dimension=0, tiled=True)  58.2 us
    all_gather x3, waiting for transfers between devices, gathered(): return lax.all_gather(rows, axes, axis=0, tiled=True)  38.6 us
    dot_general x1, matrix products, per_device_dense(): jnp.dot(normed_all.T, d_both, preferred_element_type=f32)  26.5 us
    psum x2, blocking collectives, row_sums(): return lax.psum(partial_rows, TENSOR)  20.9 us
    ppermute x4, waiting for transfers between devices, swapped(): return lax.ppermute(rows, WEIGHTS, [(k, k ^ flip) for k in range(4)])  17.6 us
    unnamed x107, local copies, waits for them, and re-layouts  16.8 us
  transfers between devices with their start and end apart: 17, of which 7 were waited for; matrix products, arithmetic and copies ran while one was open for 27% of the time, Pallas kernels for 16%

profile of v4, /device:TPU:0, one launch (start us, length us, event | category | flops | bytes accessed | tf_op | source)
XLA Modules:
  0.0 694.1 jit_solution(8904142336278037703)
XLA Ops:
  9.8 3.4 concatenate.72
  24.2 38.6 %all-gather.4.cloned.1.call-done = bf16[2048,1539]{0,1:T(8,128)(2,1)} async-done(((bf16[256,1539]{0,1:T(8,128)(2,1)}), bf16[2048,1539]{0,1:T(8,128)(2,1)}) %all-gather.4.cloned.1.call-update) | async-done | bytes 6303760 | tf_op jit(solution)/shard_map/all_gather | solution.py:1311
  64.4 6.3 fusion.4
  79.5 11.7 %psum.14 = f32[512,2]{0,1:T(2,128)S(1)} all-reduce(f32[512,2]{0,1:T(2,128)S(1)} %pad_maximum_fusion.6), channel_id=1, replica_groups=mesh['weights'=4,'context'=2,'tensor'=4] {'tensor'}, use_global_device_ids=true, to_apply=%region_3.4 | all-reduce | flops 1024 | bytes 8192 | tf_op jit(solution)/shard_map/psum | solution.py:69
  103.1 3.5 fusion.77
  109.9 3.1 fusion.25
  113.0 17.4 %collective-permute-done = bf16[512,2048]{1,0:T(8,128)(2,1)} collective-permute-done((bf16[512,2048]{1,0:T(8,128)(2,1)}, bf16[512,2048]{1,0:T(8,128)(2,1)}, u32[]{:S(2)}, u32[]{:S(2)}) %collective-permute-start) | collective-permute-done | bytes 2097184 | tf_op jit(solution)/shard_map/ppermute | solution.py:1290
  130.6 4.2 convolution_convert_fusion.2
  134.9 2.4 slice.132
  141.6 2.5 convert_element_type.141
  148.5 30.4 %reduce-scatter.4.cloned.1.call-done = bf16[128,2048]{1,0:T(8,128)(2,1)} async-done(((bf16[512,2048]{1,0:T(8,128)(2,1)}), bf16[128,2048]{1,0:T(8,128)(2,1)}) %reduce-scatter.4.cloned.1.call-update) | async-done | bytes 524304 | tf_op jit(solution)/shard_map/reduce_scatter | solution.py:1315
  181.5 201.0 %shard_map.187 = (bf16[4,2,4,128,2048]{4,3,2,1,0:T(8,128)(2,1)}, bf16[4,2,4,128,2048]{4,3,2,1,0:T(8,128)(2,1)}, bf16[4,2,4,128,512]{4,3,2,1,0:T(8,128)(2,1)}, bf...) custom-call(bf16[128,2048]{1,0:T(8,128)(2,1)} %multiply_convert_fusion.1.x_ref, ...), custom_call_target="tpu_custom_call" | custom-call | tf_op jit(solution)/shard_map/pallas_call | solution.py:873
  391.7 3.8 collective-permute-start.7
  395.5 26.5 %fusion.80 = f32[2048,1024]{0,1:T(8,128)} fusion(bf16[4096,2048]{1,0:T(8,128)(2,1)} %bitcast.240, bf16[4096,1024]{1,0:T(8,128)(2,1)} %bitcast.241), kind=kOutput, calls=%fused_computation.166 | convolution fusion | flops 17179869184 | bytes 33554432 | tf_op jit(solution)/shard_map/dot_general | solution.py:1496
  422.0 14.3 %fusion.81 = f32[512,2048]{1,0:T(8,128)} fusion(bf16[4096,512]{1,0:T(8,128)(2,1)S(1)} %bitcast.242, bf16[4096,2048]{1,0:T(8,128)(2,1)} %bitcast.239), kind=kOutput, calls=%fused_computation.167 | convolution fusion | flops 8589934592 | bytes 25165824 | tf_op jit(solution)/shard_map/dot_general | solution.py:1500
  439.8 8.9 %copy.153 = f32[2048,2,2,256]{3,0,2,1:T(8,128)} copy(f32[2048,2,2,256]{0,3,2,1:T(8,128)} %bitcast.192) | data formatting | bytes 16777216 | tf_op jit(solution)/shard_map/reshape | solution.py:1497
  454.6 3.0 fusion.22
  457.6 5.2 multiply_reduce_fusion
  470.1 3.1 broadcast_multiply_fusion
  474.6 2.6 copy.175
  482.5 9.2 %psum.15 = f32[512,2]{0,1:T(2,128)S(1)} all-reduce(f32[512,2]{0,1:T(2,128)S(1)} %pad_maximum_fusion.7), channel_id=1, replica_groups=mesh['weights'=4,'context'=2,'tensor'=4] {'tensor'}, use_global_device_ids=true, to_apply=%region_17.18 | all-reduce | flops 1024 | bytes 8192 | tf_op jit(solution)/shard_map/psum | solution.py:69
  491.7 5.0 reduce-scatter.6.cloned.1.call-done
  496.8 5.2 fusion.19
  503.4 2.5 collective-permute-done.10
  508.9 2.8 subtract_convert_fusion
  512.7 7.4 %fusion.13 = bf16[512,2048]{1,0:T(8,128)(2,1)} fusion(bf16[2048,1539]{0,1:T(8,128)(2,1)} %all-gather.4.cloned.1.call-done, bf16[512,512]{1,0:T(8,128)(2,1)S(1)} %copy-done.31, bf16[512,512]{1,0:T(8,128)(2,1)S(1)} %get-tuple-element.120, bf16[512,512]{1,0:T(8,128)(2,1)S(1)} %get-tuple-element.119), kind=kOutput, calls=%fused_computation.22 | convolution fusion | flops 3226992640 | bytes 9961472 | tf_op jit(solution)/shard_map/tf,df->td/dot_general | solution.py:1565
  520.1 22.8 %reduce-scatter.8.cloned.1.call-done = bf16[128,2048]{1,0:T(8,128)(2,1)} async-done(((bf16[512,2048]{1,0:T(8,128)(2,1)}), bf16[128,2048]{1,0:T(8,128)(2,1)}) %reduce-scatter.8.cloned.1.call-update) | async-done | bytes 524304 | tf_op jit(solution)/shard_map/reduce_scatter | solution.py:1315
  548.7 4.5 convolution_convert_fusion.1
  553.7 7.0 %convolution_convert_fusion = bf16[2048,1536]{1,0:T(8,128)(2,1)} fusion(bf16[512,512]{1,0:T(8,128)(2,1)} %copy.176, bf16[512,512]{1,0:T(8,128)(2,1)} %copy-done.30, bf16[512,512]{1,0:T(8,128)(2,1)} %copy-done.29, f32[2048]{0:T(1024)S(1)} %bitcast.235, f32[512]{0:T(512)S(1)} %copy-done.43, bf16[1,512,2048]{2,1,0:T(8,128)(2,1)S(1)} %copy-done.10), kind=kOutput, calls=%fused_computation.7 | convolution fusion | flops 3233284096 | bytes 9971712 | tf_op jit(solution)/shard_map/td,tf->df/dot_general | solution.py:1568
  560.7 113.9 %shard_map.188 = (bf16[4,128,2048]{2,1,0:T(8,128)(2,1)S(1)}, f32[3,256,512]{2,1,0:T(8,128)S(1)}, f32[256,512]{1,0:T(8,128)S(1)}, f32[40,128]{1,0:T(8,128)S(1)}) custom-call(bf16[4,128,2048]{2,1,0:T(8,128)(2,1)} %bitcast.200, bf16[128,2048]{1,0:T(8,128)(2,1)S(1)} %copy-done, f32[128,1]{1,0:T(8,128)S(1)} %copy.165.refs_2_, ...), custom_call_target="tpu_custom_call" | custom-call | tf_op jit(solution)/shard_map/pallas_call | solution.py:1240
  679.0 2.5 bitcast_convert_fusion
  681.5 3.3 copy.198
  (252 shorter events, 100.5 us)
Async XLA Ops:
  7.2 6.5 copy-start.36
  7.2 7.5 %copy-start.37 = (s32[1,512,8]{1,2,0:T(8,128)S(1)}, s32[1,512,8]{1,2,0:T(8,128)}, u32[]{:S(2)}) copy-start(s32[1,512,8]{1,2,0:T(8,128)} %param.22) | copy-start | bytes 49156
  7.2 10.3 %copy-start.38 = (bf16[256,16]{0,1:T(8,128)(2,1)S(1)}, bf16[256,16]{0,1:T(8,128)(2,1)}, u32[]{:S(2)}) copy-start(bf16[256,16]{0,1:T(8,128)(2,1)} %param.17) | copy-start | bytes 24580
  7.2 10.5 %copy-start.35 = (bf16[256,512]{1,0:T(8,128)(2,1)S(1)}, bf16[256,512]{1,0:T(8,128)(2,1)}, u32[]{:S(2)}) copy-start(bf16[256,512]{1,0:T(8,128)(2,1)} %param.16) | copy-start | bytes 786436
  7.2 11.5 %copy-start.8 = (bf16[1,512,2048]{2,1,0:T(8,128)(2,1)S(1)}, bf16[1,512,2048]{2,1,0:T(8,128)(2,1)}, u32[]{:S(2)}) copy-start(bf16[1,512,2048]{2,1,0:T(8,128)(2,1)} %param.12) | copy-start | bytes 6291460
  7.2 55.6 %all-gather.4.cloned.1.call-start = ((), (), s32[]{:S(2)}) async-start(), calls=%async_computation.3 | async-start | bytes 7114752 | tf_op jit(solution)/shard_map/all_gather | solution.py:1311
  13.2 117.5 %all-gather.6.cloned.1.call-start = ((), (), s32[]{:S(2)}) async-start(), calls=%async_computation.4 | async-start | bytes 2949120 | tf_op jit(solution)/shard_map/all_gather | solution.py:1311
  14.7 8.1 %copy-start.41 = (s32[1,1024]{1,0:T(1,128)S(1)}, s32[1,1024]{1,0:T(1,128)}, u32[]{:S(2)}) copy-start(s32[1,1024]{1,0:T(1,128)} %param.21) | copy-start | bytes 12292
  18.5 160.3 %reduce-scatter.4.cloned.1.call-start = ((), (), s32[]{:S(2)}) async-start(), calls=%async_computation.5 | async-start | bytes 2621440 | tf_op jit(solution)/shard_map/reduce_scatter | solution.py:1315
  19.2 51.5 %copy-start.42 = (f32[512]{0:T(512)}, f32[512]{0:T(512)S(1)}, u32[]{:S(2)}) copy-start(f32[512]{0:T(512)S(1)} %add_rsqrt_fusion) | copy-start | bytes 6148
  21.2 43.3 %copy-start.16 = (f32[512,128]{1,0:T(8,128)}, f32[512,128]{1,0:T(8,128)S(1)}, u32[]{:S(2)}) copy-start(f32[512,128]{1,0:T(8,128)S(1)} %get-tuple-element.133) | copy-start | bytes 786436
  70.7 22.0 %copy-start.6 = (f32[512,1536]{1,0:T(8,128)}, f32[512,1536]{1,0:T(8,128)S(1)}, u32[]{:S(2)}) copy-start(f32[512,1536]{1,0:T(8,128)S(1)} %fusion.4) | copy-start | bytes 9437188
  72.6 57.8 %collective-permute-start = (bf16[512,2048]{1,0:T(8,128)(2,1)}, bf16[512,2048]{1,0:T(8,128)(2,1)}, u32[]{:S(2)}, u32[]{:S(2)}) collective-permute-start(bf16[512,2048]{1,0:T(8,128)(2,1)} %bitcast.2), channel_id=1, source_target_pairs={{0,8},{8,0},{16,24},{24,16},{1,9},{9,1},{17,25},{25,17},{2,10},{10... | collective-permute-start | bytes 6291464 | tf_op jit(solution)/shard_map/ppermute | solution.py:1290
  74.1 56.5 %collective-permute-start.1 = (bf16[512,2048]{1,0:T(8,128)(2,1)}, bf16[512,2048]{1,0:T(8,128)(2,1)}, u32[]{:S(2)}, u32[]{:S(2)}) collective-permute-start(bf16[512,2048]{1,0:T(8,128)(2,1)} %bitcast.2), channel_id=1, source_target_pairs={{0,16},{8,24},{16,0},{24,8},{1,17},{9,25},{17,1},{25,9},{2,18},{10... | collective-permute-start | bytes 6291464 | tf_op jit(solution)/shard_map/ppermute | solution.py:1290
  96.4 6.7 collective-permute-start.3
  100.0 8.4 %collective-permute-start.2 = (bf16[1,512,4,128]{1,3,2,0:T(8,128)(2,1)}, bf16[1,512,4,128]{1,3,2,0:T(8,128)(2,1)S(1)}, u32[]{:S(2)}, u32[]{:S(2)}) collective-permute-start(bf16[1,512,4,128]{1,3,2,0:T(8,128)(2,1)} %bitcast.86), channel_id=1, source_target_pairs={{0,4},{1,5},{2,6},{3,7},{8,12},{9,13},{10,14},{11,15},{16,20},{17,... | collective-permute-start | bytes 1572872 | tf_op jit(solution)/shard_map/ppermute | solution.py:25
  113.0 21.9 %copy-start.45 = (bf16[4,128,512]{2,1,0:T(8,128)(2,1)}, bf16[4,128,512]{2,1,0:T(8,128)(2,1)S(1)}, u32[]{:S(2)}) copy-start(bf16[4,128,512]{2,1,0:T(8,128)(2,1)S(1)} %fusion.25) | copy-start | bytes 1572868
  134.8 6.8 copy-start.9
  134.9 361.9 %reduce-scatter.6.cloned.1.call-start = ((), (), s32[]{:S(2)}) async-start(), calls=%async_computation.6 | async-start | bytes 18874368 | tf_op jit(solution)/shard_map/reduce_scatter | solution.py:1315
  137.3 44.1 %collective-permute-start.4 = (bf16[512,1024]{1,0:T(8,128)(2,1)}, bf16[512,1024]{1,0:T(8,128)(2,1)}, u32[]{:S(2)}, u32[]{:S(2)}) collective-permute-start(bf16[512,1024]{1,0:T(8,128)(2,1)} %slice.132), channel_id=1, source_target_pairs={{0,16},{8,24},{16,0},{24,8},{1,17},{9,25},{17,1},{25,9},{2,18},{10... | collective-permute-start | bytes 3145736 | tf_op jit(solution)/shard_map/ppermute | solution.py:1290
  140.6 40.9 %collective-permute-start.5 = (bf16[512,1024]{1,0:T(8,128)(2,1)}, bf16[512,1024]{1,0:T(8,128)(2,1)}, u32[]{:S(2)}, u32[]{:S(2)}) collective-permute-start(bf16[512,1024]{1,0:T(8,128)(2,1)} %slice.133), channel_id=1, source_target_pairs={{0,8},{8,0},{16,24},{24,16},{1,9},{9,1},{17,25},{25,17},{2,10},{10... | collective-permute-start | bytes 3145736 | tf_op jit(solution)/shard_map/ppermute | solution.py:1290
  382.5 160.4 %reduce-scatter.8.cloned.1.call-start = ((), (), s32[]{:S(2)}) async-start(), calls=%async_computation.7 | async-start | bytes 2621440 | tf_op jit(solution)/shard_map/reduce_scatter | solution.py:1315
  391.7 30.3 %copy-start.44 = (bf16[4,2,4,128,512]{4,3,2,1,0:T(8,128)(2,1)S(1)}, bf16[4,2,4,128,512]{4,3,2,1,0:T(8,128)(2,1)}, u32[]{:S(2)}) copy-start(bf16[4,2,4,128,512]{4,3,2,1,0:T(8,128)(2,1)} %get-tuple-element.44) | copy-start | bytes 12582916
  391.7 57.0 %collective-permute-start.6 = (bf16[128,2048]{1,0:T(8,128)(2,1)}, bf16[128,2048]{1,0:T(8,128)(2,1)}, u32[]{:S(2)}, u32[]{:S(2)}) collective-permute-start(bf16[128,2048]{1,0:T(8,128)(2,1)} %get-tuple-element.46), channel_id=1, source_target_pairs={{0,1},{1,2},{2,3},{3,0},{4,5},{5,6},{6,7},{7,4},{8,9},{9,10},{10,1... | collective-permute-start | bytes 1572872 | tf_op jit(solution)/shard_map/ppermute | solution.py:1302
  391.7 59.1 %collective-permute-start.7 = (bf16[128,2048]{1,0:T(8,128)(2,1)}, bf16[128,2048]{1,0:T(8,128)(2,1)}, u32[]{:S(2)}, u32[]{:S(2)}) collective-permute-start(bf16[128,2048]{1,0:T(8,128)(2,1)} %get-tuple-element.46), channel_id=1, source_target_pairs={{0,3},{1,0},{2,1},{3,2},{4,7},{5,4},{6,5},{7,6},{8,11},{9,8},{10,9... | collective-permute-start | bytes 1572872 | tf_op jit(solution)/shard_map/ppermute | solution.py:1302
  395.5 57.2 %collective-permute-start.8 = (bf16[128,2048]{1,0:T(8,128)(2,1)}, bf16[128,2048]{1,0:T(8,128)(2,1)}, u32[]{:S(2)}, u32[]{:S(2)}) collective-permute-start(bf16[128,2048]{1,0:T(8,128)(2,1)} %get-tuple-element.46), channel_id=1, source_target_pairs={{0,2},{1,3},{2,0},{3,1},{4,6},{5,7},{6,4},{7,5},{8,10},{9,11},{10,... | collective-permute-start | bytes 1572872 | tf_op jit(solution)/shard_map/ppermute | solution.py:1302
  457.6 6.4 slice-start.1
  468.7 8.5 %collective-permute-start.9 = (bf16[1,512,4,128]{3,1,2,0:T(8,128)(2,1)}, bf16[1,512,4,128]{3,1,2,0:T(8,128)(2,1)}, u32[]{:S(2)}, u32[]{:S(2)}) collective-permute-start(bf16[1,512,4,128]{3,1,2,0:T(8,128)(2,1)} %slice.243), channel_id=1, source_target_pairs={{4,0},{5,1},{6,2},{7,3},{12,8},{13,9},{14,10},{15,11},{20,16},{21,... | collective-permute-start | bytes 1572872 | tf_op jit(solution)/shard_map/ppermute | solution.py:25
  496.8 184.8 %all-gather.8.cloned.1.call-start = ((), (), s32[]{:S(2)}) async-start(), calls=%async_computation.8 | async-start | bytes 2621440 | tf_op jit(solution)/shard_map/all_gather | solution.py:1311
  502.1 3.8 collective-permute-start.10
  520.1 24.9 %copy-start.43 = (f32[512]{0:T(512)S(1)}, f32[512]{0:T(512)}, u32[]{:S(2)}) copy-start(f32[512]{0:T(512)} %copy-done.42) | copy-start | bytes 6148
  553.7 7.0 %copy-start = (bf16[128,2048]{1,0:T(8,128)(2,1)S(1)}, bf16[128,2048]{1,0:T(8,128)(2,1)}, u32[]{:S(2)}) copy-start(bf16[128,2048]{1,0:T(8,128)(2,1)} %dynamic-slice_bitcast_fusion.refs_1_) | copy-start | bytes 1572868
  (34 other events, 110.0 us)
Sparse Core Ops, SparseCore 0:
  13.3 49.5 all-gather.3
  64.7 40.6 all-gather.5
  135.0 43.8 reduce-scatter.3
  382.6 114.0 reduce-scatter.5
  499.0 43.8 reduce-scatter.7
  545.1 63.3 all-gather.7

commit v5 on v4

--- a/solution.py
+++ b/solution.py
@@ -390,8 +390,10 @@
     experts,
     x_ref,
     grad_own,
-    grad_x,
-    grad_y,
+    grad_x_low,
+    grad_x_high,
+    grad_y_low,
+    grad_y_high,
     grad_low,
     grad_high,
     kept_ref,
@@ -476,8 +478,10 @@
 
     grad_parts = (
         (grad_own, w, None),
-        (grad_x, wx, None),
-        (grad_y, wy, None),
+        (grad_x_low, wx, lo),
+        (grad_x_high, wx, hi),
+        (grad_y_low, wy, lo),
+        (grad_y_high, wy, hi),
         (grad_low, wd, lo),
         (grad_high, wd, hi),
     )
@@ -661,7 +665,7 @@
 
     def other_grads(step):
         zj, cc = tile_of(step)
-        return pltpu.make_async_copy(grads_out.at[:, cc, zj], grads.at[0], grads_sem.at[5])
+        return pltpu.make_async_copy(grads_out.at[:, cc, zj], grads.at[0], grads_sem.at[7])
 
     def my_grads(step):
         zj, cc = tile_of(step)
@@ -781,7 +785,7 @@
 
     def before_other(j):
         if j == 0:
-            for i in range(5):
+            for i in range(7):
                 over(i, c).start()
             along(0)
             spread(0)
@@ -793,7 +797,7 @@
             keep().wait()
             for load in loads():
                 load.wait()
-            for i in range(5):
+            for i in range(7):
                 over(i, 1 - c).wait_recv()
             other_grads(0).start()
         if j >= 2:
@@ -853,7 +857,7 @@
     dx_own[...] = total(*(from_z[k] for k in range(4)))
     all_sent(2)
     all_sent(3)
-    for i in range(5):
+    for i in range(7):
         over(i, c).wait_send()
     for chunk, cols, slot, sem, device in sent:
         copy(view(chunk, cols), chunk, cols, slot, sem, device).wait_send()
@@ -877,7 +881,7 @@
             for n in (width, width, 2 * hidden, 4 * hidden, width)
         )
         + (jax.ShapeDtypeStruct((share, wide), f32),),
-        in_specs=[anywhere] * 6 + [vmem, vmem, anywhere, anywhere],
+        in_specs=[anywhere] * 8 + [vmem, vmem, anywhere, anywhere],
         out_specs=(anywhere,) * 5 + (vmem,),
         scratch_shapes=[
             pltpu.VMEM((4, share, width), bf16),
@@ -898,15 +902,15 @@
             dma,
             dma,
             dma((6,)),
-            dma((6,)),
+            dma((8,)),
             dma((4,)),
             dma((4, 2)),
             dma((4, 2)),
             dma((4, 2)),
             dma((4, 5)),
             dma((4, 2, 5)),
-            dma((5,)),
-            dma((5,)),
+            dma((7,)),
+            dma((7,)),
             dma,
             dma,
             pltpu.SemaphoreType.REGULAR,
@@ -1290,9 +1294,17 @@
     return lax.ppermute(rows, WEIGHTS, [(k, k ^ flip) for k in range(4)])
 
 
-def grads_around(rows, from_x, from_y, share):
+def grads_around(rows, x_low, y_high, share):
     half = rows.shape[1] // 2
-    parts = (rows, from_x, from_y, swapped(from_x[:, :half], 2), swapped(from_y[:, half:], 1))
+    parts = (
+        rows,
+        x_low,
+        swapped(rows[:, half:], 1),
+        swapped(rows[:, :half], 2),
+        y_high,
+        swapped(x_low, 2),
+        swapped(y_high, 1),
+    )
     return [part.reshape(-1, share, part.shape[1]) for part in parts]
 
 
@@ -1369,7 +1381,8 @@
     )
     own_grads = grad_out.reshape(token_count, model_width)
     front, own_grads = lax.optimization_barrier((front, own_grads))
-    from_x, from_y = (swapped(own_grads, 1), swapped(own_grads, 2))
+    half = model_width // 2
+    x_low, y_high = (swapped(own_grads[:, :half], 1), swapped(own_grads[:, half:], 2))
     back_small = jnp.concatenate(
         [router, fit_rows(kept.astype(bf16), weight_rows)], axis=1
     )
@@ -1443,8 +1456,8 @@
     attn_probs = (exponent / row_total).astype(bf16)
     attended = jnp.einsum(BY_QUERY, attn_probs, all_values, preferred_element_type=f32)
     attended_low = attended.reshape(token_count, -1).astype(bf16)
-    from_x, from_y, attended_low = lax.optimization_barrier((from_x, from_y, attended_low))
-    around = grads_around(own_grads, from_x, from_y, share)
+    x_low, y_high, attended_low = lax.optimization_barrier((x_low, y_high, attended_low))
+    around = grads_around(own_grads, x_low, y_high, share)
     attn_partial = jnp.einsum("tf,df->td", attended_low, out_full, preferred_element_type=f32)
 
     own_rows = lambda rows: lax.dynamic_slice_in_dim(rows, tensor_rank * share, share, 0)
@@ -1578,7 +1591,9 @@
         ],
         axis=1,
     )
-    d_normed_parts, moe_own = lax.optimization_barrier((d_normed_parts, moe_own))
+    d_normed_parts, d_qkv, d_out_weight, moe_own = lax.optimization_barrier(
+        (d_normed_parts, d_qkv.astype(bf16), d_out_weight.astype(bf16), moe_own)
+    )
     layer_out = gathered((hidden + moe_own).astype(bf16), TENSOR).reshape(layer_in.shape)
     grad_in, grad_qkv, grad_out_weight, small = finish_call(
         d_normed_parts.reshape(tensor_count, share, model_width),
@@ -1586,8 +1601,8 @@
         own_rows(scale_one),
         gain_attn[None],
         d_hidden,
-        d_qkv.astype(bf16).reshape(4, 2, weight_rows, -1),
-        d_out_weight.astype(bf16).reshape(4, 2, weight_rows, -1),
+        d_qkv.reshape(4, 2, weight_rows, -1),
+        d_out_weight.reshape(4, 2, weight_rows, -1),
         small.reshape((4, 2) + small.shape[1:]),
     )
     grad_in = grad_in.astype(f32).reshape(layer_in.shape)

time: 703 us -> 693 us (0.986)
  waiting for transfers between devices: 117 us -> 104 us
    pallas_call x1, Pallas kernels: 114 us -> 123 us  [finish_call(): pl.pallas_call(body, out_shape=(jax.ShapeDtypeStruct((4, share, width), b...]
    reduce_scatter x3, waiting for transfers between devices: 58.2 us -> 51 us  [scattered(): return lax.psum_scatter(rows, axes, scatter_dimension=0, tiled=True)]
    ppermute x4 -> x6, waiting for transfers between devices: 17.6 us -> 14 us  [swapped(): return lax.ppermute(rows, WEIGHTS, [(k, k ^ flip) for k in range(4)])]
    unnamed x107 -> x109, local copies, waits for them, and re-layouts: 16.8 us -> 16.3 us
  transfers between devices with their start and end apart: 17 -> 19, of which waited for: 7 -> 7; matrix products, arithmetic and copies ran while one was open for 27% -> 27% of each run, Pallas kernels for 16% -> 18%
where the time goes in v5:
time: 693 us; the launch traced here: 685 us
  Pallas kernels  322 us (46%)
  waiting for transfers between devices  104 us (15%)
  matrix products  97.7 us (14%)
  local copies, waits for them, and re-layouts  67.9 us (10%)
  other arithmetic  40.7 us (6%)
  blocking collectives  20.9 us (3%)
  starting transfers between devices  16.8 us (2%)
  between operations  15.5 us (2%)
    pallas_call x1, Pallas kernels, experts_call(): pl.pallas_call(functools.partial(experts_kernel, experts), out_shape=tupl...  199 us
    pallas_call x1, Pallas kernels, finish_call(): pl.pallas_call(body, out_shape=(jax.ShapeDtypeStruct((4, share, width), b...  123 us
    reduce_scatter x3, waiting for transfers between devices, scattered(): return lax.psum_scatter(rows, axes, scatter_dimension=0, tiled=True)  51 us
    all_gather x3, waiting for transfers between devices, gathered(): return lax.all_gather(rows, axes, axis=0, tiled=True)  38.6 us
    dot_general x1, matrix products, per_device_dense(): jnp.dot(normed_all.T, d_both, preferred_element_type=f32)  26.6 us
    psum x2, blocking collectives, row_sums(): return lax.psum(partial_rows, TENSOR)  20.9 us
    unnamed x109, local copies, waits for them, and re-layouts  16.3 us
    dot_general x1, matrix products, per_device_dense(): jnp.dot(gated.T, grads_all, preferred_element_type=f32)  14.3 us
  transfers between devices with their start and end apart: 19, of which 7 were waited for; matrix products, arithmetic and copies ran while one was open for 27% of the time, Pallas kernels for 18%

profile of v5, /device:TPU:0, one launch (start us, length us, event | category | flops | bytes accessed | tf_op | source)
XLA Modules:
  0.0 685.2 jit_solution(11444780080632587076)
XLA Ops:
  9.8 3.4 concatenate.72
  24.2 38.6 %all-gather.4.cloned.1.call-done = bf16[2048,1539]{0,1:T(8,128)(2,1)} async-done(((bf16[256,1539]{0,1:T(8,128)(2,1)}), bf16[2048,1539]{0,1:T(8,128)(2,1)}) %all-gather.4.cloned.1.call-update) | async-done | bytes 6303760 | tf_op jit(solution)/shard_map/all_gather | solution.py:1323
  64.4 6.3 fusion.4
  71.0 12.3 %psum.14 = f32[512,2]{0,1:T(2,128)} all-reduce(f32[512,2]{0,1:T(2,128)S(1)} %pad_maximum_fusion.6), channel_id=1, replica_groups=mesh['weights'=4,'context'=2,'tensor'=4] {'tensor'}, use_global_device_ids=true, to_apply=%region_3.4 | all-reduce | flops 1024 | bytes 8192 | tf_op jit(solution)/shard_map/psum | solution.py:69
  94.3 2.1 collective-permute-start.3
  105.7 3.5 fusion.78
  112.5 2.1 fusion.25
  114.6 11.3 %collective-permute-done = bf16[512,1024]{1,0:T(8,128)(2,1)} collective-permute-done((bf16[512,1024]{1,0:T(8,128)(2,1)}, bf16[512,1024]{1,0:T(8,128)(2,1)}, u32[]{:S(2)}, u32[]{:S(2)}) %collective-permute-start) | collective-permute-done | bytes 1048608 | tf_op jit(solution)/shard_map/ppermute | solution.py:1294
  127.1 4.2 convolution_convert_fusion.2
  135.6 2.5 convert_element_type.141
  142.5 29.3 %reduce-scatter.4.cloned.1.call-done = bf16[128,2048]{1,0:T(8,128)(2,1)} async-done(((bf16[512,2048]{1,0:T(8,128)(2,1)}), bf16[128,2048]{1,0:T(8,128)(2,1)}) %reduce-scatter.4.cloned.1.call-update) | async-done | bytes 524304 | tf_op jit(solution)/shard_map/reduce_scatter | solution.py:1327
  175.8 199.1 %shard_map.187 = (bf16[4,2,4,128,2048]{4,3,2,1,0:T(8,128)(2,1)}, bf16[4,2,4,128,2048]{4,3,2,1,0:T(8,128)(2,1)}, bf16[4,2,4,128,512]{4,3,2,1,0:T(8,128)(2,1)}, bf...) custom-call(bf16[128,2048]{1,0:T(8,128)(2,1)} %multiply_convert_fusion.1.x_ref, ...), custom_call_target="tpu_custom_call" | custom-call | tf_op jit(solution)/shard_map/pallas_call | solution.py:877
  381.8 2.3 fusion.70
  384.1 3.8 collective-permute-start.9
  387.9 26.6 %fusion.81 = f32[2048,1024]{0,1:T(8,128)} fusion(bf16[4096,2048]{1,0:T(8,128)(2,1)} %bitcast.247, bf16[4096,1024]{1,0:T(8,128)(2,1)} %bitcast.248), kind=kOutput, calls=%fused_computation.167 | convolution fusion | flops 17179869184 | bytes 33554432 | tf_op jit(solution)/shard_map/dot_general | solution.py:1509
  414.5 14.3 %fusion.82 = f32[512,2048]{1,0:T(8,128)} fusion(bf16[4096,512]{1,0:T(8,128)(2,1)S(1)} %bitcast.249, bf16[4096,2048]{1,0:T(8,128)(2,1)} %bitcast.246), kind=kOutput, calls=%fused_computation.168 | convolution fusion | flops 8589934592 | bytes 25165824 | tf_op jit(solution)/shard_map/dot_general | solution.py:1513
  432.3 9.0 %copy.153 = f32[2048,2,2,256]{3,0,2,1:T(8,128)} copy(f32[2048,2,2,256]{0,3,2,1:T(8,128)} %bitcast.196) | data formatting | bytes 16777216 | tf_op jit(solution)/shard_map/reshape | solution.py:1510
  447.2 3.0 fusion.22
  450.2 5.6 multiply_reduce_fusion
  462.6 3.0 broadcast_multiply_fusion
  467.0 2.6 copy.175
  475.0 8.6 %psum.15 = f32[512,2]{0,1:T(2,128)S(1)} all-reduce(f32[512,2]{0,1:T(2,128)S(1)} %pad_maximum_fusion.7), channel_id=1, replica_groups=mesh['weights'=4,'context'=2,'tensor'=4] {'tensor'}, use_global_device_ids=true, to_apply=%region_17.18 | all-reduce | flops 1024 | bytes 8192 | tf_op jit(solution)/shard_map/psum | solution.py:69
  483.6 6.0 reduce-scatter.6.cloned.1.call-done
  489.7 5.2 fusion.19
  496.3 4.3 convolution_convert_fusion.1
  503.6 3.0 subtract_convert_fusion
  506.7 5.6 convolution_convert_fusion
  512.3 7.6 %fusion.13 = bf16[512,2048]{1,0:T(8,128)(2,1)} fusion(bf16[2048,1539]{0,1:T(8,128)(2,1)} %all-gather.4.cloned.1.call-done, bf16[512,512]{1,0:T(8,128)(2,1)S(1)} %copy-done.32, bf16[512,512]{1,0:T(8,128)(2,1)S(1)} %get-tuple-element.124, bf16[512,512]{1,0:T(8,128)(2,1)S(1)} %get-tuple-element.123), kind=kOutput, calls=%fused_computation.22 | convolution fusion | flops 3226992640 | bytes 9961472 | tf_op jit(solution)/shard_map/tf,df->td/dot_general | solution.py:1578
  519.9 15.8 %reduce-scatter.8.cloned.1.call-done = bf16[128,2048]{1,0:T(8,128)(2,1)} async-done(((bf16[512,2048]{1,0:T(8,128)(2,1)}), bf16[128,2048]{1,0:T(8,128)(2,1)}) %reduce-scatter.8.cloned.1.call-update) | async-done | bytes 524304 | tf_op jit(solution)/shard_map/reduce_scatter | solution.py:1327
  543.0 122.8 %shard_map.188 = (bf16[4,128,2048]{2,1,0:T(8,128)(2,1)S(1)}, f32[3,256,512]{2,1,0:T(8,128)S(1)}, f32[256,512]{1,0:T(8,128)S(1)}, f32[40,128]{1,0:T(8,128)S(1)}) custom-call(bf16[4,128,2048]{2,1,0:T(8,128)(2,1)} %bitcast.205, bf16[128,2048]{1,0:T(8,128)(2,1)S(1)} %copy-done, f32[128,1]{1,0:T(8,128)S(1)} %copy.165.refs_2_, ...), custom_call_target="tpu_custom_call" | custom-call | tf_op jit(solution)/shard_map/pallas_call | solution.py:1244
  670.1 2.5 bitcast_convert_fusion
  672.7 3.3 copy.198
  (257 shorter events, 99.9 us)
Async XLA Ops:
  7.2 6.5 copy-start.36
  7.2 7.5 %copy-start.37 = (s32[1,512,8]{1,2,0:T(8,128)S(1)}, s32[1,512,8]{1,2,0:T(8,128)}, u32[]{:S(2)}) copy-start(s32[1,512,8]{1,2,0:T(8,128)} %param.22) | copy-start | bytes 49156
  7.2 10.4 %copy-start.38 = (bf16[256,16]{0,1:T(8,128)(2,1)S(1)}, bf16[256,16]{0,1:T(8,128)(2,1)}, u32[]{:S(2)}) copy-start(bf16[256,16]{0,1:T(8,128)(2,1)} %param.17) | copy-start | bytes 24580
  7.2 10.5 %copy-start.35 = (bf16[256,512]{1,0:T(8,128)(2,1)S(1)}, bf16[256,512]{1,0:T(8,128)(2,1)}, u32[]{:S(2)}) copy-start(bf16[256,512]{1,0:T(8,128)(2,1)} %param.16) | copy-start | bytes 786436
  7.2 11.4 %copy-start.8 = (bf16[1,512,2048]{2,1,0:T(8,128)(2,1)S(1)}, bf16[1,512,2048]{2,1,0:T(8,128)(2,1)}, u32[]{:S(2)}) copy-start(bf16[1,512,2048]{2,1,0:T(8,128)(2,1)} %param.12) | copy-start | bytes 6291460
  7.2 55.6 %all-gather.4.cloned.1.call-start = ((), (), s32[]{:S(2)}) async-start(), calls=%async_computation.3 | async-start | bytes 7114752 | tf_op jit(solution)/shard_map/all_gather | solution.py:1323
  13.2 114.0 %all-gather.6.cloned.1.call-start = ((), (), s32[]{:S(2)}) async-start(), calls=%async_computation.4 | async-start | bytes 2949120 | tf_op jit(solution)/shard_map/all_gather | solution.py:1323
  14.7 8.1 %copy-start.41 = (s32[1,1024]{1,0:T(1,128)S(1)}, s32[1,1024]{1,0:T(1,128)}, u32[]{:S(2)}) copy-start(s32[1,1024]{1,0:T(1,128)} %param.21) | copy-start | bytes 12292
  18.5 153.2 %reduce-scatter.4.cloned.1.call-start = ((), (), s32[]{:S(2)}) async-start(), calls=%async_computation.5 | async-start | bytes 2621440 | tf_op jit(solution)/shard_map/reduce_scatter | solution.py:1327
  19.2 51.6 %copy-start.42 = (f32[512]{0:T(512)}, f32[512]{0:T(512)S(1)}, u32[]{:S(2)}) copy-start(f32[512]{0:T(512)S(1)} %add_rsqrt_fusion) | copy-start | bytes 6148
  21.1 43.3 %copy-start.17 = (f32[512,128]{1,0:T(8,128)}, f32[512,128]{1,0:T(8,128)S(1)}, u32[]{:S(2)}) copy-start(f32[512,128]{1,0:T(8,128)S(1)} %get-tuple-element.139) | copy-start | bytes 786436
  70.7 19.9 %copy-start.6 = (f32[512,1536]{1,0:T(8,128)}, f32[512,1536]{1,0:T(8,128)S(1)}, u32[]{:S(2)}) copy-start(f32[512,1536]{1,0:T(8,128)S(1)} %fusion.4) | copy-start | bytes 9437188
  93.1 8.5 %copy-start.13 = (bf16[1,512,2048]{2,1,0:T(8,128)(2,1)S(1)}, bf16[1,512,2048]{2,1,0:T(8,128)(2,1)}, u32[]{:S(2)}) copy-start(bf16[1,512,2048]{2,1,0:T(8,128)(2,1)} %param.20) | copy-start | bytes 6291460
  94.3 11.4 %collective-permute-start.3 = (bf16[1,512,4,128]{3,1,2,0:T(8,128)(2,1)}, bf16[1,512,4,128]{3,1,2,0:T(8,128)(2,1)}, u32[]{:S(2)}, u32[]{:S(2)}) collective-permute-start(bf16[1,512,4,128]{3,1,2,0:T(8,128)(2,1)} %fusion.36), channel_id=1, source_target_pairs={{0,4},{1,5},{2,6},{3,7},{8,12},{9,13},{10,14},{11,15},{16,20},{17,... | collective-permute-start | bytes 1572872 | tf_op jit(solution)/shard_map/ppermute | solution.py:25
  100.0 11.0 %collective-permute-start.2 = (bf16[1,512,4,128]{1,3,2,0:T(8,128)(2,1)}, bf16[1,512,4,128]{1,3,2,0:T(8,128)(2,1)S(1)}, u32[]{:S(2)}, u32[]{:S(2)}) collective-permute-start(bf16[1,512,4,128]{1,3,2,0:T(8,128)(2,1)} %bitcast.208), channel_id=1, source_target_pairs={{0,4},{1,5},{2,6},{3,7},{8,12},{9,13},{10,14},{11,15},{16,20},{17,... | collective-permute-start | bytes 1572872 | tf_op jit(solution)/shard_map/ppermute | solution.py:25
  103.2 22.8 %collective-permute-start = (bf16[512,1024]{1,0:T(8,128)(2,1)}, bf16[512,1024]{1,0:T(8,128)(2,1)}, u32[]{:S(2)}, u32[]{:S(2)}) collective-permute-start(bf16[512,1024]{1,0:T(8,128)(2,1)} %get-tuple-element.128), channel_id=1, source_target_pairs={{0,8},{8,0},{16,24},{24,16},{1,9},{9,1},{17,25},{25,17},{2,10},{10... | collective-permute-start | bytes 3145736 | tf_op jit(solution)/shard_map/ppermute | solution.py:1294
  104.7 22.5 %collective-permute-start.1 = (bf16[512,1024]{1,0:T(8,128)(2,1)}, bf16[512,1024]{1,0:T(8,128)(2,1)}, u32[]{:S(2)}, u32[]{:S(2)}) collective-permute-start(bf16[512,1024]{1,0:T(8,128)(2,1)} %get-tuple-element.127), channel_id=1, source_target_pairs={{0,16},{8,24},{16,0},{24,8},{1,17},{9,25},{17,1},{25,9},{2,18},{10... | collective-permute-start | bytes 3145736 | tf_op jit(solution)/shard_map/ppermute | solution.py:1294
  114.6 12.5 %copy-start.45 = (bf16[4,128,512]{2,1,0:T(8,128)(2,1)}, bf16[4,128,512]{2,1,0:T(8,128)(2,1)S(1)}, u32[]{:S(2)}) copy-start(bf16[4,128,512]{2,1,0:T(8,128)(2,1)S(1)} %fusion.25) | copy-start | bytes 1572868
  131.4 358.2 %reduce-scatter.6.cloned.1.call-start = ((), (), s32[]{:S(2)}) async-start(), calls=%async_computation.6 | async-start | bytes 18874368 | tf_op jit(solution)/shard_map/reduce_scatter | solution.py:1327
  131.4 42.9 %collective-permute-start.4 = (bf16[512,1024]{1,0:T(8,128)(2,1)}, bf16[512,1024]{1,0:T(8,128)(2,1)}, u32[]{:S(2)}, u32[]{:S(2)}) collective-permute-start(bf16[512,1024]{1,0:T(8,128)(2,1)} %get-tuple-element.127), channel_id=1, source_target_pairs={{0,8},{8,0},{16,24},{24,16},{1,9},{9,1},{17,25},{25,17},{2,10},{10... | collective-permute-start | bytes 3145736 | tf_op jit(solution)/shard_map/ppermute | solution.py:1294
  132.1 42.3 %collective-permute-start.5 = (bf16[512,1024]{1,0:T(8,128)(2,1)}, bf16[512,1024]{1,0:T(8,128)(2,1)}, u32[]{:S(2)}, u32[]{:S(2)}) collective-permute-start(bf16[512,1024]{1,0:T(8,128)(2,1)} %get-tuple-element.128), channel_id=1, source_target_pairs={{0,16},{8,24},{16,0},{24,8},{1,17},{9,25},{17,1},{25,9},{2,18},{10... | collective-permute-start | bytes 3145736 | tf_op jit(solution)/shard_map/ppermute | solution.py:1294
  132.6 43.2 %collective-permute-start.6 = (bf16[512,1024]{1,0:T(8,128)(2,1)}, bf16[512,1024]{1,0:T(8,128)(2,1)}, u32[]{:S(2)}, u32[]{:S(2)}) collective-permute-start(bf16[512,1024]{1,0:T(8,128)(2,1)} %collective-permute-done), channel_id=1, source_target_pairs={{0,16},{8,24},{16,0},{24,8},{1,17},{9,25},{17,1},{25,9},{2,18},{10... | collective-permute-start | bytes 3145736 | tf_op jit(solution)/shard_map/ppermute | solution.py:1294
  134.1 41.7 %collective-permute-start.7 = (bf16[512,1024]{1,0:T(8,128)(2,1)}, bf16[512,1024]{1,0:T(8,128)(2,1)}, u32[]{:S(2)}, u32[]{:S(2)}) collective-permute-start(bf16[512,1024]{1,0:T(8,128)(2,1)} %collective-permute-done.1), channel_id=1, source_target_pairs={{0,8},{8,0},{16,24},{24,16},{1,9},{9,1},{17,25},{25,17},{2,10},{10... | collective-permute-start | bytes 3145736 | tf_op jit(solution)/shard_map/ppermute | solution.py:1294
  375.0 160.7 %reduce-scatter.8.cloned.1.call-start = ((), (), s32[]{:S(2)}) async-start(), calls=%async_computation.7 | async-start | bytes 2621440 | tf_op jit(solution)/shard_map/reduce_scatter | solution.py:1327
  384.1 30.4 %copy-start.44 = (bf16[4,2,4,128,512]{4,3,2,1,0:T(8,128)(2,1)S(1)}, bf16[4,2,4,128,512]{4,3,2,1,0:T(8,128)(2,1)}, u32[]{:S(2)}) copy-start(bf16[4,2,4,128,512]{4,3,2,1,0:T(8,128)(2,1)} %get-tuple-element.46) | copy-start | bytes 12582916
  384.1 57.2 %collective-permute-start.8 = (bf16[128,2048]{1,0:T(8,128)(2,1)}, bf16[128,2048]{1,0:T(8,128)(2,1)}, u32[]{:S(2)}, u32[]{:S(2)}) collective-permute-start(bf16[128,2048]{1,0:T(8,128)(2,1)} %get-tuple-element.48), channel_id=1, source_target_pairs={{0,1},{1,2},{2,3},{3,0},{4,5},{5,6},{6,7},{7,4},{8,9},{9,10},{10,1... | collective-permute-start | bytes 1572872 | tf_op jit(solution)/shard_map/ppermute | solution.py:1314
  384.1 59.3 %collective-permute-start.9 = (bf16[128,2048]{1,0:T(8,128)(2,1)}, bf16[128,2048]{1,0:T(8,128)(2,1)}, u32[]{:S(2)}, u32[]{:S(2)}) collective-permute-start(bf16[128,2048]{1,0:T(8,128)(2,1)} %get-tuple-element.48), channel_id=1, source_target_pairs={{0,3},{1,0},{2,1},{3,2},{4,7},{5,4},{6,5},{7,6},{8,11},{9,8},{10,9... | collective-permute-start | bytes 1572872 | tf_op jit(solution)/shard_map/ppermute | solution.py:1314
  387.9 57.4 %collective-permute-start.10 = (bf16[128,2048]{1,0:T(8,128)(2,1)}, bf16[128,2048]{1,0:T(8,128)(2,1)}, u32[]{:S(2)}, u32[]{:S(2)}) collective-permute-start(bf16[128,2048]{1,0:T(8,128)(2,1)} %get-tuple-element.48), channel_id=1, source_target_pairs={{0,2},{1,3},{2,0},{3,1},{4,6},{5,7},{6,4},{7,5},{8,10},{9,11},{10,... | collective-permute-start | bytes 1572872 | tf_op jit(solution)/shard_map/ppermute | solution.py:1314
  461.1 8.4 %collective-permute-start.11 = (bf16[1,512,4,128]{3,1,2,0:T(8,128)(2,1)}, bf16[1,512,4,128]{3,1,2,0:T(8,128)(2,1)}, u32[]{:S(2)}, u32[]{:S(2)}) collective-permute-start(bf16[1,512,4,128]{3,1,2,0:T(8,128)(2,1)} %slice.245), channel_id=1, source_target_pairs={{4,0},{5,1},{6,2},{7,3},{12,8},{13,9},{14,10},{15,11},{20,16},{21,... | collective-permute-start | bytes 1572872 | tf_op jit(solution)/shard_map/ppermute | solution.py:25
  489.6 183.1 %all-gather.8.cloned.1.call-start = ((), (), s32[]{:S(2)}) async-start(), calls=%async_computation.8 | async-start | bytes 2621440 | tf_op jit(solution)/shard_map/all_gather | solution.py:1323
  489.6 6.6 copy-start.46
  495.0 5.6 collective-permute-start.12
  (37 other events, 125.5 us)
Sparse Core Ops, SparseCore 0:
  13.3 49.5 all-gather.3
  64.7 30.1 all-gather.5
  131.5 40.1 reduce-scatter.3
  375.1 114.3 reduce-scatter.5
  491.8 43.8 reduce-scatter.7
  537.9 73.9 all-gather.7

commit v6 on v5

--- a/solution.py
+++ b/solution.py
@@ -935,8 +935,10 @@
     d_hidden_ref,
     qkv_ref,
     out_ref,
+    layer_ref,
     small_ref,
     rows_out,
+    layer_out,
     qkv_out,
     out_out,
     small_out,
@@ -1101,25 +1103,28 @@
                 out_out[...] = part
 
 
-    def moved(j, side):
+    spread = ((own_rows, rows_out), (layer_ref, layer_out))
+
+    def moved(i, j, side):
+        own, whole = spread[i]
         return remote(
-            own_rows if j == 0 else rows_out.at[order[j]],
-            rows_out.at[order[j]],
-            send_z.at[j, side],
-            recv_z.at[order[j]],
+            own if j == 0 else whole.at[order[j]],
+            whole.at[order[j]],
+            send_z.at[i, j, side],
+            recv_z.at[i, order[j]],
             sides[side],
         )
 
     def onward(j):
         return (((order[j] <= z) & (z < 3), 0), ((order[j] >= z) & (z > 0), 1))
 
-    def along(j):
+    def along(i, j):
         for there, side in onward(j):
-            pl.when(there)(lambda: moved(j, side).start())
-
-    def passed_on(j):
-        moved(j, 0).wait_recv()
-        along(j)
+            pl.when(there)(lambda: moved(i, j, side).start())
+
+    def passed_on(i, j):
+        moved(i, j, 0).wait_recv()
+        along(i, j)
 
 
     def small(i, src, dst, device):
@@ -1145,11 +1150,16 @@
 
     for part in to_sibling():
         part.start()
+    inner = (z > 0) & (z < 3)
+    pl.when(inner)(lambda: along(1, 0))
     for s in range(3):
         pass_right(3 - s)
         pass_left(s)
+        if s == 0:
+            passed_on(1, 1)
         if s == 1:
             weights_first()
+    pl.when((z == 0) | (z == 3))(lambda: along(1, 0))
     d_normed = parts_ref[z].astype(f32)
     right_in[0] = jnp.zeros(right_in.shape[1:], bf16)
     left_in[3] = jnp.zeros(left_in.shape[1:], bf16)
@@ -1168,8 +1178,9 @@
     scaled = gain_ref[...] * d_normed
     shift = jnp.mean(scaled * unit, axis=1, keepdims=True)
     own_rows[...] = (d_hidden_ref[...] + scale * (scaled - unit * shift)).astype(bf16)
-    along(0)
+    along(0, 0)
     rows_out[z] = own_rows[...]
+    layer_out[z] = layer_ref[...]
     d_gain = jnp.sum(d_normed * unit, axis=0, keepdims=True)
     for k in range(8):
         for i in range(2):
@@ -1188,18 +1199,20 @@
     sums[w] = sums[w] + from_x[0]
     sums[wy] = sums[wy] + from_x[1]
     small_y().start()
-    passed_on(1)
+    passed_on(1, 2)
+    passed_on(0, 1)
     small_y().wait_recv()
     sums[w] = sums[w] + from_y[...]
     for k in range(1, 4):
         small_z((z + k) % 4, z).start()
-    passed_on(2)
+    passed_on(1, 3)
+    passed_on(0, 2)
     weights_last()
     for k in range(1, 4):
         small_z(z, (z + k) % 4).wait_recv()
     from_z[z] = sums[w]
     small_out[...] = add(*(from_z[k] for k in range(4)))
-    passed_on(3)
+    passed_on(0, 3)
     for s in range(3):
 
         @pl.when(z < 3 - s)
@@ -1219,12 +1232,13 @@
     small_y().wait_send()
     for k in range(1, 4):
         small_z((z + k) % 4, z).wait_send()
-    for j in range(4):
-        for there, side in onward(j):
-            pl.when(there)(lambda: moved(j, side).wait_send())
-
-
-def finish_call(parts, rows, scale, gain, d_hidden, d_qkv, d_out, small):
+    for i in range(2):
+        for j in range(4):
+            for there, side in onward(j):
+                pl.when(there)(lambda: moved(i, j, side).wait_send())
+
+
+def finish_call(parts, rows, scale, gain, d_hidden, d_qkv, d_out, layer, small):
     dma = pltpu.SemaphoreType.DMA
     anywhere, vmem = (pl.BlockSpec(memory_space=pl.ANY), pl.BlockSpec(memory_space=pltpu.VMEM))
     share, width = rows.shape
@@ -1234,23 +1248,24 @@
     bf16, f32 = (jnp.bfloat16, jnp.float32)
 
     def body(*refs):
-        ins, outs, rest = (refs[:8], refs[8:12], refs[12:])
-        parts_in, small_in = (ins[0], ins[7])
+        ins, outs, rest = (refs[:9], refs[9:14], refs[14:])
+        parts_in, small_in = (ins[0], ins[8])
         parts_own, small_own = rest[:2]
         parts_own[...] = parts_in[...]
         small_own[...] = small_in[...]
-        finish_kernel(parts_own, *ins[1:7], small_own, *outs, *rest[2:])
+        finish_kernel(parts_own, *ins[1:8], small_own, *outs, *rest[2:])
 
     return pl.pallas_call(
         body,
         out_shape=(
+            jax.ShapeDtypeStruct((4, share, width), bf16),
             jax.ShapeDtypeStruct((4, share, width), bf16),
             jax.ShapeDtypeStruct((3, count, heads), f32),
             jax.ShapeDtypeStruct((count, heads), f32),
             jax.ShapeDtypeStruct(block, f32),
         ),
-        in_specs=[vmem, vmem, vmem, vmem, vmem, anywhere, anywhere, vmem],
-        out_specs=(vmem, vmem, vmem, vmem),
+        in_specs=[vmem] * 5 + [anywhere, anywhere, vmem, vmem],
+        out_specs=(vmem,) * 5,
         scratch_shapes=[
             pltpu.VMEM((4, share, width), bf16),
             pltpu.VMEM((4, 2) + block, f32),
@@ -1272,8 +1287,8 @@
             dma((4,)),
             dma((4,)),
             dma((4,)),
-            dma((4, 2)),
-            dma((4,)),
+            dma((2, 4, 2)),
+            dma((2, 4)),
             dma((11,)),
             dma((11,)),
             dma((2,)),
@@ -1287,7 +1302,7 @@
         compiler_params=pltpu.CompilerParams(
             collective_id=1, has_side_effects=True, vmem_limit_bytes=48 << 20
         ),
-    )(parts, rows, scale, gain, d_hidden, d_qkv, d_out, small)
+    )(parts, rows, scale, gain, d_hidden, d_qkv, d_out, layer, small)
 
 
 def swapped(rows, flip):
@@ -1594,8 +1609,7 @@
     d_normed_parts, d_qkv, d_out_weight, moe_own = lax.optimization_barrier(
         (d_normed_parts, d_qkv.astype(bf16), d_out_weight.astype(bf16), moe_own)
     )
-    layer_out = gathered((hidden + moe_own).astype(bf16), TENSOR).reshape(layer_in.shape)
-    grad_in, grad_qkv, grad_out_weight, small = finish_call(
+    grad_in, layer_out, grad_qkv, grad_out_weight, small = finish_call(
         d_normed_parts.reshape(tensor_count, share, model_width),
         own_rows(layer_in.reshape(token_count, model_width)),
         own_rows(scale_one),
@@ -1603,9 +1617,11 @@
         d_hidden,
         d_qkv.reshape(4, 2, weight_rows, -1),
         d_out_weight.reshape(4, 2, weight_rows, -1),
+        (hidden + moe_own).astype(bf16),
         small.reshape((4, 2) + small.shape[1:]),
     )
     grad_in = grad_in.astype(f32).reshape(layer_in.shape)
+    layer_out = layer_out.reshape(layer_in.shape)
     grad_qkv = grad_qkv.transpose(1, 0, 2)
     lines_of = weight_rows // 128
     gain_share = weight_rows // tensor_count

time: 693 us -> 675 us (0.974)
  Pallas kernels: 322 us -> 311 us
  waiting for transfers between devices: 104 us -> 96.3 us
    pallas_call x1, Pallas kernels: 123 us -> 111 us  [finish_call(): pl.pallas_call(body, out_shape=(jax.ShapeDtypeStruct((4, share, width), b...]
    reduce_scatter x3, waiting for transfers between devices: 51 us -> 43.6 us  [scattered(): return lax.psum_scatter(rows, axes, scatter_dimension=0, tiled=True)]
    unnamed x109 -> x157, local copies, waits for them, and re-layouts: 16.3 us -> 14.6 us
    all_gather x3 -> x2, waiting for transfers between devices: 38.6 us -> 38.6 us  [gathered(): return lax.all_gather(rows, axes, axis=0, tiled=True)]
  transfers between devices with their start and end apart: 19 -> 18, of which waited for: 7 -> 7; matrix products, arithmetic and copies ran while one was open for 27% -> 27% of each run, Pallas kernels for 18% -> 0%
where the time goes in v6:
time: 675 us; the launch traced here: 667 us
  Pallas kernels  311 us (46%)
  matrix products  96.4 us (14%)
  waiting for transfers between devices  96.3 us (14%)
  local copies, waits for them, and re-layouts  66 us (10%)
  other arithmetic  43.6 us (6%)
  blocking collectives  22.2 us (3%)
  starting transfers between devices  16.8 us (2%)
  between operations  15.6 us (2%)
    pallas_call x1, Pallas kernels, experts_call(): pl.pallas_call(functools.partial(experts_kernel, experts), out_shape=tupl...  199 us
    pallas_call x1, Pallas kernels, finish_call(): pl.pallas_call(body, out_shape=(jax.ShapeDtypeStruct((4, share, width), b...  111 us
    reduce_scatter x3, waiting for transfers between devices, scattered(): return lax.psum_scatter(rows, axes, scatter_dimension=0, tiled=True)  43.6 us
    all_gather x2, waiting for transfers between devices, gathered(): return lax.all_gather(rows, axes, axis=0, tiled=True)  38.6 us
    dot_general x1, matrix products, per_device_dense(): jnp.dot(normed_all.T, d_both, preferred_element_type=f32)  26.5 us
    psum x2, blocking collectives, row_sums(): return lax.psum(partial_rows, TENSOR)  22.2 us
    unnamed x157, local copies, waits for them, and re-layouts  14.6 us
    dot_general x1, matrix products, per_device_dense(): jnp.dot(gated.T, grads_all, preferred_element_type=f32)  14.3 us
  transfers between devices with their start and end apart: 18, of which 7 were waited for; matrix products, arithmetic and copies ran while one was open for 27% of the time, Pallas kernels for 0%

profile of v6, /device:TPU:0, one launch (start us, length us, event | category | flops | bytes accessed | tf_op | source)
XLA Modules:
  0.0 667.4 jit_solution(982881059675814902)
XLA Ops:
  9.8 3.4 concatenate.72
  24.3 38.6 %all-gather.3.cloned.1.call-done = bf16[2048,1539]{0,1:T(8,128)(2,1)} async-done(((bf16[256,1539]{0,1:T(8,128)(2,1)}), bf16[2048,1539]{0,1:T(8,128)(2,1)}) %all-gather.3.cloned.1.call-update) | async-done | bytes 6303760 | tf_op jit(solution)/shard_map/all_gather | solution.py:1338
  64.4 6.3 fusion.4
  71.0 12.3 %psum.14 = f32[512,2]{0,1:T(2,128)} all-reduce(f32[512,2]{0,1:T(2,128)S(1)} %pad_maximum_fusion.6), channel_id=1, replica_groups=mesh['weights'=4,'context'=2,'tensor'=4] {'tensor'}, use_global_device_ids=true, to_apply=%region_3.4 | all-reduce | flops 1024 | bytes 8192 | tf_op jit(solution)/shard_map/psum | solution.py:69
  88.2 2.3 multiply_multiply_fusion.1
  105.6 3.5 fusion.78
  114.5 11.3 %collective-permute-done.1 = bf16[512,1024]{1,0:T(8,128)(2,1)} collective-permute-done((bf16[512,1024]{1,0:T(8,128)(2,1)}, bf16[512,1024]{1,0:T(8,128)(2,1)}, u32[]{:S(2)}, u32[]{:S(2)}) %collective-permute-start.1) | collective-permute-done | bytes 1048608 | tf_op jit(solution)/shard_map/ppermute | solution.py:1309
  127.0 4.2 convolution_convert_fusion.2
  135.5 2.5 convert_element_type.141
  142.4 29.2 %reduce-scatter.4.cloned.1.call-done = bf16[128,2048]{1,0:T(8,128)(2,1)} async-done(((bf16[512,2048]{1,0:T(8,128)(2,1)}), bf16[128,2048]{1,0:T(8,128)(2,1)}) %reduce-scatter.4.cloned.1.call-update) | async-done | bytes 524304 | tf_op jit(solution)/shard_map/reduce_scatter | solution.py:1342
  175.7 199.1 %shard_map.187 = (bf16[4,2,4,128,2048]{4,3,2,1,0:T(8,128)(2,1)}, bf16[4,2,4,128,2048]{4,3,2,1,0:T(8,128)(2,1)}, bf16[4,2,4,128,512]{4,3,2,1,0:T(8,128)(2,1)}, bf...) custom-call(bf16[128,2048]{1,0:T(8,128)(2,1)} %multiply_convert_fusion.1.x_ref, ...), custom_call_target="tpu_custom_call" | custom-call | tf_op jit(solution)/shard_map/pallas_call | solution.py:877
  382.4 2.9 multiply_reduce_fusion.2
  387.1 3.8 collective-permute-start.9
  390.9 26.5 %fusion.81 = f32[2048,1024]{0,1:T(8,128)} fusion(bf16[4096,2048]{1,0:T(8,128)(2,1)} %bitcast.249, bf16[4096,1024]{1,0:T(8,128)(2,1)} %bitcast.250), kind=kOutput, calls=%fused_computation.167 | convolution fusion | flops 17179869184 | bytes 33554432 | tf_op jit(solution)/shard_map/dot_general | solution.py:1524
  417.4 14.3 %fusion.82 = f32[512,2048]{1,0:T(8,128)} fusion(bf16[4096,512]{1,0:T(8,128)(2,1)S(1)} %bitcast.251, bf16[4096,2048]{1,0:T(8,128)(2,1)} %bitcast.248), kind=kOutput, calls=%fused_computation.168 | convolution fusion | flops 8589934592 | bytes 25165824 | tf_op jit(solution)/shard_map/dot_general | solution.py:1528
  434.1 8.7 %copy.153 = f32[2048,2,2,256]{3,0,2,1:T(8,128)} copy(f32[2048,2,2,256]{0,3,2,1:T(8,128)} %bitcast.195) | data formatting | bytes 16777216 | tf_op jit(solution)/shard_map/reshape | solution.py:1525
  448.7 3.0 fusion.22
  451.8 5.7 multiply_reduce_fusion
  464.1 2.8 broadcast_multiply_fusion
  468.2 2.6 copy.175
  476.1 9.9 %psum.15 = f32[512,2]{0,1:T(2,128)} all-reduce(f32[512,2]{0,1:T(2,128)S(1)} %pad_maximum_fusion.7), channel_id=1, replica_groups=mesh['weights'=4,'context'=2,'tensor'=4] {'tensor'}, use_global_device_ids=true, to_apply=%region_17.18 | all-reduce | flops 1024 | bytes 8192 | tf_op jit(solution)/shard_map/psum | solution.py:69
  486.0 3.6 reduce-scatter.6.cloned.1.call-done
  490.8 5.2 fusion.19
  499.5 2.2 fusion.80
  503.3 4.3 convolution_convert_fusion.1
  511.7 3.0 subtract_convert_fusion
  514.8 5.6 convolution_convert_fusion
  520.4 4.6 fusion.13
  525.1 10.7 %reduce-scatter.8.cloned.1.call-done = bf16[128,2048]{1,0:T(8,128)(2,1)} async-done(((bf16[512,2048]{1,0:T(8,128)(2,1)}), bf16[128,2048]{1,0:T(8,128)(2,1)}) %reduce-scatter.8.cloned.1.call-update) | async-done | bytes 524304 | tf_op jit(solution)/shard_map/reduce_scatter | solution.py:1342
  537.1 111.5 %shard_map.188 = (bf16[4,128,2048]{2,1,0:T(8,128)(2,1)}, bf16[4,128,2048]{2,1,0:T(8,128)(2,1)}, f32[3,256,512]{2,1,0:T(8,128)S(1)}, f32[256,512]{1,0:T(8,128)S(1)}, f32[40,128]{1,0:T(8,128)S(1)}) custom-call(bf16[4,128,2048]{2,1,0:T(8,128)(2,1)} %bitcast.205, bf16[128,2048]{1,0:T(8,128)(2,1)S(1)} %dynamic-slice_bitcast_fusion.refs_1_, ...), custom_call_target="tpu_custom_call" | custom-call | tf_op jit(solution)/shard_map/pallas_call | solution.py:1258
  648.6 4.3 bitcast_convert_fusion
  655.2 3.2 copy.198
  (303 shorter events, 100.4 us)
Async XLA Ops:
  7.2 10.4 %copy-start.55 = (bf16[256,16]{0,1:T(8,128)(2,1)S(1)}, bf16[256,16]{0,1:T(8,128)(2,1)}, u32[]{:S(2)}) copy-start(bf16[256,16]{0,1:T(8,128)(2,1)} %param.17) | copy-start | bytes 24580
  7.2 10.5 %copy-start.34 = (bf16[256,512]{1,0:T(8,128)(2,1)S(1)}, bf16[256,512]{1,0:T(8,128)(2,1)}, u32[]{:S(2)}) copy-start(bf16[256,512]{1,0:T(8,128)(2,1)} %param.16) | copy-start | bytes 786436
  7.2 11.4 %copy-start.5 = (bf16[1,512,2048]{2,1,0:T(8,128)(2,1)S(1)}, bf16[1,512,2048]{2,1,0:T(8,128)(2,1)}, u32[]{:S(2)}) copy-start(bf16[1,512,2048]{2,1,0:T(8,128)(2,1)} %param.12) | copy-start | bytes 6291460
  7.2 55.6 %all-gather.3.cloned.1.call-start = ((), (), s32[]{:S(2)}) async-start(), calls=%async_computation.3 | async-start | bytes 7114752 | tf_op jit(solution)/shard_map/all_gather | solution.py:1338
  13.2 113.9 %all-gather.5.cloned.1.call-start = ((), (), s32[]{:S(2)}) async-start(), calls=%async_computation.4 | async-start | bytes 2949120 | tf_op jit(solution)/shard_map/all_gather | solution.py:1338
  18.5 153.1 %reduce-scatter.4.cloned.1.call-start = ((), (), s32[]{:S(2)}) async-start(), calls=%async_computation.5 | async-start | bytes 2621440 | tf_op jit(solution)/shard_map/reduce_scatter | solution.py:1342
  19.2 51.5 %copy-start.64 = (f32[512]{0:T(512)}, f32[512]{0:T(512)S(1)}, u32[]{:S(2)}) copy-start(f32[512]{0:T(512)S(1)} %add_rsqrt_fusion) | copy-start | bytes 6148
  21.2 43.3 %copy-start.15 = (f32[512,128]{1,0:T(8,128)}, f32[512,128]{1,0:T(8,128)S(1)}, u32[]{:S(2)}) copy-start(f32[512,128]{1,0:T(8,128)S(1)} %get-tuple-element.141) | copy-start | bytes 786436
  64.4 108.9 %copy-start.37 = (f32[2048,1]{0,1:T(1,128)}, f32[2048,1]{0,1:T(1,128)S(1)}, u32[]{:S(2)}) copy-start(f32[2048,1]{0,1:T(1,128)S(1)} %get-tuple-element.148) | copy-start | bytes 24580
  70.7 19.8 %copy-start.3 = (f32[512,1536]{1,0:T(8,128)}, f32[512,1536]{1,0:T(8,128)S(1)}, u32[]{:S(2)}) copy-start(f32[512,1536]{1,0:T(8,128)S(1)} %fusion.4) | copy-start | bytes 9437188
  94.2 11.4 %collective-permute-start = (bf16[1,512,4,128]{3,1,2,0:T(8,128)(2,1)}, bf16[1,512,4,128]{3,1,2,0:T(8,128)(2,1)}, u32[]{:S(2)}, u32[]{:S(2)}) collective-permute-start(bf16[1,512,4,128]{3,1,2,0:T(8,128)(2,1)} %fusion.34), channel_id=1, source_target_pairs={{0,4},{1,5},{2,6},{3,7},{8,12},{9,13},{10,14},{11,15},{16,20},{17,... | collective-permute-start | bytes 1572872 | tf_op jit(solution)/shard_map/ppermute | solution.py:25
  99.9 11.0 %collective-permute-start.3 = (bf16[1,512,4,128]{1,3,2,0:T(8,128)(2,1)}, bf16[1,512,4,128]{1,3,2,0:T(8,128)(2,1)S(1)}, u32[]{:S(2)}, u32[]{:S(2)}) collective-permute-start(bf16[1,512,4,128]{1,3,2,0:T(8,128)(2,1)} %bitcast.208), channel_id=1, source_target_pairs={{0,4},{1,5},{2,6},{3,7},{8,12},{9,13},{10,14},{11,15},{16,20},{17,... | collective-permute-start | bytes 1572872 | tf_op jit(solution)/shard_map/ppermute | solution.py:25
  103.1 22.8 %collective-permute-start.1 = (bf16[512,1024]{1,0:T(8,128)(2,1)}, bf16[512,1024]{1,0:T(8,128)(2,1)}, u32[]{:S(2)}, u32[]{:S(2)}) collective-permute-start(bf16[512,1024]{1,0:T(8,128)(2,1)} %get-tuple-element.130), channel_id=1, source_target_pairs={{0,8},{8,0},{16,24},{24,16},{1,9},{9,1},{17,25},{25,17},{2,10},{10... | collective-permute-start | bytes 3145736 | tf_op jit(solution)/shard_map/ppermute | solution.py:1309
  104.6 22.5 %collective-permute-start.2 = (bf16[512,1024]{1,0:T(8,128)(2,1)}, bf16[512,1024]{1,0:T(8,128)(2,1)}, u32[]{:S(2)}, u32[]{:S(2)}) collective-permute-start(bf16[512,1024]{1,0:T(8,128)(2,1)} %get-tuple-element.129), channel_id=1, source_target_pairs={{0,16},{8,24},{16,0},{24,8},{1,17},{9,25},{17,1},{25,9},{2,18},{10... | collective-permute-start | bytes 3145736 | tf_op jit(solution)/shard_map/ppermute | solution.py:1309
  114.5 12.5 %copy-start.68 = (bf16[4,128,512]{2,1,0:T(8,128)(2,1)}, bf16[4,128,512]{2,1,0:T(8,128)(2,1)S(1)}, u32[]{:S(2)}) copy-start(bf16[4,128,512]{2,1,0:T(8,128)(2,1)S(1)} %fusion.25) | copy-start | bytes 1572868
  131.3 358.3 %reduce-scatter.6.cloned.1.call-start = ((), (), s32[]{:S(2)}) async-start(), calls=%async_computation.6 | async-start | bytes 18874368 | tf_op jit(solution)/shard_map/reduce_scatter | solution.py:1342
  131.3 42.9 %collective-permute-start.4 = (bf16[512,1024]{1,0:T(8,128)(2,1)}, bf16[512,1024]{1,0:T(8,128)(2,1)}, u32[]{:S(2)}, u32[]{:S(2)}) collective-permute-start(bf16[512,1024]{1,0:T(8,128)(2,1)} %get-tuple-element.129), channel_id=1, source_target_pairs={{0,8},{8,0},{16,24},{24,16},{1,9},{9,1},{17,25},{25,17},{2,10},{10... | collective-permute-start | bytes 3145736 | tf_op jit(solution)/shard_map/ppermute | solution.py:1309
  132.0 42.3 %collective-permute-start.5 = (bf16[512,1024]{1,0:T(8,128)(2,1)}, bf16[512,1024]{1,0:T(8,128)(2,1)}, u32[]{:S(2)}, u32[]{:S(2)}) collective-permute-start(bf16[512,1024]{1,0:T(8,128)(2,1)} %get-tuple-element.130), channel_id=1, source_target_pairs={{0,16},{8,24},{16,0},{24,8},{1,17},{9,25},{17,1},{25,9},{2,18},{10... | collective-permute-start | bytes 3145736 | tf_op jit(solution)/shard_map/ppermute | solution.py:1309
  132.5 43.2 %collective-permute-start.6 = (bf16[512,1024]{1,0:T(8,128)(2,1)}, bf16[512,1024]{1,0:T(8,128)(2,1)}, u32[]{:S(2)}, u32[]{:S(2)}) collective-permute-start(bf16[512,1024]{1,0:T(8,128)(2,1)} %collective-permute-done.1), channel_id=1, source_target_pairs={{0,16},{8,24},{16,0},{24,8},{1,17},{9,25},{17,1},{25,9},{2,18},{10... | collective-permute-start | bytes 3145736 | tf_op jit(solution)/shard_map/ppermute | solution.py:1309
  134.0 41.7 %collective-permute-start.7 = (bf16[512,1024]{1,0:T(8,128)(2,1)}, bf16[512,1024]{1,0:T(8,128)(2,1)}, u32[]{:S(2)}, u32[]{:S(2)}) collective-permute-start(bf16[512,1024]{1,0:T(8,128)(2,1)} %collective-permute-done.2), channel_id=1, source_target_pairs={{0,8},{8,0},{16,24},{24,16},{1,9},{9,1},{17,25},{25,17},{2,10},{10... | collective-permute-start | bytes 3145736 | tf_op jit(solution)/shard_map/ppermute | solution.py:1309
  173.3 209.1 %copy-start.61 = (f32[128]{0:T(128)}, f32[128]{0:T(128)S(1)}, u32[]{:S(2)}) copy-start(f32[128]{0:T(128)S(1)} %add_rsqrt_fusion.1) | copy-start | bytes 1540
  374.9 160.9 %reduce-scatter.8.cloned.1.call-start = ((), (), s32[]{:S(2)}) async-start(), calls=%async_computation.7 | async-start | bytes 2621440 | tf_op jit(solution)/shard_map/reduce_scatter | solution.py:1342
  376.0 9.3 %copy-start.35 = (pred[16,128]{0,1:T(32,128)(4,1)}, pred[16,128]{0,1:T(32,128)(4,1)S(1)}, u32[]{:S(2)}) copy-start(pred[16,128]{0,1:T(32,128)(4,1)S(1)} %copy.179) | copy-start | bytes 6148
  387.0 30.4 %copy-start.67 = (bf16[4,2,4,128,512]{4,3,2,1,0:T(8,128)(2,1)S(1)}, bf16[4,2,4,128,512]{4,3,2,1,0:T(8,128)(2,1)}, u32[]{:S(2)}) copy-start(bf16[4,2,4,128,512]{4,3,2,1,0:T(8,128)(2,1)} %get-tuple-element.47) | copy-start | bytes 12582916
  387.0 55.8 %collective-permute-start.8 = (bf16[128,2048]{1,0:T(8,128)(2,1)S(1)}, bf16[128,2048]{1,0:T(8,128)(2,1)}, u32[]{:S(2)}, u32[]{:S(2)}) collective-permute-start(bf16[128,2048]{1,0:T(8,128)(2,1)S(1)} %get-tuple-element.49), channel_id=1, source_target_pairs={{0,1},{1,2},{2,3},{3,0},{4,5},{5,6},{6,7},{7,4},{8,9},{9,10},{10,1... | collective-permute-start | bytes 1572872 | tf_op jit(solution)/shard_map/ppermute | solution.py:1329
  387.1 57.8 %collective-permute-start.9 = (bf16[128,2048]{1,0:T(8,128)(2,1)S(1)}, bf16[128,2048]{1,0:T(8,128)(2,1)}, u32[]{:S(2)}, u32[]{:S(2)}) collective-permute-start(bf16[128,2048]{1,0:T(8,128)(2,1)S(1)} %get-tuple-element.49), channel_id=1, source_target_pairs={{0,3},{1,0},{2,1},{3,2},{4,7},{5,4},{6,5},{7,6},{8,11},{9,8},{10,9... | collective-permute-start | bytes 1572872 | tf_op jit(solution)/shard_map/ppermute | solution.py:1329
  390.9 55.9 %collective-permute-start.10 = (bf16[128,2048]{1,0:T(8,128)(2,1)S(1)}, bf16[128,2048]{1,0:T(8,128)(2,1)}, u32[]{:S(2)}, u32[]{:S(2)}) collective-permute-start(bf16[128,2048]{1,0:T(8,128)(2,1)S(1)} %get-tuple-element.49), channel_id=1, source_target_pairs={{0,2},{1,3},{2,0},{3,1},{4,6},{5,7},{6,4},{7,5},{8,10},{9,11},{10,... | collective-permute-start | bytes 1572872 | tf_op jit(solution)/shard_map/ppermute | solution.py:1329
  462.6 8.2 %collective-permute-start.11 = (bf16[1,512,4,128]{3,1,2,0:T(8,128)(2,1)}, bf16[1,512,4,128]{3,1,2,0:T(8,128)(2,1)}, u32[]{:S(2)}, u32[]{:S(2)}) collective-permute-start(bf16[1,512,4,128]{3,1,2,0:T(8,128)(2,1)} %slice.245), channel_id=1, source_target_pairs={{4,0},{5,1},{6,2},{7,3},{12,8},{13,9},{14,10},{15,11},{20,16},{21,... | collective-permute-start | bytes 1572872 | tf_op jit(solution)/shard_map/ppermute | solution.py:25
  490.8 8.7 %copy-start.36 = (pred[16,128]{0,1:T(32,128)(4,1)S(1)}, pred[16,128]{0,1:T(32,128)(4,1)}, u32[]{:S(2)}) copy-start(pred[16,128]{0,1:T(32,128)(4,1)} %copy-done.35) | copy-start | bytes 6148
  490.8 8.7 %copy-start.54 = (f32[128]{0:T(128)S(1)}, f32[128]{0:T(128)}, u32[]{:S(2)}) copy-start(f32[128]{0:T(128)} %copy-done.53) | copy-start | bytes 1540
  498.2 9.8 %collective-permute-start.12 = (bf16[1,512,4,128]{1,3,2,0:T(8,128)(2,1)}, bf16[1,512,4,128]{1,3,2,0:T(8,128)(2,1)}, u32[]{:S(2)}, u32[]{:S(2)}) collective-permute-start(bf16[1,512,4,128]{1,3,2,0:T(8,128)(2,1)} %slice.244), channel_id=1, source_target_pairs={{4,0},{5,1},{6,2},{7,3},{12,8},{13,9},{14,10},{15,11},{20,16},{21,... | collective-permute-start | bytes 1572872 | tf_op jit(solution)/shard_map/ppermute | solution.py:25
  511.7 8.7 %slice-start.3 = ((s8[6324224]{0:T(1024)(128)(4,1)}), s8[4194304]{0:T(1024)(128)(4,1)S(1)}, s32[]{:S(2)}) async-start(s8[6324224]{0:T(1024)(128)(4,1)} %bitcast.246), calls=%async_computation.11 | async-start | bytes 8388608
  (60 other events, 251.0 us)
Sparse Core Ops, SparseCore 0:
  13.3 49.5 all-gather.2
  64.7 30.1 all-gather.4
  131.4 40.1 reduce-scatter.3
  375.1 114.5 reduce-scatter.5
  491.9 43.8 reduce-scatter.7

commit v7 on v6

--- a/solution.py
+++ b/solution.py
@@ -1157,9 +1157,8 @@
         pass_left(s)
         if s == 0:
             passed_on(1, 1)
-        if s == 1:
-            weights_first()
     pl.when((z == 0) | (z == 3))(lambda: along(1, 0))
+    weights_first()
     d_normed = parts_ref[z].astype(f32)
     right_in[0] = jnp.zeros(right_in.shape[1:], bf16)
     left_in[3] = jnp.zeros(left_in.shape[1:], bf16)

time: 675 us -> 675 us (level)
  no operation moved by 1% of the time
where the time goes in v7:
time: 675 us; the launch traced here: 667 us
  Pallas kernels  311 us (46%)
  matrix products  96.4 us (14%)
  waiting for transfers between devices  96.3 us (14%)
  local copies, waits for them, and re-layouts  66 us (10%)
  other arithmetic  43.6 us (6%)
  blocking collectives  22.2 us (3%)
  starting transfers between devices  16.8 us (2%)
  between operations  15.6 us (2%)
    pallas_call x1, Pallas kernels, experts_call(): pl.pallas_call(functools.partial(experts_kernel, experts), out_shape=tupl...  199 us
    pallas_call x1, Pallas kernels, finish_call(): pl.pallas_call(body, out_shape=(jax.ShapeDtypeStruct((4, share, width), b...  111 us
    reduce_scatter x3, waiting for transfers between devices, scattered(): return lax.psum_scatter(rows, axes, scatter_dimension=0, tiled=True)  43.6 us
    all_gather x2, waiting for transfers between devices, gathered(): return lax.all_gather(rows, axes, axis=0, tiled=True)  38.6 us
    dot_general x1, matrix products, per_device_dense(): jnp.dot(normed_all.T, d_both, preferred_element_type=f32)  26.5 us
    psum x2, blocking collectives, row_sums(): return lax.psum(partial_rows, TENSOR)  22.2 us
    unnamed x157, local copies, waits for them, and re-layouts  14.6 us
    dot_general x1, matrix products, per_device_dense(): jnp.dot(gated.T, grads_all, preferred_element_type=f32)  14.3 us
  transfers between devices with their start and end apart: 18, of which 7 were waited for; matrix products, arithmetic and copies ran while one was open for 27% of the time, Pallas kernels for 0%

profile of v7, /device:TPU:0, one launch (start us, length us, event | category | flops | bytes accessed | tf_op | source)
XLA Modules:
  0.0 667.4 jit_solution(2038602725174792325)
XLA Ops:
  9.8 3.4 concatenate.72
  24.3 38.6 %all-gather.3.cloned.1.call-done = bf16[2048,1539]{0,1:T(8,128)(2,1)} async-done(((bf16[256,1539]{0,1:T(8,128)(2,1)}), bf16[2048,1539]{0,1:T(8,128)(2,1)}) %all-gather.3.cloned.1.call-update) | async-done | bytes 6303760 | tf_op jit(solution)/shard_map/all_gather | solution.py:1337
  64.4 6.3 fusion.4
  71.0 12.3 %psum.14 = f32[512,2]{0,1:T(2,128)} all-reduce(f32[512,2]{0,1:T(2,128)S(1)} %pad_maximum_fusion.6), channel_id=1, replica_groups=mesh['weights'=4,'context'=2,'tensor'=4] {'tensor'}, use_global_device_ids=true, to_apply=%region_3.4 | all-reduce | flops 1024 | bytes 8192 | tf_op jit(solution)/shard_map/psum | solution.py:69
  88.2 2.3 multiply_multiply_fusion.1
  105.6 3.5 fusion.78
  114.5 11.3 %collective-permute-done.1 = bf16[512,1024]{1,0:T(8,128)(2,1)} collective-permute-done((bf16[512,1024]{1,0:T(8,128)(2,1)}, bf16[512,1024]{1,0:T(8,128)(2,1)}, u32[]{:S(2)}, u32[]{:S(2)}) %collective-permute-start.1) | collective-permute-done | bytes 1048608 | tf_op jit(solution)/shard_map/ppermute | solution.py:1308
  127.0 4.2 convolution_convert_fusion.2
  135.5 2.5 convert_element_type.141
  142.4 29.2 %reduce-scatter.4.cloned.1.call-done = bf16[128,2048]{1,0:T(8,128)(2,1)} async-done(((bf16[512,2048]{1,0:T(8,128)(2,1)}), bf16[128,2048]{1,0:T(8,128)(2,1)}) %reduce-scatter.4.cloned.1.call-update) | async-done | bytes 524304 | tf_op jit(solution)/shard_map/reduce_scatter | solution.py:1341
  175.7 199.1 %shard_map.187 = (bf16[4,2,4,128,2048]{4,3,2,1,0:T(8,128)(2,1)}, bf16[4,2,4,128,2048]{4,3,2,1,0:T(8,128)(2,1)}, bf16[4,2,4,128,512]{4,3,2,1,0:T(8,128)(2,1)}, bf...) custom-call(bf16[128,2048]{1,0:T(8,128)(2,1)} %multiply_convert_fusion.1.x_ref, ...), custom_call_target="tpu_custom_call" | custom-call | tf_op jit(solution)/shard_map/pallas_call | solution.py:877
  382.4 2.9 multiply_reduce_fusion.2
  387.1 3.8 collective-permute-start.9
  390.9 26.5 %fusion.81 = f32[2048,1024]{0,1:T(8,128)} fusion(bf16[4096,2048]{1,0:T(8,128)(2,1)} %bitcast.249, bf16[4096,1024]{1,0:T(8,128)(2,1)} %bitcast.250), kind=kOutput, calls=%fused_computation.167 | convolution fusion | flops 17179869184 | bytes 33554432 | tf_op jit(solution)/shard_map/dot_general | solution.py:1523
  417.4 14.3 %fusion.82 = f32[512,2048]{1,0:T(8,128)} fusion(bf16[4096,512]{1,0:T(8,128)(2,1)S(1)} %bitcast.251, bf16[4096,2048]{1,0:T(8,128)(2,1)} %bitcast.248), kind=kOutput, calls=%fused_computation.168 | convolution fusion | flops 8589934592 | bytes 25165824 | tf_op jit(solution)/shard_map/dot_general | solution.py:1527
  434.1 8.7 %copy.153 = f32[2048,2,2,256]{3,0,2,1:T(8,128)} copy(f32[2048,2,2,256]{0,3,2,1:T(8,128)} %bitcast.195) | data formatting | bytes 16777216 | tf_op jit(solution)/shard_map/reshape | solution.py:1524
  448.7 3.0 fusion.22
  451.8 5.7 multiply_reduce_fusion
  464.1 2.8 broadcast_multiply_fusion
  468.2 2.6 copy.175
  476.1 9.9 %psum.15 = f32[512,2]{0,1:T(2,128)} all-reduce(f32[512,2]{0,1:T(2,128)S(1)} %pad_maximum_fusion.7), channel_id=1, replica_groups=mesh['weights'=4,'context'=2,'tensor'=4] {'tensor'}, use_global_device_ids=true, to_apply=%region_17.18 | all-reduce | flops 1024 | bytes 8192 | tf_op jit(solution)/shard_map/psum | solution.py:69
  486.0 3.6 reduce-scatter.6.cloned.1.call-done
  490.8 5.2 fusion.19
  499.5 2.2 fusion.80
  503.3 4.3 convolution_convert_fusion.1
  511.7 3.0 subtract_convert_fusion
  514.8 5.6 convolution_convert_fusion
  520.4 4.6 fusion.13
  525.1 10.7 %reduce-scatter.8.cloned.1.call-done = bf16[128,2048]{1,0:T(8,128)(2,1)} async-done(((bf16[512,2048]{1,0:T(8,128)(2,1)}), bf16[128,2048]{1,0:T(8,128)(2,1)}) %reduce-scatter.8.cloned.1.call-update) | async-done | bytes 524304 | tf_op jit(solution)/shard_map/reduce_scatter | solution.py:1341
  537.1 111.5 %shard_map.188 = (bf16[4,128,2048]{2,1,0:T(8,128)(2,1)}, bf16[4,128,2048]{2,1,0:T(8,128)(2,1)}, f32[3,256,512]{2,1,0:T(8,128)S(1)}, f32[256,512]{1,0:T(8,128)S(1)}, f32[40,128]{1,0:T(8,128)S(1)}) custom-call(bf16[4,128,2048]{2,1,0:T(8,128)(2,1)} %bitcast.205, bf16[128,2048]{1,0:T(8,128)(2,1)S(1)} %dynamic-slice_bitcast_fusion.refs_1_, ...), custom_call_target="tpu_custom_call" | custom-call | tf_op jit(solution)/shard_map/pallas_call | solution.py:1257
  648.6 4.3 bitcast_convert_fusion
  655.2 3.2 copy.198
  (303 shorter events, 100.4 us)
Async XLA Ops:
  7.2 10.4 %copy-start.55 = (bf16[256,16]{0,1:T(8,128)(2,1)S(1)}, bf16[256,16]{0,1:T(8,128)(2,1)}, u32[]{:S(2)}) copy-start(bf16[256,16]{0,1:T(8,128)(2,1)} %param.17) | copy-start | bytes 24580
  7.2 10.5 %copy-start.34 = (bf16[256,512]{1,0:T(8,128)(2,1)S(1)}, bf16[256,512]{1,0:T(8,128)(2,1)}, u32[]{:S(2)}) copy-start(bf16[256,512]{1,0:T(8,128)(2,1)} %param.16) | copy-start | bytes 786436
  7.2 11.4 %copy-start.5 = (bf16[1,512,2048]{2,1,0:T(8,128)(2,1)S(1)}, bf16[1,512,2048]{2,1,0:T(8,128)(2,1)}, u32[]{:S(2)}) copy-start(bf16[1,512,2048]{2,1,0:T(8,128)(2,1)} %param.12) | copy-start | bytes 6291460
  7.2 55.6 %all-gather.3.cloned.1.call-start = ((), (), s32[]{:S(2)}) async-start(), calls=%async_computation.3 | async-start | bytes 7114752 | tf_op jit(solution)/shard_map/all_gather | solution.py:1337
  13.2 113.9 %all-gather.5.cloned.1.call-start = ((), (), s32[]{:S(2)}) async-start(), calls=%async_computation.4 | async-start | bytes 2949120 | tf_op jit(solution)/shard_map/all_gather | solution.py:1337
  18.5 153.1 %reduce-scatter.4.cloned.1.call-start = ((), (), s32[]{:S(2)}) async-start(), calls=%async_computation.5 | async-start | bytes 2621440 | tf_op jit(solution)/shard_map/reduce_scatter | solution.py:1341
  19.2 51.5 %copy-start.64 = (f32[512]{0:T(512)}, f32[512]{0:T(512)S(1)}, u32[]{:S(2)}) copy-start(f32[512]{0:T(512)S(1)} %add_rsqrt_fusion) | copy-start | bytes 6148
  21.2 43.3 %copy-start.15 = (f32[512,128]{1,0:T(8,128)}, f32[512,128]{1,0:T(8,128)S(1)}, u32[]{:S(2)}) copy-start(f32[512,128]{1,0:T(8,128)S(1)} %get-tuple-element.141) | copy-start | bytes 786436
  64.4 108.9 %copy-start.37 = (f32[2048,1]{0,1:T(1,128)}, f32[2048,1]{0,1:T(1,128)S(1)}, u32[]{:S(2)}) copy-start(f32[2048,1]{0,1:T(1,128)S(1)} %get-tuple-element.148) | copy-start | bytes 24580
  70.7 19.8 %copy-start.3 = (f32[512,1536]{1,0:T(8,128)}, f32[512,1536]{1,0:T(8,128)S(1)}, u32[]{:S(2)}) copy-start(f32[512,1536]{1,0:T(8,128)S(1)} %fusion.4) | copy-start | bytes 9437188
  94.2 11.4 %collective-permute-start = (bf16[1,512,4,128]{3,1,2,0:T(8,128)(2,1)}, bf16[1,512,4,128]{3,1,2,0:T(8,128)(2,1)}, u32[]{:S(2)}, u32[]{:S(2)}) collective-permute-start(bf16[1,512,4,128]{3,1,2,0:T(8,128)(2,1)} %fusion.34), channel_id=1, source_target_pairs={{0,4},{1,5},{2,6},{3,7},{8,12},{9,13},{10,14},{11,15},{16,20},{17,... | collective-permute-start | bytes 1572872 | tf_op jit(solution)/shard_map/ppermute | solution.py:25
  99.9 11.0 %collective-permute-start.3 = (bf16[1,512,4,128]{1,3,2,0:T(8,128)(2,1)}, bf16[1,512,4,128]{1,3,2,0:T(8,128)(2,1)S(1)}, u32[]{:S(2)}, u32[]{:S(2)}) collective-permute-start(bf16[1,512,4,128]{1,3,2,0:T(8,128)(2,1)} %bitcast.208), channel_id=1, source_target_pairs={{0,4},{1,5},{2,6},{3,7},{8,12},{9,13},{10,14},{11,15},{16,20},{17,... | collective-permute-start | bytes 1572872 | tf_op jit(solution)/shard_map/ppermute | solution.py:25
  103.1 22.8 %collective-permute-start.1 = (bf16[512,1024]{1,0:T(8,128)(2,1)}, bf16[512,1024]{1,0:T(8,128)(2,1)}, u32[]{:S(2)}, u32[]{:S(2)}) collective-permute-start(bf16[512,1024]{1,0:T(8,128)(2,1)} %get-tuple-element.130), channel_id=1, source_target_pairs={{0,8},{8,0},{16,24},{24,16},{1,9},{9,1},{17,25},{25,17},{2,10},{10... | collective-permute-start | bytes 3145736 | tf_op jit(solution)/shard_map/ppermute | solution.py:1308
  104.6 22.5 %collective-permute-start.2 = (bf16[512,1024]{1,0:T(8,128)(2,1)}, bf16[512,1024]{1,0:T(8,128)(2,1)}, u32[]{:S(2)}, u32[]{:S(2)}) collective-permute-start(bf16[512,1024]{1,0:T(8,128)(2,1)} %get-tuple-element.129), channel_id=1, source_target_pairs={{0,16},{8,24},{16,0},{24,8},{1,17},{9,25},{17,1},{25,9},{2,18},{10... | collective-permute-start | bytes 3145736 | tf_op jit(solution)/shard_map/ppermute | solution.py:1308
  114.5 12.5 %copy-start.68 = (bf16[4,128,512]{2,1,0:T(8,128)(2,1)}, bf16[4,128,512]{2,1,0:T(8,128)(2,1)S(1)}, u32[]{:S(2)}) copy-start(bf16[4,128,512]{2,1,0:T(8,128)(2,1)S(1)} %fusion.25) | copy-start | bytes 1572868
  131.3 358.3 %reduce-scatter.6.cloned.1.call-start = ((), (), s32[]{:S(2)}) async-start(), calls=%async_computation.6 | async-start | bytes 18874368 | tf_op jit(solution)/shard_map/reduce_scatter | solution.py:1341
  131.3 42.9 %collective-permute-start.4 = (bf16[512,1024]{1,0:T(8,128)(2,1)}, bf16[512,1024]{1,0:T(8,128)(2,1)}, u32[]{:S(2)}, u32[]{:S(2)}) collective-permute-start(bf16[512,1024]{1,0:T(8,128)(2,1)} %get-tuple-element.129), channel_id=1, source_target_pairs={{0,8},{8,0},{16,24},{24,16},{1,9},{9,1},{17,25},{25,17},{2,10},{10... | collective-permute-start | bytes 3145736 | tf_op jit(solution)/shard_map/ppermute | solution.py:1308
  132.0 42.3 %collective-permute-start.5 = (bf16[512,1024]{1,0:T(8,128)(2,1)}, bf16[512,1024]{1,0:T(8,128)(2,1)}, u32[]{:S(2)}, u32[]{:S(2)}) collective-permute-start(bf16[512,1024]{1,0:T(8,128)(2,1)} %get-tuple-element.130), channel_id=1, source_target_pairs={{0,16},{8,24},{16,0},{24,8},{1,17},{9,25},{17,1},{25,9},{2,18},{10... | collective-permute-start | bytes 3145736 | tf_op jit(solution)/shard_map/ppermute | solution.py:1308
  132.5 43.2 %collective-permute-start.6 = (bf16[512,1024]{1,0:T(8,128)(2,1)}, bf16[512,1024]{1,0:T(8,128)(2,1)}, u32[]{:S(2)}, u32[]{:S(2)}) collective-permute-start(bf16[512,1024]{1,0:T(8,128)(2,1)} %collective-permute-done.1), channel_id=1, source_target_pairs={{0,16},{8,24},{16,0},{24,8},{1,17},{9,25},{17,1},{25,9},{2,18},{10... | collective-permute-start | bytes 3145736 | tf_op jit(solution)/shard_map/ppermute | solution.py:1308
  134.0 41.7 %collective-permute-start.7 = (bf16[512,1024]{1,0:T(8,128)(2,1)}, bf16[512,1024]{1,0:T(8,128)(2,1)}, u32[]{:S(2)}, u32[]{:S(2)}) collective-permute-start(bf16[512,1024]{1,0:T(8,128)(2,1)} %collective-permute-done.2), channel_id=1, source_target_pairs={{0,8},{8,0},{16,24},{24,16},{1,9},{9,1},{17,25},{25,17},{2,10},{10... | collective-permute-start | bytes 3145736 | tf_op jit(solution)/shard_map/ppermute | solution.py:1308
  173.3 209.1 %copy-start.61 = (f32[128]{0:T(128)}, f32[128]{0:T(128)S(1)}, u32[]{:S(2)}) copy-start(f32[128]{0:T(128)S(1)} %add_rsqrt_fusion.1) | copy-start | bytes 1540
  374.9 160.9 %reduce-scatter.8.cloned.1.call-start = ((), (), s32[]{:S(2)}) async-start(), calls=%async_computation.7 | async-start | bytes 2621440 | tf_op jit(solution)/shard_map/reduce_scatter | solution.py:1341
  376.0 9.3 %copy-start.35 = (pred[16,128]{0,1:T(32,128)(4,1)}, pred[16,128]{0,1:T(32,128)(4,1)S(1)}, u32[]{:S(2)}) copy-start(pred[16,128]{0,1:T(32,128)(4,1)S(1)} %copy.179) | copy-start | bytes 6148
  387.0 30.4 %copy-start.67 = (bf16[4,2,4,128,512]{4,3,2,1,0:T(8,128)(2,1)S(1)}, bf16[4,2,4,128,512]{4,3,2,1,0:T(8,128)(2,1)}, u32[]{:S(2)}) copy-start(bf16[4,2,4,128,512]{4,3,2,1,0:T(8,128)(2,1)} %get-tuple-element.47) | copy-start | bytes 12582916
  387.0 55.8 %collective-permute-start.8 = (bf16[128,2048]{1,0:T(8,128)(2,1)S(1)}, bf16[128,2048]{1,0:T(8,128)(2,1)}, u32[]{:S(2)}, u32[]{:S(2)}) collective-permute-start(bf16[128,2048]{1,0:T(8,128)(2,1)S(1)} %get-tuple-element.49), channel_id=1, source_target_pairs={{0,1},{1,2},{2,3},{3,0},{4,5},{5,6},{6,7},{7,4},{8,9},{9,10},{10,1... | collective-permute-start | bytes 1572872 | tf_op jit(solution)/shard_map/ppermute | solution.py:1328
  387.1 57.8 %collective-permute-start.9 = (bf16[128,2048]{1,0:T(8,128)(2,1)S(1)}, bf16[128,2048]{1,0:T(8,128)(2,1)}, u32[]{:S(2)}, u32[]{:S(2)}) collective-permute-start(bf16[128,2048]{1,0:T(8,128)(2,1)S(1)} %get-tuple-element.49), channel_id=1, source_target_pairs={{0,3},{1,0},{2,1},{3,2},{4,7},{5,4},{6,5},{7,6},{8,11},{9,8},{10,9... | collective-permute-start | bytes 1572872 | tf_op jit(solution)/shard_map/ppermute | solution.py:1328
  390.9 55.9 %collective-permute-start.10 = (bf16[128,2048]{1,0:T(8,128)(2,1)S(1)}, bf16[128,2048]{1,0:T(8,128)(2,1)}, u32[]{:S(2)}, u32[]{:S(2)}) collective-permute-start(bf16[128,2048]{1,0:T(8,128)(2,1)S(1)} %get-tuple-element.49), channel_id=1, source_target_pairs={{0,2},{1,3},{2,0},{3,1},{4,6},{5,7},{6,4},{7,5},{8,10},{9,11},{10,... | collective-permute-start | bytes 1572872 | tf_op jit(solution)/shard_map/ppermute | solution.py:1328
  462.6 8.2 %collective-permute-start.11 = (bf16[1,512,4,128]{3,1,2,0:T(8,128)(2,1)}, bf16[1,512,4,128]{3,1,2,0:T(8,128)(2,1)}, u32[]{:S(2)}, u32[]{:S(2)}) collective-permute-start(bf16[1,512,4,128]{3,1,2,0:T(8,128)(2,1)} %slice.245), channel_id=1, source_target_pairs={{4,0},{5,1},{6,2},{7,3},{12,8},{13,9},{14,10},{15,11},{20,16},{21,... | collective-permute-start | bytes 1572872 | tf_op jit(solution)/shard_map/ppermute | solution.py:25
  490.8 8.7 %copy-start.36 = (pred[16,128]{0,1:T(32,128)(4,1)S(1)}, pred[16,128]{0,1:T(32,128)(4,1)}, u32[]{:S(2)}) copy-start(pred[16,128]{0,1:T(32,128)(4,1)} %copy-done.35) | copy-start | bytes 6148
  490.8 8.7 %copy-start.54 = (f32[128]{0:T(128)S(1)}, f32[128]{0:T(128)}, u32[]{:S(2)}) copy-start(f32[128]{0:T(128)} %copy-done.53) | copy-start | bytes 1540
  498.2 9.8 %collective-permute-start.12 = (bf16[1,512,4,128]{1,3,2,0:T(8,128)(2,1)}, bf16[1,512,4,128]{1,3,2,0:T(8,128)(2,1)}, u32[]{:S(2)}, u32[]{:S(2)}) collective-permute-start(bf16[1,512,4,128]{1,3,2,0:T(8,128)(2,1)} %slice.244), channel_id=1, source_target_pairs={{4,0},{5,1},{6,2},{7,3},{12,8},{13,9},{14,10},{15,11},{20,16},{21,... | collective-permute-start | bytes 1572872 | tf_op jit(solution)/shard_map/ppermute | solution.py:25
  511.7 8.7 %slice-start.3 = ((s8[6324224]{0:T(1024)(128)(4,1)}), s8[4194304]{0:T(1024)(128)(4,1)S(1)}, s32[]{:S(2)}) async-start(s8[6324224]{0:T(1024)(128)(4,1)} %bitcast.246), calls=%async_computation.11 | async-start | bytes 8388608
  (60 other events, 251.0 us)
Sparse Core Ops, SparseCore 0:
  13.3 49.5 all-gather.2
  64.7 30.1 all-gather.4
  131.4 40.1 reduce-scatter.3
  375.1 114.5 reduce-scatter.5
  491.9 43.8 reduce-scatter.7
